TPU v7x, 512 devices: a whole 4x4x16 slice. The times are simulated.
512 devices in a mesh: segment: 4 (over x), shard: 128 (over z, y, core).
Axes of the slice: x: 4, y: 4, z: 16, core: 2. Of those that a mesh axis runs over, the one named last changes fastest.
Arguments:
- item_table: bfloat16 [262144, 256], P('shard'), may hold values from -6 to 6
- user_states: bfloat16 [512, 1024], P('shard'), may hold values from -6 to 6
- w_lift: bfloat16 [4, 256, 1024], P('segment', 'shard'), may hold values from -0.375 to 0.375
- w_pair: bfloat16 [4, 1024, 2048], P('segment', 'shard'), may hold values from -0.1875 to 0.1875
- w_ask: bfloat16 [4, 1024, 1024], P('segment', 'shard'), may hold values from -0.1875 to 0.1875
- w_back: bfloat16 [4, 1024, 1024], P('segment', 'shard'), may hold values from -0.1875 to 0.1875
- norm_gains: float32 [4, 1024], P('segment'), may hold values from 0.5 to 2
- item_ids: int32 [4, 512, 128], P('segment', 'shard'), may hold values from 0 to 262143, as said below
- lengths: int32 [4, 512], P('segment', 'shard'), may hold values from 1 to 128, as said below
Outputs:
- section_states: bfloat16 [4, 512, 1024], P('segment', 'shard')
- section_scores: float32 [4, 512, 128], P('segment', 'shard')
Inputs may be any that keep to these rules, and one draw needn't show every extreme that they name: `item_ids`: for every section and every micro-batch of one index of shard (2 users, 256 ids), at most 4 ids fall in any one table shard (ids j * 2048 to (j + 1) * 2048 - 1), and exactly 4 fall in one shard j that is the same for all indices of shard in that section and micro-batch. `lengths`: in every section, every micro-batch of one index of shard has a user with all 128 items live.
All inputs are finite; a program needn't handle non-finite values.
Results may differ from a plain program's by a relative error of at most 0.019.
Values may be sent and summed in bfloat16 or wider, within the bound.
No kernel may reach another device: no remote copies, remote signals or barrier semaphores. Data moves between devices by JAX's collectives and lax.ppermute only.
A program may use at most 64 MiB of HBM per device.

v0:
```python
import math

import jax
import jax.numpy as jnp
from jax import lax
from jax.sharding import PartitionSpec as P

HEADS = 8
BU = 2


def shifted(block, axis, distance):
    devices = range(lax.axis_size(axis))
    route = [(i - distance, i) for i in devices if i - distance in devices]
    return lax.ppermute(block, axis, route)


def item_side(item_rows, lift, pair):
    lifted = jax.nn.silu(jnp.dot(item_rows, lift, preferred_element_type=jnp.float32)).astype(
        jnp.bfloat16
    )
    return jnp.dot(lifted, pair, preferred_element_type=jnp.float32).astype(jnp.bfloat16)


def user_side(user_state, paired, live_mask, ask, back, norm_gain):
    user_count = user_state.shape[0]
    model_width = ask.shape[0]
    item_count = live_mask.shape[1]
    head_size = model_width // HEADS
    paired = paired.reshape(user_count, item_count, 2, HEADS, head_size)
    queries = jnp.dot(user_state, ask, preferred_element_type=jnp.float32).astype(jnp.bfloat16)
    queries = queries.reshape(user_count, HEADS, head_size)
    logits = jnp.einsum(
        "uhd,ukhd->uhk", queries, paired[:, :, 0], preferred_element_type=jnp.float32
    ) / math.sqrt(head_size)
    weights = jax.nn.silu(logits) * live_mask[:, None, :]
    item_scores = jnp.mean(weights, axis=1)
    attended = jnp.einsum(
        "uhk,ukhd->uhd",
        weights.astype(jnp.bfloat16),
        paired[:, :, 1],
        preferred_element_type=jnp.float32,
    ).reshape(user_count, model_width)
    normed = (
        attended
        * lax.rsqrt(jnp.mean(attended * attended, axis=1, keepdims=True) + 1e-05)
        * norm_gain
    ).astype(jnp.bfloat16)
    update = jnp.dot(normed, back, preferred_element_type=jnp.float32)
    return ((user_state.astype(jnp.float32) + update).astype(jnp.bfloat16), item_scores)


def request_rows(wanted, table_shard, shard_count, capacity):
    shard_rows = table_shard.shape[0]
    owners = wanted // shard_rows
    offsets = wanted - owners * shard_rows
    onehot = (owners[:, None] == jnp.arange(shard_count, dtype=jnp.int32)[None, :]).astype(
        jnp.int32
    )
    placing = jnp.sum(jnp.cumsum(onehot, axis=0) * onehot, axis=1) - 1
    request = jnp.zeros((shard_count, capacity), jnp.int32).at[owners, placing].set(offsets)
    arrived = lax.all_to_all(request, "shard", split_axis=0, concat_axis=0, tiled=True)
    returned = lax.all_to_all(
        table_shard[arrived], "shard", split_axis=0, concat_axis=0, tiled=True
    )
    return returned[owners, placing]


def per_device(
    item_table, user_states, w_lift, w_pair, w_ask, w_back, norm_gains, item_ids, lengths
):
    segment_index = lax.axis_index("segment")
    segment_count = lax.axis_size("segment")
    shard_count = lax.axis_size("shard")
    full_lift, full_pair, full_ask, full_back = (
        lax.all_gather(w_lift, "shard", axis=1, tiled=True),
        lax.all_gather(w_pair, "shard", axis=1, tiled=True),
        lax.all_gather(w_ask, "shard", axis=1, tiled=True),
        lax.all_gather(w_back, "shard", axis=1, tiled=True),
    )
    full_lift = full_lift[0]
    full_pair = full_pair[0]
    full_ask = full_ask[0]
    full_back = full_back[0]
    norm_gain = norm_gains[0]
    item_count = item_ids.shape[2]
    model_width = user_states.shape[1]
    micro_count = user_states.shape[0] // BU
    capacity = max(2, 2 * BU * item_count // shard_count)
    wanted_all = item_ids[0].reshape(micro_count, BU * item_count)
    live_all = (
        jnp.arange(item_count, dtype=jnp.int32)[None, None, :]
        < lengths[0].reshape(micro_count, BU)[:, :, None]
    ).astype(jnp.float32)
    inputs = user_states.reshape(micro_count, BU, model_width)
    paired_list = []
    for micro_index in range(micro_count):
        rows_now = request_rows(wanted_all[micro_index], item_table, shard_count, capacity)
        paired_list.append(item_side(rows_now, full_lift, full_pair))
    paired_all = jnp.stack(paired_list)
    incoming = jnp.zeros_like(inputs[0])
    out_states = jnp.zeros_like(inputs)
    out_scores = jnp.zeros((micro_count, BU, item_count), jnp.float32)
    total_steps = micro_count + segment_count - 1
    for time_step in range(total_steps):
        batch_index = time_step - segment_index
        clamped = jnp.clip(batch_index, 0, micro_count - 1)
        is_valid = (batch_index >= 0) & (batch_index < micro_count)
        entering = jnp.where(segment_index == 0, inputs[min(time_step, micro_count - 1)], incoming)
        paired_now = lax.dynamic_index_in_dim(paired_all, clamped, 0, keepdims=False)
        live_mask = lax.dynamic_index_in_dim(live_all, clamped, 0, keepdims=False)
        leaving, item_scores = user_side(
            entering, paired_now, live_mask, full_ask, full_back, norm_gain
        )
        kept_state = jnp.where(
            is_valid, leaving, lax.dynamic_index_in_dim(out_states, clamped, 0, keepdims=False)
        )
        kept_scores = jnp.where(
            is_valid, item_scores, lax.dynamic_index_in_dim(out_scores, clamped, 0, keepdims=False)
        )
        out_states = lax.dynamic_update_index_in_dim(out_states, kept_state, clamped, 0)
        out_scores = lax.dynamic_update_index_in_dim(out_scores, kept_scores, clamped, 0)
        if time_step + 1 < total_steps:
            incoming = shifted(leaving, "segment", 1)
    return (
        out_states.reshape(1, micro_count * BU, model_width),
        out_scores.reshape(1, micro_count * BU, item_count),
    )


def solution(mesh):
    in_specs = (
        P("shard", None),
        P("shard", None),
        P("segment", "shard", None),
        P("segment", "shard", None),
        P("segment", "shard", None),
        P("segment", "shard", None),
        P("segment", None),
        P("segment", "shard", None),
        P("segment", "shard"),
    )
    out_specs = (P("segment", "shard", None), P("segment", "shard", None))
    return jax.shard_map(
        per_device, mesh=mesh, in_specs=in_specs, out_specs=out_specs, check_vma=False
    )
```

profile of v0, /device:TPU:6, one launch (start us, length us, event | category | flops | bytes accessed | tf_op | source)
XLA Modules:
  0.0 494.3 jit_solution(12492884210052167631)
XLA Ops:
  7.2 0.7 all-gather.4.cloned.1.call-update
  8.0 0.7 all-gather.6.cloned.1.call-update
  8.7 0.8 and_select_fusion.2
  10.3 0.8 bitcast_subtract_fusion
  11.4 0.8 fusion.182
  12.2 11.1 %scatter_fusion.1 = s32[128,4]{0,1:T(4,128)S(1)} fusion(s32[128,4]{0,1:T(4,128)S(1)} %broadcast.494.clone.1, s32[256]{0:T(256)S(1)} %bitcast.336, s32[256]{0:T(256)S(1)} %get-tuple-element.2), kind=kCustom, calls=%fused_computation.5 | custom fusion | bytes 5120 | tf_op jit(solution)/shard_map/scatter | solution.py:61
  23.3 0.7 copy.39
  24.0 20.0 %all-to-all-start.2 = ((s32[128,1,4]{2,1,0:T(1,128)}), s32[128,1,4]{2,1,0:T(1,128)S(1)}, u32[]{:S(2)}, u32[]{:S(2)}) async-start(s32[128,1,4]{2,1,0:T(1,128)} %copy.39), calls=%async_computation.2 | async-start | bytes 131072 | tf_op jit(solution)/shard_map/all_to_all | solution.py:62
  44.0 11.1 %scatter_fusion = s32[128,4]{0,1:T(4,128)S(1)} fusion(s32[128,4]{0,1:T(4,128)S(1)} %broadcast.494.clone, s32[256]{0:T(256)S(1)} %bitcast.335, s32[256]{0:T(256)S(1)} %get-tuple-element.40), kind=kCustom, calls=%fused_computation.4 | custom fusion | bytes 5120 | tf_op jit(solution)/shard_map/scatter | solution.py:61
  55.1 0.7 copy.35
  55.8 2.6 all-to-all-done.2
  58.4 13.5 %all-to-all-start = ((s32[128,1,4]{2,1,0:T(1,128)}), s32[128,1,4]{2,1,0:T(1,128)S(1)}, u32[]{:S(2)}, u32[]{:S(2)}) async-start(s32[128,1,4]{2,1,0:T(1,128)} %copy.35), calls=%async_computation | async-start | bytes 131072 | tf_op jit(solution)/shard_map/all_to_all | solution.py:62
  72.1 2.0 gather_fusion.2
  74.1 0.8 reshape.562
  74.8 11.6 %all-to-all-done = s32[128,1,4]{2,1,0:T(1,128)S(1)} async-done(((s32[128,1,4]{2,1,0:T(1,128)}), s32[128,1,4]{2,1,0:T(1,128)S(1)}, u32[]{:S(2)}, u32[]{:S(2)}) %all-to-all-start) | async-done | bytes 2080 | tf_op jit(solution)/shard_map/all_to_all | solution.py:62
  86.4 6.2 %all-to-all-start.3 = ((bf16[128,4,256]{2,1,0:T(4,128)(2,1)}), bf16[128,4,256]{2,1,0:T(4,128)(2,1)S(1)}, u32[]{:S(2)}, u32[]{:S(2)}) async-start(bf16[128,4,256]{2,1,0:T(4,128)(2,1)} %reshape.562), calls=%async_computation.3 | async-start | bytes 524288 | tf_op jit(solution)/shard_map/all_to_all | solution.py:63
  92.6 0.7 all-gather.8.cloned.1.call-update
  93.5 2.0 gather_fusion
  95.4 0.8 reshape.548
  96.2 17.3 %all-to-all-done.3 = bf16[128,4,256]{2,1,0:T(4,128)(2,1)S(1)} async-done(((bf16[128,4,256]{2,1,0:T(4,128)(2,1)}), bf16[128,4,256]{2,1,0:T(4,128)(2,1)S(1)}, u32[]{:S(2)}, u32[]{:S(2)}) %all-to-all-start.3) | async-done | bytes 262176 | tf_op jit(solution)/shard_map/all_to_all | solution.py:63
  113.5 8.5 %all-to-all-start.1 = ((bf16[128,4,256]{2,1,0:T(4,128)(2,1)}), bf16[128,4,256]{2,1,0:T(4,128)(2,1)S(1)}, u32[]{:S(2)}, u32[]{:S(2)}) async-start(bf16[128,4,256]{2,1,0:T(4,128)(2,1)} %reshape.548), calls=%async_computation.1 | async-start | bytes 524288 | tf_op jit(solution)/shard_map/all_to_all | solution.py:63
  122.1 0.5 broadcast.670
  122.6 0.7 reduce.8
  123.4 107.3 %all_gather.13 = bf16[1,256,1024]{2,0,1:T(2,128)(2,1)S(1)} all-gather(bf16[1,2,1024]{2,0,1:T(2,128)(2,1)S(1)} %copy.36), channel_id=1, replica_groups=mesh['segment'=4,'shard'=128] {'shard'}, dimensions={1}, use_global_device_ids=true | all-gather | bytes 528384 | tf_op jit(solution)/shard_map/all_gather | solution.py:76
  230.7 1.7 gather_fusion.3
  232.4 1.7 gather_fusion.1
  234.1 2.0 fusion.42
  236.1 63.3 %all-gather.6.cloned.1.call-done = bf16[1,1024,2048]{2,1,0:T(8,128)(2,1)} async-done(((bf16[1,8,2048]{2,1,0:T(8,128)(2,1)}), bf16[1,1024,2048]{2,1,0:T(8,128)(2,1)}) %all-gather.6.cloned.1.call-update) | async-done | bytes 4194320 | tf_op jit(solution)/shard_map/all_gather | solution.py:77
  299.4 4.7 fusion.10
  304.1 4.8 fusion.13
  308.9 5.6 %fusion.58 = (bf16[32,8,16,128]{3,1,2,0:T(8,128)(2,1)}, bf16[32,8,16,128]{3,1,2,0:T(8,128)(2,1)S(1)}, bf16[32,8,16,128]{3,1,2,0:T(8,128)(2,1)}, bf16[32,8,16,128...) fusion(s32[]{:T(128)S(6)} %min.20, bf16[1,256,2048]{2,1,0:T(8,128)(2,1)} %fusion.13, bf16[1,256,2048]{2,1,0:T(8,128)(2,1)} %fusion.10, ...), kind=kLoop, calls=%fused_computation.52 | loop fusion | flops 2621440 | bytes 7340052
  314.9 0.4 fusion.97
  315.7 122.5 %all-gather.8.cloned.1.call-done = bf16[1,1024,1024]{2,1,0:T(8,128)(2,1)} async-done(((bf16[1,8,1024]{2,1,0:T(8,128)(2,1)}), bf16[1,1024,1024]{2,1,0:T(8,128)(2,1)}) %all-gather.8.cloned.1.call-update) | async-done | bytes 2097168 | tf_op jit(solution)/shard_map/all_gather | solution.py:79
  438.3 2.1 constant_dynamic-update-slice_fusion.9
  440.3 1.5 collective-permute-start
  442.1 1.2 slice_bitcast_fusion.7
  443.5 1.2 slice_bitcast_fusion.5
  444.9 1.2 slice_bitcast_fusion.3
  446.4 1.2 slice_bitcast_fusion.1
  447.6 0.5 copy-done.1
  448.1 0.4 fusion.45
  448.5 1.4 fusion.93
  450.0 1.3 fusion.91
  451.4 2.0 constant_dynamic-update-slice_fusion.8
  453.4 1.3 collective-permute-start.1
  454.8 4.8 collective-permute-done.1
  459.5 0.4 fusion.48
  459.9 1.4 fusion.89
  461.4 1.3 fusion.87
  462.9 2.0 constant_dynamic-update-slice_fusion.7
  464.9 1.3 collective-permute-start.2
  466.2 4.2 collective-permute-done.2
  470.4 0.4 fusion.51
  470.8 1.4 fusion.85
  472.2 1.3 fusion.83
  473.7 2.0 constant_dynamic-update-slice_fusion.6
  475.7 1.3 collective-permute-start.3
  477.1 4.2 collective-permute-done.3
  481.2 0.4 fusion.54
  481.6 1.4 fusion.81
  483.1 1.3 fusion.79
  484.6 2.0 constant_dynamic-update-slice_fusion.5
  486.6 0.6 reshape.545
  487.2 0.6 copy-done.6
  (98 shorter events, 4.8 us)
Async XLA Ops:
  7.2 64.9 %copy-start = (bf16[2048,256]{1,0:T(8,128)(2,1)S(1)}, bf16[2048,256]{1,0:T(8,128)(2,1)}, u32[]{:S(2)}) copy-start(bf16[2048,256]{1,0:T(8,128)(2,1)} %param.9) | copy-start | bytes 3145732
  7.2 226.9 %all-gather.4.cloned.1.call-start = ((), (), s32[]{:S(2)}) async-start(), calls=%async_computation.4 | async-start | bytes 2113536 | tf_op jit(solution)/shard_map/all_gather | solution.py:78
  7.9 291.5 %all-gather.6.cloned.1.call-start = ((), (), s32[]{:S(2)}) async-start(), calls=%async_computation.5 | async-start | bytes 4227072 | tf_op jit(solution)/shard_map/all_gather | solution.py:77
  24.0 34.4 %all-to-all-start.2 = ((s32[128,1,4]{2,1,0:T(1,128)}), s32[128,1,4]{2,1,0:T(1,128)S(1)}, u32[]{:S(2)}, u32[]{:S(2)}) async-start(s32[128,1,4]{2,1,0:T(1,128)} %copy.39), calls=%async_computation.2 | async-start | bytes 131072 | tf_op jit(solution)/shard_map/all_to_all | solution.py:62
  58.4 28.0 %all-to-all-start = ((s32[128,1,4]{2,1,0:T(1,128)}), s32[128,1,4]{2,1,0:T(1,128)S(1)}, u32[]{:S(2)}, u32[]{:S(2)}) async-start(s32[128,1,4]{2,1,0:T(1,128)} %copy.35), calls=%async_computation | async-start | bytes 131072 | tf_op jit(solution)/shard_map/all_to_all | solution.py:62
  74.8 47.2 %copy-start.7 = (bf16[1,2,1024]{2,1,0:T(2,128)(2,1)S(1)}, bf16[1,2,1024]{2,1,0:T(2,128)(2,1)}, u32[]{:S(2)}) copy-start(bf16[1,2,1024]{2,1,0:T(2,128)(2,1)} %param.11) | copy-start | bytes 12292
  74.8 47.8 %copy-start.8 = (s32[1,4]{1,0:T(1,128)S(1)}, s32[1,4]{1,0:T(1,128)}, u32[]{:S(2)}) copy-start(s32[1,4]{1,0:T(1,128)} %param.17) | copy-start | bytes 52
  86.4 27.1 %all-to-all-start.3 = ((bf16[128,4,256]{2,1,0:T(4,128)(2,1)}), bf16[128,4,256]{2,1,0:T(4,128)(2,1)S(1)}, u32[]{:S(2)}, u32[]{:S(2)}) async-start(bf16[128,4,256]{2,1,0:T(4,128)(2,1)} %reshape.562), calls=%async_computation.3 | async-start | bytes 524288 | tf_op jit(solution)/shard_map/all_to_all | solution.py:63
  92.6 345.6 %all-gather.8.cloned.1.call-start = ((), (), s32[]{:S(2)}) async-start(), calls=%async_computation.6 | async-start | bytes 2113536 | tf_op jit(solution)/shard_map/all_gather | solution.py:79
  96.2 137.9 %copy-start.4 = (bf16[4,1024]{1,0:T(4,128)(2,1)S(1)}, bf16[4,1024]{1,0:T(4,128)(2,1)}, u32[]{:S(2)}) copy-start(bf16[4,1024]{1,0:T(4,128)(2,1)} %param.10) | copy-start | bytes 24580
  113.5 118.9 %all-to-all-start.1 = ((bf16[128,4,256]{2,1,0:T(4,128)(2,1)}), bf16[128,4,256]{2,1,0:T(4,128)(2,1)S(1)}, u32[]{:S(2)}, u32[]{:S(2)}) async-start(bf16[128,4,256]{2,1,0:T(4,128)(2,1)} %reshape.548), calls=%async_computation.1 | async-start | bytes 524288 | tf_op jit(solution)/shard_map/all_to_all | solution.py:63
  314.7 1.0 copy-start.5
  438.2 3.6 copy-start.3
  440.3 7.2 %collective-permute-start = (bf16[2,1024]{1,0:T(2,128)(2,1)S(1)}, bf16[2,1024]{1,0:T(2,128)(2,1)S(1)}, u32[]{:S(2)}, u32[]{:S(2)}) collective-permute-start(bf16[2,1024]{1,0:T(2,128)(2,1)S(1)} %get-tuple-element.51), channel_id=1, source_target_pairs={{0,128},{128,256},{256,384},{1,129},{129,257},{257,385},{2,130},{1... | collective-permute-start | bytes 12296 | tf_op jit(solution)/shard_map/ppermute | solution.py:15
  444.7 1.4 copy-start.2
  446.1 2.0 copy-start.1
  453.4 6.1 %collective-permute-start.1 = (bf16[2,1024]{1,0:T(2,128)(2,1)S(1)}, bf16[2,1024]{1,0:T(2,128)(2,1)S(1)}, u32[]{:S(2)}, u32[]{:S(2)}) collective-permute-start(bf16[2,1024]{1,0:T(2,128)(2,1)S(1)} %get-tuple-element.53), channel_id=1, source_target_pairs={{0,128},{128,256},{256,384},{1,129},{129,257},{257,385},{2,130},{1... | collective-permute-start | bytes 12296 | tf_op jit(solution)/shard_map/ppermute | solution.py:15
  464.9 5.5 %collective-permute-start.2 = (bf16[2,1024]{1,0:T(2,128)(2,1)S(1)}, bf16[2,1024]{1,0:T(2,128)(2,1)S(1)}, u32[]{:S(2)}, u32[]{:S(2)}) collective-permute-start(bf16[2,1024]{1,0:T(2,128)(2,1)S(1)} %get-tuple-element.55), channel_id=1, source_target_pairs={{0,128},{128,256},{256,384},{1,129},{129,257},{257,385},{2,130},{1... | collective-permute-start | bytes 12296 | tf_op jit(solution)/shard_map/ppermute | solution.py:15
  475.7 5.5 %collective-permute-start.3 = (bf16[2,1024]{1,0:T(2,128)(2,1)S(1)}, bf16[2,1024]{1,0:T(2,128)(2,1)S(1)}, u32[]{:S(2)}, u32[]{:S(2)}) collective-permute-start(bf16[2,1024]{1,0:T(2,128)(2,1)S(1)} %get-tuple-element.57), channel_id=1, source_target_pairs={{0,128},{128,256},{256,384},{1,129},{129,257},{257,385},{2,130},{1... | collective-permute-start | bytes 12296 | tf_op jit(solution)/shard_map/ppermute | solution.py:15
  487.2 0.6 copy-start.6
Sparse Core Ops, SparseCore 0:
  11.2 146.0 all-gather.3
  160.4 138.9 all-gather.5
  302.5 135.6 all-gather.7
where the time goes:
time: 497 us; the launch traced here: 494 us
  waiting for transfers between devices  232 us (47%)
  blocking collectives  107 us (22%)
  starting transfers between devices  53.6 us (11%)
  local copies, waits for them, and re-layouts  42.2 us (8%)
  matrix products  34.4 us (7%)
  between operations  14.2 us (3%)
  other arithmetic  10.1 us (2%)
    all_gather x1, waiting for transfers between devices, per_device(): lax.all_gather(w_back, 'shard', axis=1, tiled=True)  123 us
    all_gather x1, blocking collectives, per_device(): lax.all_gather(w_lift, 'shard', axis=1, tiled=True)  107 us
    all_gather x1, waiting for transfers between devices, per_device(): lax.all_gather(w_pair, 'shard', axis=1, tiled=True)  63.3 us
    all_to_all x2, starting transfers between devices, request_rows(): lax.all_to_all(request, 'shard', split_axis=0, concat_axis=0, tiled=True)  33.5 us
    scatter x2, local copies, waits for them, and re-layouts, request_rows(): jnp.zeros((shard_count, capacity), jnp.int32).at[owners, placing]  22.1 us
    all_to_all x2, waiting for transfers between devices, request_rows(): lax.all_to_all(table_shard[arrived], 'shard', split_axis=0, concat_axis=0...  17.3 us
    all_to_all x2, starting transfers between devices, request_rows(): lax.all_to_all(table_shard[arrived], 'shard', split_axis=0, concat_axis=0...  14.7 us
    all_to_all x2, waiting for transfers between devices, request_rows(): lax.all_to_all(request, 'shard', split_axis=0, concat_axis=0, tiled=True)  14.2 us
  transfers between devices with their start and end apart: 11, of which 8 were waited for; matrix products, arithmetic and copies ran while one was open for 12% of the time, Pallas kernels for 0%

commit v1 on v0

v1 whole, which is shorter than its diff:
```python
import math

import jax
import jax.numpy as jnp
from jax import lax
from jax.experimental import pallas as pl
from jax.experimental.pallas import tpu as pltpu
from jax.sharding import Mesh
from jax.sharding import PartitionSpec as P

HEADS = 8
BU = 2
CAP = 8
F32 = jnp.float32
BF16 = jnp.bfloat16
SHARD = ("z", "y", "core")


def vmem():
    return pl.BlockSpec(memory_space=pltpu.VMEM)


def anywhere():
    return pl.BlockSpec(memory_space=pltpu.HBM)


def request_kernel(shard_rows, ids_ref, request_ref, slot_ref):
    users, items = ids_ref.shape
    shards, capacity = request_ref.shape
    ids = ids_ref[...]
    owners = ids // shard_rows
    offsets = ids - owners * shard_rows
    owner_row = lax.broadcasted_iota(jnp.int32, (shards, items), 0)
    before = (
        lax.broadcasted_iota(jnp.int32, (items, items), 0)
        < lax.broadcasted_iota(jnp.int32, (items, items), 1)
    ).astype(BF16)
    place_row = lax.broadcasted_iota(jnp.int32, (capacity, items), 0)
    base = jnp.zeros((shards, 1), F32)
    high = jnp.zeros((shards, capacity), F32)
    low = jnp.zeros((shards, capacity), F32)
    for user in range(users):
        mine = owner_row == owners[user : user + 1, :]
        onehot = mine.astype(F32)
        onehot_low = onehot.astype(BF16)
        earlier = jnp.dot(onehot_low, before, preferred_element_type=F32) + base
        place = jnp.sum(onehot * earlier, axis=0, keepdims=True).astype(jnp.int32)
        base = base + jnp.sum(onehot, axis=1, keepdims=True)
        at_place = place_row == place
        offset = offsets[user : user + 1, :]
        offset_high = jnp.where(at_place, offset // 64, 0).astype(F32).astype(BF16)
        offset_low = jnp.where(at_place, offset % 64, 0).astype(F32).astype(BF16)
        contract = (((1,), (1,)), ((), ()))
        high = high + lax.dot_general(
            onehot_low, offset_high, contract, preferred_element_type=F32
        )
        low = low + lax.dot_general(
            onehot_low, offset_low, contract, preferred_element_type=F32
        )
        slot_ref[user : user + 1, :] = owners[user : user + 1, :] * capacity + place
    request_ref[...] = (high * 64.0 + low).astype(jnp.int32)


def table_kernel(arrived_ref, table_ref, rows_ref):
    shards, capacity, width = rows_ref.shape
    shard_rows = table_ref.shape[0]
    block = 32
    count = block * capacity
    diagonal = lax.broadcasted_iota(
        jnp.int32, (block, capacity, capacity), 1
    ) == lax.broadcasted_iota(jnp.int32, (block, capacity, capacity), 2)
    row = lax.broadcasted_iota(jnp.int32, (count, shard_rows), 1)
    for start in range(0, shards, block):
        asked = arrived_ref[start : start + block, :]
        spread = jnp.broadcast_to(asked[:, None, :], (block, capacity, capacity))
        column = jnp.sum(jnp.where(diagonal, spread, 0).astype(F32), axis=2, keepdims=True)
        column = column.astype(jnp.int32).reshape(count, 1)
        onehot = (row == column).astype(F32).astype(BF16)
        found = jnp.dot(onehot, table_ref[...], preferred_element_type=F32)
        rows_ref[start : start + block] = found.astype(BF16).reshape(block, capacity, width)


def item_kernel(
    gathered_ref,
    returned_ref,
    slot_ref,
    key_ref,
    value_ref,
    ask_ref,
    back_ref,
    pair_buf,
    lift_buf,
    ask_buf,
    back_buf,
    sems,
):
    zs, cores, ys, rows8, _ = gathered_ref.shape
    depth = zs * cores * ys * rows8
    emb = returned_ref.shape[1]
    users, items = slot_ref.shape
    width = depth
    parts = ((lift_buf, 4 * width), (pair_buf, 0), (ask_buf, 2 * width), (back_buf, 3 * width))
    copies = []
    for part, (buf, first) in enumerate(parts):
        mine = []
        for core in range(cores):
            for y in range(ys):
                copy = pltpu.make_async_copy(
                    gathered_ref.at[:, core, y, :, pl.ds(first, buf.shape[-1])],
                    buf.at[:, y, core],
                    sems.at[part, core * ys + y],
                )
                copy.start()
                mine.append(copy)
        copies.append(mine)

    slots = slot_ref[...]
    slot_row = lax.broadcasted_iota(jnp.int32, (returned_ref.shape[0], items), 0)
    returned = returned_ref[...]
    listed = []
    for user in range(users):
        onehot = (slot_row == slots[user : user + 1, :]).astype(F32).astype(BF16)
        listed.append(
            lax.dot_general(
                onehot, returned, (((0,), (0,)), ((), ())), preferred_element_type=F32
            ).astype(BF16)
        )
    listed = jnp.concatenate(listed, axis=0)

    for copy in copies[0]:
        copy.wait()
    packed = lift_buf[...].reshape(depth, emb)
    split = depth // emb
    lifted = []
    for part in range(split):
        pick = (
            lax.broadcasted_iota(jnp.int32, (emb, depth), 0) * split + part
            == lax.broadcasted_iota(jnp.int32, (emb, depth), 1)
        )
        lift = jnp.dot(
            pick.astype(F32).astype(BF16), packed, preferred_element_type=F32
        ).astype(BF16)
        lifted.append(
            jax.nn.silu(jnp.dot(listed, lift, preferred_element_type=F32)).astype(BF16)
        )
    lifted = jnp.concatenate(lifted, axis=1)
    for copy in copies[1]:
        copy.wait()
    block = 512
    for first in range(0, 2 * width, block):
        pair = pair_buf[:, :, :, :, first : first + block].reshape(depth, block)
        made = jnp.dot(lifted, pair, preferred_element_type=F32).astype(BF16)
        if first < width:
            key_ref[:, first : first + block] = made
        else:
            value_ref[:, first - width : first - width + block] = made
    for buf, ref, mine in ((ask_buf, ask_ref, copies[2]), (back_buf, back_ref, copies[3])):
        for copy in mine:
            copy.wait()
        ref[...] = buf[...].reshape(depth, width)


def section_kernel(
    state_ref, key_ref, value_ref, ask_ref, back_ref, gain_ref, length_ref, next_ref, score_ref
):
    users, width = state_ref.shape
    count = key_ref.shape[0]
    items = count // users
    head_size = width // HEADS
    rows = users * HEADS
    state = state_ref[...]
    query = jnp.dot(state, ask_ref[...], preferred_element_type=F32).astype(BF16)
    spread = jnp.broadcast_to(query.astype(F32)[:, None, :], (users, HEADS, width)).reshape(
        rows, width
    )
    in_head = (
        lax.broadcasted_iota(jnp.int32, (rows, width), 1) // head_size
        == lax.broadcasted_iota(jnp.int32, (rows, width), 0) % HEADS
    )
    spread = jnp.where(in_head, spread, 0.0).astype(BF16)
    logits = lax.dot_general(
        spread, key_ref[...], (((1,), (1,)), ((), ())), preferred_element_type=F32
    ) * (1.0 / math.sqrt(head_size))
    column = lax.broadcasted_iota(jnp.int32, (rows, count), 1)
    owner = lax.broadcasted_iota(jnp.int32, (rows, count), 0) // HEADS
    live = (column // items == owner) & (column % items < length_ref[...])
    weights = jnp.where(live, jax.nn.silu(logits), 0.0)
    score_ref[...] = jnp.sum(weights, axis=0, keepdims=True) * (1.0 / HEADS)
    mixed = jnp.dot(weights.astype(BF16), value_ref[...], preferred_element_type=F32)
    mixed = jnp.where(in_head, mixed, 0.0).reshape(users, HEADS, width)
    attended = jnp.sum(mixed, axis=1)
    scale = lax.rsqrt(jnp.mean(attended * attended, axis=1, keepdims=True) + 1e-05)
    normed = (attended * scale * gain_ref[...]).astype(BF16)
    update = jnp.dot(normed, back_ref[...], preferred_element_type=F32)
    next_ref[...] = (state.astype(F32) + update).astype(BF16)


def per_device(
    item_table, user_states, w_lift, w_pair, w_ask, w_back, norm_gains, item_ids, lengths
):
    segment_index = lax.axis_index("segment")
    segment_count = lax.axis_size("segment")
    zs, ys, cores = (lax.axis_size(name) for name in SHARD)
    shards = zs * ys * cores
    users, width = user_states.shape
    items = item_ids.shape[2]
    shard_rows, emb = item_table.shape
    depth = w_ask.shape[1]
    small, big = (pltpu.CompilerParams(vmem_limit_bytes=size << 20) for size in (12, 24))

    own = jnp.concatenate(
        [w_pair[0], w_ask[0], w_back[0], w_lift[0].reshape(depth, emb)], axis=1
    )
    near = lax.all_gather(own, "y", axis=0, tiled=True)
    gathered = lax.all_gather(near, ("z", "core"), axis=0, tiled=True)
    gathered = gathered.reshape(zs, cores, ys, depth, own.shape[1])

    request, slots = pl.pallas_call(
        lambda *refs: request_kernel(shard_rows, *refs),
        out_shape=(
            jax.ShapeDtypeStruct((shards, CAP), jnp.int32),
            jax.ShapeDtypeStruct((users, items), jnp.int32),
        ),
        in_specs=[vmem()],
        out_specs=(vmem(), vmem()),
        compiler_params=small,
        name="request",
    )(item_ids[0])
    arrived = lax.all_to_all(
        request.reshape(shards, 1, CAP), SHARD, split_axis=0, concat_axis=0, tiled=True
    )
    found = pl.pallas_call(
        table_kernel,
        out_shape=jax.ShapeDtypeStruct((shards, CAP, emb), BF16),
        in_specs=[vmem(), vmem()],
        out_specs=vmem(),
        compiler_params=small,
        name="table",
    )(arrived.reshape(shards, CAP), item_table)
    returned = lax.all_to_all(found, SHARD, split_axis=0, concat_axis=0, tiled=True)

    keys, values, ask, back = pl.pallas_call(
        item_kernel,
        out_shape=(
            jax.ShapeDtypeStruct((users * items, width), BF16),
            jax.ShapeDtypeStruct((users * items, width), BF16),
            jax.ShapeDtypeStruct((width, width), BF16),
            jax.ShapeDtypeStruct((width, width), BF16),
        ),
        in_specs=[anywhere(), vmem(), vmem()],
        out_specs=(vmem(), vmem(), vmem(), vmem()),
        scratch_shapes=[
            pltpu.VMEM((zs, ys, cores, depth, 2 * width), BF16),
            pltpu.VMEM((zs, ys, cores, depth, emb), BF16),
            pltpu.VMEM((zs, ys, cores, depth, width), BF16),
            pltpu.VMEM((zs, ys, cores, depth, width), BF16),
            pltpu.SemaphoreType.DMA((4, cores * ys)),
        ],
        compiler_params=big,
        name="item",
    )(gathered, returned.reshape(shards * CAP, emb), slots)

    length_row = jnp.repeat(lengths[0], items).reshape(1, users * items)
    section = pl.pallas_call(
        section_kernel,
        out_shape=(
            jax.ShapeDtypeStruct((users, width), BF16),
            jax.ShapeDtypeStruct((1, users * items), F32),
        ),
        in_specs=[vmem()] * 7,
        out_specs=(vmem(), vmem()),
        compiler_params=small,
        name="section",
    )
    entering = user_states
    out_state = jnp.zeros_like(user_states)
    out_score = jnp.zeros((1, users * items), F32)
    for step in range(segment_count):
        leaving, score = section(entering, keys, values, ask, back, norm_gains, length_row)
        mine = segment_index == step
        out_state = jnp.where(mine, leaving, out_state)
        out_score = jnp.where(mine, score, out_score)
        if step + 1 < segment_count:
            entering = lax.ppermute(
                leaving, "segment", [(i, i + 1) for i in range(segment_count - 1)]
            )
    return out_state[None], out_score.reshape(1, users, items)


def solution(mesh):
    split = Mesh(mesh.devices.reshape(4, 16, 4, 2), ("segment",) + SHARD)
    in_specs = (
        P(SHARD, None),
        P(SHARD, None),
        P("segment", SHARD, None),
        P("segment", SHARD, None),
        P("segment", SHARD, None),
        P("segment", SHARD, None),
        P("segment", None),
        P("segment", SHARD, None),
        P("segment", SHARD),
    )
    out_specs = (P("segment", SHARD, None), P("segment", SHARD, None))
    return jax.shard_map(
        per_device, mesh=split, in_specs=in_specs, out_specs=out_specs, check_vma=False
    )
```

time: 497 us -> 174 us (0.35)
  waiting for transfers between devices: 232 us -> 37.3 us
  starting transfers between devices: 53.6 us -> 3.91 us
  matrix products: 34.4 us -> 0 us
  local copies, waits for them, and re-layouts: 42.2 us -> 10.1 us
  blocking collectives: 107 us -> 92 us
  Pallas kernels: 0 us -> 14.2 us
  other arithmetic: 10.1 us -> 2 us
    all_gather x3 -> x1, waiting for transfers between devices: 186 us -> 24.5 us  [per_device(): gathered = lax.all_gather(near, ('z', 'core'), axis=0, tiled=True)]
    all_gather x1, blocking collectives: 107 us -> 13.5 us  [per_device(): near = lax.all_gather(own, 'y', axis=0, tiled=True)]
    all_to_all x0 -> x2, blocking collectives: none -> 78.4 us  [the longest x1 44.3 us: per_device(): lax.all_to_all(found, SHARD, split_axis=0, concat_axis=0, tiled=True)]
    all_to_all x4 -> x0, starting transfers between devices: 48.1 us -> none  [the longest x2 33.5 us: request_rows(): lax.all_to_all(request, 'shard', split_axis=0, concat_axis=0, tiled=True)]
    dot_general x22 -> x0, matrix products: 34.4 us -> none  [the longest x5 10.1 us: user_side(): update = jnp.dot(normed, back, preferred_element_type=jnp.float32)]
    all_to_all x4 -> x0, waiting for transfers between devices: 31.5 us -> none  [the longest x2 17.3 us: request_rows(): lax.all_to_all(table_shard[arrived], 'shard', split_axis=0, concat_axis=0...]
    scatter x2 -> x0, local copies, waits for them, and re-layouts: 22.1 us -> none  [request_rows(): jnp.zeros((shard_count, capacity), jnp.int32).at[owners, placing]]
    pallas_call x0 -> x7, Pallas kernels: none -> 14.2 us  [the longest x1 6.34 us: per_device(): pl.pallas_call(item_kernel, out_shape=(jax.ShapeDtypeStruct((users * item...]
  transfers between devices with their start and end apart: 11 -> 4, of which waited for: 8 -> 4; matrix products, arithmetic and copies ran while one was open for 12% -> 0% of each run, Pallas kernels for 0% -> 1%
where the time goes in v1:
time: 174 us
  blocking collectives  92 us (53%)
  waiting for transfers between devices  37.3 us (21%)
  Pallas kernels  14.2 us (8%)
  between operations  14.1 us (8%)
  local copies, waits for them, and re-layouts  10.1 us (6%)
  starting transfers between devices  3.91 us (2%)
  other arithmetic  2 us (1%)
    all_to_all x1, blocking collectives, per_device(): lax.all_to_all(found, SHARD, split_axis=0, concat_axis=0, tiled=True)  44.3 us
    all_to_all x1, blocking collectives, per_device(): lax.all_to_all(request.reshape(shards, 1, CAP), SHARD, split_axis=0, conc...  34.1 us
    all_gather x1, waiting for transfers between devices, per_device(): gathered = lax.all_gather(near, ('z', 'core'), axis=0, tiled=True)  24.5 us
    all_gather x1, blocking collectives, per_device(): near = lax.all_gather(own, 'y', axis=0, tiled=True)  13.5 us
    ppermute x3, waiting for transfers between devices, per_device(): lax.ppermute(leaving, 'segment', [(i, i + 1) for i in range(segment_count...  12.7 us
    unnamed x22, local copies, waits for them, and re-layouts  9.31 us
    pallas_call x1, Pallas kernels, per_device(): pl.pallas_call(item_kernel, out_shape=(jax.ShapeDtypeStruct((users * item...  6.34 us
    pallas_call x4, Pallas kernels, per_device(): section(entering, keys, values, ask, back, norm_gains, length_row)  5.88 us
  transfers between devices with their start and end apart: 4, of which 4 were waited for; matrix products, arithmetic and copies ran while one was open for 0% of the time, Pallas kernels for 1%

profile of v1, /device:TPU:6, one launch (start us, length us, event | category | flops | bytes accessed | tf_op | source)
XLA Modules:
  0.0 173.5 jit_solution(413340490784385680)
XLA Ops:
  7.2 0.0 all-gather.2.cloned.1.call-start
  7.2 0.7 reshape_squeeze.3
  7.9 0.8 pad_maximum_fusion
  8.7 13.5 %all_gather.6 = bf16[32,4352]{1,0:T(8,128)(2,1)} all-gather(bf16[8,4352]{1,0:T(8,128)(2,1)S(1)} %pad_maximum_fusion), channel_id=1, replica_groups=mesh['segment'=4,'z'=16,'y'=4,'core'=2] {'y'}, dimensions={0}, use_global_device_ids=true | all-gather | bytes 348160 | tf_op jit(solution)/shard_map/all_gather | solution.py:214
  22.2 0.0 all-gather.2.cloned.1.call-update
  22.3 0.0 copy-start.9
  22.3 0.7 copy-done.9
  23.0 0.7 request.1
  23.6 34.1 %all_to_all.10 = s32[128,1,8]{2,1,0:T(1,128)S(1)} all-to-all(s32[128,1,8]{2,1,0:T(1,128)S(1)} %bitcast.18), channel_id=1, replica_groups=mesh['segment'=4,'z'=16,'y'=4,'core'=2] {'z','y','core'}, dimensions={0} | all-to-all | bytes 8192 | tf_op jit(solution)/shard_map/all_to_all | solution.py:229
  57.7 0.0 copy-start.6
  57.7 1.2 copy-done.6
  58.9 1.3 table.1
  60.3 44.3 %all_to_all.11 = bf16[128,8,256]{2,1,0:T(8,128)(2,1)} all-to-all(bf16[128,8,256]{2,1,0:T(8,128)(2,1)S(1)} %table.1), channel_id=1, replica_groups=mesh['segment'=4,'z'=16,'y'=4,'core'=2] {'z','y','core'}, dimensions={0} | all-to-all | bytes 1048576 | tf_op jit(solution)/shard_map/all_to_all | solution.py:240
  104.6 24.5 %all-gather.2.cloned.1.call-done = bf16[1024,4352]{1,0:T(8,128)(2,1)} async-done(((bf16[32,4352]{1,0:T(8,128)(2,1)}), bf16[1024,4352]{1,0:T(8,128)(2,1)}) %all-gather.2.cloned.1.call-update) | async-done | bytes 8912912 | tf_op jit(solution)/shard_map/all_gather | solution.py:215
  129.1 0.0 copy-start.4
  129.1 3.5 %copy-done.4 = bf16[1024,4352]{1,0:T(8,128)(2,1)S(1)} copy-done((bf16[1024,4352]{1,0:T(8,128)(2,1)S(1)}, bf16[1024,4352]{1,0:T(8,128)(2,1)}, u32[]{:S(2)}) %copy-start.4) | copy-done | bytes 8912920
  132.7 0.0 copy-start.5
  132.7 1.0 copy-done.5
  133.7 0.0 copy-start.10
  133.7 0.0 copy-start.7
  133.7 0.0 copy-start.8
  133.7 6.3 %item.1 = (bf16[512,1024]{1,0:T(8,128)(2,1)S(1)}, bf16[512,1024]{1,0:T(8,128)(2,1)S(1)}, bf16[1024,1024]{1,0:T(8,128)(2,1)S(1)}, bf16[1024,1024]{1,0:T(8,128)(2,1)S(1)}) custom-call(bf16[16,2,4,8,4352]{4,3,2,1,0:T(8,128)(2,1)S(1)} %bitcast.15, bf16[1024,256]{1,0:T(8,128)(2,1)S(1)} %bitcast.16, s32[4,128]{1,0:T(4,128)S(1)} %get-tuple-element.17.slot_ref), custom_call_target="tpu_custom_call" | custom-call | tf_op jit(solution)/shard_map/item/pallas_call | solution.py:242
  140.1 0.0 copy-start
  140.1 0.0 copy-start.2
  140.1 0.0 copy-done.10
  140.1 0.1 broadcast_in_dim.12
  140.2 0.0 copy-done.7
  140.2 0.0 copy-done.8
  140.2 1.5 section.4
  141.6 1.3 collective-permute-start
  142.9 4.2 %collective-permute-done.state_ref = bf16[4,1024]{1,0:T(4,128)(2,1)S(1)} collective-permute-done((bf16[4,1024]{1,0:T(4,128)(2,1)S(1)}, bf16[4,1024]{1,0:T(4,128)(2,1)S(1)}, u32[]{:S(2)}, u32[]{:S(2)}) %collective-permute-start) | collective-permute-done | bytes 8224 | tf_op jit(solution)/shard_map/ppermute | solution.py:284
  147.2 1.5 section.5
  148.6 1.3 collective-permute-start.1
  149.9 4.2 %collective-permute-done.1.state_ref = bf16[4,1024]{1,0:T(4,128)(2,1)S(1)} collective-permute-done((bf16[4,1024]{1,0:T(4,128)(2,1)S(1)}, bf16[4,1024]{1,0:T(4,128)(2,1)S(1)}, u32[]{:S(2)}, u32[]{:S(2)}) %collective-permute-start.1) | collective-permute-done | bytes 8224 | tf_op jit(solution)/shard_map/ppermute | solution.py:284
  154.2 0.0 copy-done
  154.2 0.0 copy-done.2
  154.2 1.5 section.6
  155.7 1.3 collective-permute-start.2
  157.0 4.2 %collective-permute-done.2.state_ref = bf16[4,1024]{1,0:T(4,128)(2,1)S(1)} collective-permute-done((bf16[4,1024]{1,0:T(4,128)(2,1)S(1)}, bf16[4,1024]{1,0:T(4,128)(2,1)S(1)}, u32[]{:S(2)}, u32[]{:S(2)}) %collective-permute-start.2) | collective-permute-done | bytes 8224 | tf_op jit(solution)/shard_map/ppermute | solution.py:284
  161.2 0.0 copy-start.1
  161.2 1.6 copy-done.1
  162.8 0.0 copy-start.3
  162.8 1.2 copy-done.3
  164.0 1.5 section.7
  165.5 0.6 select_bitcast_fusion
  166.1 0.6 broadcast_select_fusion.3
Async XLA Ops:
  7.2 122.0 %all-gather.2.cloned.1.call-start = ((), (), s32[]{:S(2)}) async-start(), calls=%async_computation.2 | async-start | bytes 9191424 | tf_op jit(solution)/shard_map/all_gather | solution.py:215
  22.3 0.7 copy-start.9
  57.7 1.2 copy-start.6
  129.1 3.5 %copy-start.4 = (bf16[1024,4352]{1,0:T(8,128)(2,1)S(1)}, bf16[1024,4352]{1,0:T(8,128)(2,1)}, u32[]{:S(2)}) copy-start(bf16[1024,4352]{1,0:T(8,128)(2,1)} %all-gather.2.cloned.1.call-done) | copy-start | bytes 26738692
  132.7 1.0 copy-start.5
  133.7 6.4 %copy-start.10 = (s32[1,4]{1,0:T(1,128)S(1)}, s32[1,4]{1,0:T(1,128)}, u32[]{:S(2)}) copy-start(s32[1,4]{1,0:T(1,128)} %param.17) | copy-start | bytes 52
  133.7 6.5 %copy-start.7 = (f32[1,1024]{1,0:T(1,128)S(1)}, f32[1,1024]{1,0:T(1,128)}, u32[]{:S(2)}) copy-start(f32[1,1024]{1,0:T(1,128)} %gain_ref.7) | copy-start | bytes 12292
  133.7 6.5 %copy-start.8 = (bf16[4,1024]{1,0:T(4,128)(2,1)S(1)}, bf16[4,1024]{1,0:T(4,128)(2,1)}, u32[]{:S(2)}) copy-start(bf16[4,1024]{1,0:T(4,128)(2,1)} %state_ref.1) | copy-start | bytes 24580
  140.1 14.1 %copy-start = (bf16[1024,1024]{1,0:T(8,128)(2,1)}, bf16[1024,1024]{1,0:T(8,128)(2,1)S(1)}, u32[]{:S(2)}) copy-start(bf16[1024,1024]{1,0:T(8,128)(2,1)S(1)} %get-tuple-element.21.back_ref) | copy-start | bytes 6291460
  140.1 14.1 %copy-start.2 = (bf16[512,1024]{1,0:T(8,128)(2,1)}, bf16[512,1024]{1,0:T(8,128)(2,1)S(1)}, u32[]{:S(2)}) copy-start(bf16[512,1024]{1,0:T(8,128)(2,1)S(1)} %get-tuple-element.19.value_ref) | copy-start | bytes 3145732
  141.6 5.5 %collective-permute-start = (bf16[4,1024]{1,0:T(4,128)(2,1)S(1)}, bf16[4,1024]{1,0:T(4,128)(2,1)S(1)}, u32[]{:S(2)}, u32[]{:S(2)}) collective-permute-start(bf16[4,1024]{1,0:T(4,128)(2,1)S(1)} %get-tuple-element.22), channel_id=1, source_target_pairs={{0,128},{128,256},{256,384},{1,129},{129,257},{257,385},{2,130},{1... | collective-permute-start | bytes 24584 | tf_op jit(solution)/shard_map/ppermute | solution.py:284
  148.6 5.5 %collective-permute-start.1 = (bf16[4,1024]{1,0:T(4,128)(2,1)S(1)}, bf16[4,1024]{1,0:T(4,128)(2,1)S(1)}, u32[]{:S(2)}, u32[]{:S(2)}) collective-permute-start(bf16[4,1024]{1,0:T(4,128)(2,1)S(1)} %get-tuple-element.23), channel_id=1, source_target_pairs={{0,128},{128,256},{256,384},{1,129},{129,257},{257,385},{2,130},{1... | collective-permute-start | bytes 24584 | tf_op jit(solution)/shard_map/ppermute | solution.py:284
  155.7 5.5 %collective-permute-start.2 = (bf16[4,1024]{1,0:T(4,128)(2,1)S(1)}, bf16[4,1024]{1,0:T(4,128)(2,1)S(1)}, u32[]{:S(2)}, u32[]{:S(2)}) collective-permute-start(bf16[4,1024]{1,0:T(4,128)(2,1)S(1)} %get-tuple-element.24), channel_id=1, source_target_pairs={{0,128},{128,256},{256,384},{1,129},{129,257},{257,385},{2,130},{1... | collective-permute-start | bytes 24584 | tf_op jit(solution)/shard_map/ppermute | solution.py:284
  161.2 1.6 copy-start.1
  162.8 1.2 copy-start.3
Sparse Core Ops, SparseCore 0:
  22.4 106.6 all-gather.1

commit v2 on v1

v2 whole, which is shorter than its diff:
```python
import math

import jax
import jax.numpy as jnp
from jax import lax
from jax.experimental import pallas as pl
from jax.experimental.pallas import tpu as pltpu
from jax.sharding import Mesh
from jax.sharding import PartitionSpec as P

HEADS = 8
BU = 2
CAP = 8
F32 = jnp.float32
BF16 = jnp.bfloat16
SHARD = ("z", "y", "core")


def vmem():
    return pl.BlockSpec(memory_space=pltpu.VMEM)


def request_kernel(shard_rows, ids_ref, request_ref, slot_ref):
    users, items = ids_ref.shape
    shards, capacity = request_ref.shape
    ids = ids_ref[...]
    owners = ids // shard_rows
    offsets = ids - owners * shard_rows
    owner_row = lax.broadcasted_iota(jnp.int32, (shards, items), 0)
    before = (
        lax.broadcasted_iota(jnp.int32, (items, items), 0)
        < lax.broadcasted_iota(jnp.int32, (items, items), 1)
    ).astype(BF16)
    place_row = lax.broadcasted_iota(jnp.int32, (capacity, items), 0)
    base = jnp.zeros((shards, 1), F32)
    high = jnp.zeros((shards, capacity), F32)
    low = jnp.zeros((shards, capacity), F32)
    for user in range(users):
        mine = owner_row == owners[user : user + 1, :]
        onehot = mine.astype(F32)
        onehot_low = onehot.astype(BF16)
        earlier = jnp.dot(onehot_low, before, preferred_element_type=F32) + base
        place = jnp.sum(onehot * earlier, axis=0, keepdims=True).astype(jnp.int32)
        base = base + jnp.sum(onehot, axis=1, keepdims=True)
        at_place = place_row == place
        offset = offsets[user : user + 1, :]
        offset_high = jnp.where(at_place, offset // 64, 0).astype(F32).astype(BF16)
        offset_low = jnp.where(at_place, offset % 64, 0).astype(F32).astype(BF16)
        contract = (((1,), (1,)), ((), ()))
        high = high + lax.dot_general(
            onehot_low, offset_high, contract, preferred_element_type=F32
        )
        low = low + lax.dot_general(
            onehot_low, offset_low, contract, preferred_element_type=F32
        )
        slot_ref[user : user + 1, :] = owners[user : user + 1, :] * capacity + place
    request_ref[...] = (high * 64.0 + low).astype(jnp.int32)


def table_kernel(arrived_ref, table_ref, rows_ref):
    shards, capacity, width = rows_ref.shape
    shard_rows = table_ref.shape[0]
    block = 32
    count = block * capacity
    diagonal = lax.broadcasted_iota(
        jnp.int32, (block, capacity, capacity), 1
    ) == lax.broadcasted_iota(jnp.int32, (block, capacity, capacity), 2)
    row = lax.broadcasted_iota(jnp.int32, (count, shard_rows), 1)
    for start in range(0, shards, block):
        asked = arrived_ref[start : start + block, :]
        spread = jnp.broadcast_to(asked[:, None, :], (block, capacity, capacity))
        column = jnp.sum(jnp.where(diagonal, spread, 0).astype(F32), axis=2, keepdims=True)
        column = column.astype(jnp.int32).reshape(count, 1)
        onehot = (row == column).astype(F32).astype(BF16)
        found = jnp.dot(onehot, table_ref[...], preferred_element_type=F32)
        rows_ref[start : start + block] = found.astype(BF16).reshape(block, capacity, width)


def list_kernel(
    count_ref,
    returned_ref,
    slot_ref,
    state_ref,
    gain_ref,
    listed_ref,
    state_out_ref,
    gain_out_ref,
    length_ref,
):
    users, items = slot_ref.shape
    state_out_ref[...] = state_ref[...]
    gain_out_ref[...] = gain_ref[...]
    owner = lax.broadcasted_iota(jnp.int32, length_ref.shape, 1) // items
    lengths = jnp.zeros(length_ref.shape, jnp.int32)
    for user in range(users):
        lengths = jnp.where(owner == user, count_ref[0, user], lengths)
    length_ref[...] = lengths
    slots = slot_ref[...]
    slot_row = lax.broadcasted_iota(jnp.int32, (returned_ref.shape[0], items), 0)
    returned = returned_ref[...]
    for user in range(users):
        onehot = (slot_row == slots[user : user + 1, :]).astype(F32).astype(BF16)
        listed_ref[user * items : (user + 1) * items, :] = lax.dot_general(
            onehot, returned, (((0,), (0,)), ((), ())), preferred_element_type=F32
        ).astype(BF16)


def section_step(state, keys, values, ask, back, gain, lengths):
    users, width = state.shape
    count = keys.shape[0]
    items = count // users
    head_size = width // HEADS
    rows = users * HEADS
    query = jnp.dot(state, ask(), preferred_element_type=F32).astype(BF16)
    spread = jnp.broadcast_to(query.astype(F32)[:, None, :], (users, HEADS, width)).reshape(
        rows, width
    )
    in_head = (
        lax.broadcasted_iota(jnp.int32, (rows, width), 1) // head_size
        == lax.broadcasted_iota(jnp.int32, (rows, width), 0) % HEADS
    )
    spread = jnp.where(in_head, spread, 0.0).astype(BF16)
    logits = lax.dot_general(
        spread, keys[...], (((1,), (1,)), ((), ())), preferred_element_type=F32
    ) * (1.0 / math.sqrt(head_size))
    column = lax.broadcasted_iota(jnp.int32, (rows, count), 1)
    owner = lax.broadcasted_iota(jnp.int32, (rows, count), 0) // HEADS
    live = (column // items == owner) & (column % items < lengths)
    weights = jnp.where(live, jax.nn.silu(logits), 0.0)
    score = jnp.sum(weights, axis=0, keepdims=True) * (1.0 / HEADS)
    mixed = jnp.dot(weights.astype(BF16), values[...], preferred_element_type=F32)
    mixed = jnp.where(in_head, mixed, 0.0).reshape(users, HEADS, width)
    attended = jnp.sum(mixed, axis=1)
    scale = lax.rsqrt(jnp.mean(attended * attended, axis=1, keepdims=True) + 1e-05)
    normed = (attended * scale * gain).astype(BF16)
    update = jnp.dot(normed, back(), preferred_element_type=F32)
    return (state.astype(F32) + update).astype(BF16), score


def item_kernel(
    gathered_ref,
    listed_ref,
    state_ref,
    gain_ref,
    length_ref,
    key_ref,
    value_ref,
    weight_ref,
    next_ref,
    score_ref,
    sems,
):
    _, cores, ys, _, columns = gathered_ref.shape
    depth, width = key_ref.shape[1], key_ref.shape[1]
    emb = listed_ref.shape[1]
    copies = []
    for part, (first, size) in enumerate(
        ((4 * width, emb), (0, 2 * width), (2 * width, 2 * width))
    ):
        mine = []
        for core in range(cores):
            for y in range(ys):
                copy = pltpu.make_async_copy(
                    gathered_ref.at[:, core, y, :, pl.ds(first, size)],
                    weight_ref.at[:, y, core, :, pl.ds(first, size)],
                    sems.at[part, core * ys + y],
                )
                copy.start()
                mine.append(copy)
        copies.append(mine)

    def weight(first, size):
        return weight_ref[:, :, :, :, first : first + size].reshape(depth, size)

    for copy in copies[0]:
        copy.wait()
    listed = listed_ref[...]
    packed = weight(4 * width, emb)
    split = depth // emb
    lifted = []
    for part in range(split):
        pick = (
            lax.broadcasted_iota(jnp.int32, (emb, depth), 0) * split + part
            == lax.broadcasted_iota(jnp.int32, (emb, depth), 1)
        )
        lift = jnp.dot(
            pick.astype(F32).astype(BF16), packed, preferred_element_type=F32
        ).astype(BF16)
        lifted.append(
            jax.nn.silu(jnp.dot(listed, lift, preferred_element_type=F32)).astype(BF16)
        )
    lifted = jnp.concatenate(lifted, axis=1)
    for copy in copies[1]:
        copy.wait()
    block = 512
    for first in range(0, 2 * width, block):
        made = jnp.dot(lifted, weight(first, block), preferred_element_type=F32).astype(BF16)
        if first < width:
            key_ref[:, first : first + block] = made
        else:
            value_ref[:, first - width : first - width + block] = made
    for copy in copies[2]:
        copy.wait()
    next_ref[...], score_ref[...] = section_step(
        state_ref[...],
        key_ref,
        value_ref,
        lambda: weight(2 * width, width),
        lambda: weight(3 * width, width),
        gain_ref[...],
        length_ref[...],
    )


def section_kernel(
    state_ref, key_ref, value_ref, weight_ref, gain_ref, length_ref, *others
):
    next_ref, score_ref = others[-2:]
    earlier = (len(others) - 2) // 2
    width = state_ref.shape[1]
    state, score = section_step(
        state_ref[...],
        key_ref,
        value_ref,
        lambda: weight_ref[:, 2 * width : 3 * width],
        lambda: weight_ref[:, 3 * width : 4 * width],
        gain_ref[...],
        length_ref[...],
    )
    segment_index = lax.axis_index("segment") if earlier else None
    for step in range(earlier):
        mine = segment_index == step
        state = jnp.where(mine, others[step][...], state)
        score = jnp.where(mine, others[earlier + step][...], score)
    next_ref[...] = state
    score_ref[...] = score


def per_device(
    item_table, user_states, w_lift, w_pair, w_ask, w_back, norm_gains, item_ids, lengths
):
    segment_count = lax.axis_size("segment")
    zs, ys, cores = (lax.axis_size(name) for name in SHARD)
    shards = zs * ys * cores
    users, width = user_states.shape
    items = item_ids.shape[2]
    shard_rows, emb = item_table.shape
    depth = w_ask.shape[1]
    small, big = (pltpu.CompilerParams(vmem_limit_bytes=size << 20) for size in (12, 38))

    own = jnp.concatenate(
        [w_pair[0], w_ask[0], w_back[0], w_lift[0].reshape(depth, emb)], axis=1
    )
    near = lax.all_gather(own, "y", axis=0, tiled=True)
    gathered = lax.all_gather(near, ("z", "core"), axis=0, tiled=True)
    gathered = gathered.reshape(zs, cores, ys, depth, own.shape[1])

    request, slots = pl.pallas_call(
        lambda *refs: request_kernel(shard_rows, *refs),
        out_shape=(
            jax.ShapeDtypeStruct((shards, CAP), jnp.int32),
            jax.ShapeDtypeStruct((users, items), jnp.int32),
        ),
        in_specs=[vmem()],
        out_specs=(vmem(), vmem()),
        compiler_params=small,
        name="request",
    )(item_ids[0])
    arrived = lax.all_to_all(
        request.reshape(shards, 1, CAP), SHARD, split_axis=0, concat_axis=0, tiled=True
    )
    found = pl.pallas_call(
        table_kernel,
        out_shape=jax.ShapeDtypeStruct((shards, CAP, emb), BF16),
        in_specs=[vmem(), vmem()],
        out_specs=vmem(),
        compiler_params=small,
        name="table",
    )(arrived.reshape(shards, CAP), item_table)
    returned = lax.all_to_all(found, SHARD, split_axis=0, concat_axis=0, tiled=True)

    smem = pl.BlockSpec(memory_space=pltpu.SMEM)
    listed, entering, gains, length_row = pl.pallas_call(
        list_kernel,
        out_shape=(
            jax.ShapeDtypeStruct((users * items, emb), BF16),
            jax.ShapeDtypeStruct(user_states.shape, BF16),
            jax.ShapeDtypeStruct(norm_gains.shape, F32),
            jax.ShapeDtypeStruct((1, users * items), jnp.int32),
        ),
        in_specs=[smem] + [vmem()] * 4,
        out_specs=(vmem(),) * 4,
        compiler_params=small,
        name="list",
    )(lengths, returned.reshape(shards * CAP, emb), slots, user_states, norm_gains)

    section_shape = (
        jax.ShapeDtypeStruct((users, width), BF16),
        jax.ShapeDtypeStruct((1, users * items), F32),
    )
    keys, values, weights, leaving, score = pl.pallas_call(
        item_kernel,
        out_shape=(
            jax.ShapeDtypeStruct((users * items, width), BF16),
            jax.ShapeDtypeStruct((users * items, width), BF16),
            jax.ShapeDtypeStruct((zs, ys, cores, depth, own.shape[1]), BF16),
        )
        + section_shape,
        in_specs=[pl.BlockSpec(memory_space=pltpu.HBM)] + [vmem()] * 4,
        out_specs=(vmem(),) * 5,
        scratch_shapes=[pltpu.SemaphoreType.DMA((3, cores * ys))],
        compiler_params=big,
        name="item",
    )(gathered, listed, entering, gains, length_row)
    weights = weights.reshape(shards * depth, own.shape[1])

    states, scores = [leaving], [score]
    for step in range(1, segment_count):
        entering = lax.ppermute(
            leaving, "segment", [(i, i + 1) for i in range(segment_count - 1)]
        )
        earlier = (*states, *scores) if step + 1 == segment_count else ()
        leaving, score = pl.pallas_call(
            section_kernel,
            out_shape=section_shape,
            in_specs=[vmem()] * (6 + len(earlier)),
            out_specs=(vmem(), vmem()),
            compiler_params=small,
            name="section",
        )(
            entering,
            keys,
            values,
            weights,
            gains,
            length_row,
            *earlier,
        )
        states.append(leaving)
        scores.append(score)
    return leaving[None], score.reshape(1, users, items)


def solution(mesh):
    split = Mesh(mesh.devices.reshape(4, 16, 4, 2), ("segment",) + SHARD)
    in_specs = (
        P(SHARD, None),
        P(SHARD, None),
        P("segment", SHARD, None),
        P("segment", SHARD, None),
        P("segment", SHARD, None),
        P("segment", SHARD, None),
        P("segment", None),
        P("segment", SHARD, None),
        P("segment", SHARD),
    )
    out_specs = (P("segment", SHARD, None), P("segment", SHARD, None))
    return jax.shard_map(
        per_device, mesh=split, in_specs=in_specs, out_specs=out_specs, check_vma=False
    )
```

time: 174 us -> 166 us (0.954)
  local copies, waits for them, and re-layouts: 10.1 us -> 4.64 us
  waiting for transfers between devices: 37.3 us -> 34.5 us
    unnamed x22 -> x10, local copies, waits for them, and re-layouts: 9.31 us -> 3.94 us
    all_gather x1, waiting for transfers between devices: 24.5 us -> 21.8 us  [per_device(): gathered = lax.all_gather(near, ('z', 'core'), axis=0, tiled=True)]
  transfers between devices with their start and end apart: 4 -> 4, of which waited for: 4 -> 4; matrix products, arithmetic and copies ran while one was open for 0% -> 0% of each run, Pallas kernels for 1% -> 2%
where the time goes in v2:
time: 166 us; the launch traced here: 165 us
  blocking collectives  91.8 us (55%)
  waiting for transfers between devices  34.5 us (21%)
  Pallas kernels  15.4 us (9%)
  between operations  14.1 us (8%)
  local copies, waits for them, and re-layouts  4.64 us (3%)
  starting transfers between devices  3.91 us (2%)
    all_to_all x1, blocking collectives, per_device(): lax.all_to_all(found, SHARD, split_axis=0, concat_axis=0, tiled=True)  44.1 us
    all_to_all x1, blocking collectives, per_device(): lax.all_to_all(request.reshape(shards, 1, CAP), SHARD, split_axis=0, conc...  34.1 us
    all_gather x1, waiting for transfers between devices, per_device(): gathered = lax.all_gather(near, ('z', 'core'), axis=0, tiled=True)  21.8 us
    all_gather x1, blocking collectives, per_device(): near = lax.all_gather(own, 'y', axis=0, tiled=True)  13.5 us
    ppermute x3, waiting for transfers between devices, per_device(): lax.ppermute(leaving, 'segment', [(i, i + 1) for i in range(segment_count...  12.7 us
    pallas_call x1, Pallas kernels, per_device(): pl.pallas_call(item_kernel, out_shape=(jax.ShapeDtypeStruct((users * item...  7.36 us
    pallas_call x3, Pallas kernels, per_device(): pl.pallas_call(section_kernel, out_shape=section_shape, in_specs=[vmem()]...  5.01 us
    unnamed x10, local copies, waits for them, and re-layouts  3.94 us
  transfers between devices with their start and end apart: 4, of which 4 were waited for; matrix products, arithmetic and copies ran while one was open for 0% of the time, Pallas kernels for 2%

profile of v2, /device:TPU:6, one launch (start us, length us, event | category | flops | bytes accessed | tf_op | source)
XLA Modules:
  0.0 165.1 jit_solution(9169909627231956843)
XLA Ops:
  7.2 0.0 all-gather.2.cloned.1.call-start
  7.2 0.7 reshape_squeeze.3
  7.9 0.8 pad_maximum_fusion
  8.7 13.5 %all_gather.6 = bf16[32,4352]{1,0:T(8,128)(2,1)} all-gather(bf16[8,4352]{1,0:T(8,128)(2,1)S(1)} %pad_maximum_fusion), channel_id=1, replica_groups=mesh['segment'=4,'z'=16,'y'=4,'core'=2] {'y'}, dimensions={0}, use_global_device_ids=true | all-gather | bytes 348160 | tf_op jit(solution)/shard_map/all_gather | solution.py:254
  22.2 0.0 all-gather.2.cloned.1.call-update
  22.3 0.0 copy-start.3
  22.3 0.7 copy-done.3
  23.0 0.7 request.1
  23.6 34.1 %all_to_all.10 = s32[128,1,8]{2,1,0:T(1,128)S(1)} all-to-all(s32[128,1,8]{2,1,0:T(1,128)S(1)} %bitcast.18), channel_id=1, replica_groups=mesh['segment'=4,'z'=16,'y'=4,'core'=2] {'z','y','core'}, dimensions={0} | all-to-all | bytes 8192 | tf_op jit(solution)/shard_map/all_to_all | solution.py:269
  57.7 0.0 copy-start
  57.7 1.2 copy-done
  58.9 1.3 table.1
  60.3 44.1 %all_to_all.11 = bf16[128,8,256]{2,1,0:T(8,128)(2,1)S(1)} all-to-all(bf16[128,8,256]{2,1,0:T(8,128)(2,1)S(1)} %table.1), channel_id=1, replica_groups=mesh['segment'=4,'z'=16,'y'=4,'core'=2] {'z','y','core'}, dimensions={0} | all-to-all | bytes 1048576 | tf_op jit(solution)/shard_map/all_to_all | solution.py:280
  104.4 0.0 copy-start.1
  104.4 0.7 copy-done.1
  105.1 0.0 copy-start.2
  105.1 0.7 copy-done.2
  105.8 0.0 copy-start.4
  105.8 0.7 copy-done.4
  106.4 1.0 list.1
  107.5 21.8 %all-gather.2.cloned.1.call-done = bf16[1024,4352]{1,0:T(8,128)(2,1)} async-done(((bf16[32,4352]{1,0:T(8,128)(2,1)}), bf16[1024,4352]{1,0:T(8,128)(2,1)}) %all-gather.2.cloned.1.call-update) | async-done | bytes 8912912 | tf_op jit(solution)/shard_map/all_gather | solution.py:255
  129.2 7.4 %item.1 = (bf16[512,1024]{1,0:T(8,128)(2,1)S(1)}, bf16[512,1024]{1,0:T(8,128)(2,1)S(1)}, bf16[16,4,2,8,4352]{4,3,2,1,0:T(8,128)(2,1)S(1)}, bf16[4,1024]{1,0:T(4,128)(2,1)S(1)}, f32[1,512]{1,0:T(1,128)S(1)}) custom-call(bf16[16,2,4,8,4352]{4,3,2,1,0:T(8,128)(2,1)} %bitcast.20, bf16[512,256]{1,0:T(8,128)(2,1)S(1)} %get-tuple-element.21.listed_ref, ...), custom_call_target="tpu_custom_call" | custom-call | tf_op jit(solution)/shard_map/item/pallas_call | solution.py:301
  136.6 1.3 collective-permute-start
  137.9 4.2 %collective-permute-done.state_ref = bf16[4,1024]{1,0:T(4,128)(2,1)S(1)} collective-permute-done((bf16[4,1024]{1,0:T(4,128)(2,1)S(1)}, bf16[4,1024]{1,0:T(4,128)(2,1)S(1)}, u32[]{:S(2)}, u32[]{:S(2)}) %collective-permute-start) | collective-permute-done | bytes 8224 | tf_op jit(solution)/shard_map/ppermute | solution.py:319
  142.2 1.5 section.3
  143.6 1.3 collective-permute-start.1
  144.9 4.2 %collective-permute-done.1.state_ref = bf16[4,1024]{1,0:T(4,128)(2,1)S(1)} collective-permute-done((bf16[4,1024]{1,0:T(4,128)(2,1)S(1)}, bf16[4,1024]{1,0:T(4,128)(2,1)S(1)}, u32[]{:S(2)}, u32[]{:S(2)}) %collective-permute-start.1) | collective-permute-done | bytes 8224 | tf_op jit(solution)/shard_map/ppermute | solution.py:319
  149.2 1.5 section.4
  150.6 1.3 collective-permute-start.2
  151.9 4.2 %collective-permute-done.2.state_ref = bf16[4,1024]{1,0:T(4,128)(2,1)S(1)} collective-permute-done((bf16[4,1024]{1,0:T(4,128)(2,1)S(1)}, bf16[4,1024]{1,0:T(4,128)(2,1)S(1)}, u32[]{:S(2)}, u32[]{:S(2)}) %collective-permute-start.2) | collective-permute-done | bytes 8224 | tf_op jit(solution)/shard_map/ppermute | solution.py:319
  156.2 2.1 %section.5 = (bf16[4,1024]{1,0:T(4,128)(2,1)}, f32[1,512]{1,0:T(1,128)}) custom-call(bf16[4,1024]{1,0:T(4,128)(2,1)S(1)} %collective-permute-done.2.state_ref, bf16[512,1024]{1,0:T(8,128)(2,1)S(1)} %get-tuple-element.26.key_ref, bf16[512,1024]{1,0:T(8,128)(2,1)S(1)} %get-tuple-element.27.value_ref, bf16[1024,4352]{1,0:T(8,128)(2,1)S(1)} %bitcast.15, ...), custom_call_target="tpu_custom_call" | custom-call | tf_op jit(solution)/shard_map/section/pallas_call | solution.py:323
Async XLA Ops:
  7.2 122.1 %all-gather.2.cloned.1.call-start = ((), (), s32[]{:S(2)}) async-start(), calls=%async_computation.2 | async-start | bytes 9191424 | tf_op jit(solution)/shard_map/all_gather | solution.py:255
  22.3 0.7 copy-start.3
  57.7 1.2 copy-start
  104.4 0.7 copy-start.1
  105.1 0.7 copy-start.2
  105.8 0.7 copy-start.4
  136.6 5.5 %collective-permute-start = (bf16[4,1024]{1,0:T(4,128)(2,1)S(1)}, bf16[4,1024]{1,0:T(4,128)(2,1)S(1)}, u32[]{:S(2)}, u32[]{:S(2)}) collective-permute-start(bf16[4,1024]{1,0:T(4,128)(2,1)S(1)} %get-tuple-element.25.others_0_), channel_id=1, source_target_pairs={{0,128},{128,256},{256,384},{1,129},{129,257},{257,385},{2,130},{1... | collective-permute-start | bytes 24584 | tf_op jit(solution)/shard_map/ppermute | solution.py:319
  143.6 5.5 %collective-permute-start.1 = (bf16[4,1024]{1,0:T(4,128)(2,1)S(1)}, bf16[4,1024]{1,0:T(4,128)(2,1)S(1)}, u32[]{:S(2)}, u32[]{:S(2)}) collective-permute-start(bf16[4,1024]{1,0:T(4,128)(2,1)S(1)} %get-tuple-element.29.others_1_), channel_id=1, source_target_pairs={{0,128},{128,256},{256,384},{1,129},{129,257},{257,385},{2,130},{1... | collective-permute-start | bytes 24584 | tf_op jit(solution)/shard_map/ppermute | solution.py:319
  150.6 5.5 %collective-permute-start.2 = (bf16[4,1024]{1,0:T(4,128)(2,1)S(1)}, bf16[4,1024]{1,0:T(4,128)(2,1)S(1)}, u32[]{:S(2)}, u32[]{:S(2)}) collective-permute-start(bf16[4,1024]{1,0:T(4,128)(2,1)S(1)} %get-tuple-element.30.others_2_), channel_id=1, source_target_pairs={{0,128},{128,256},{256,384},{1,129},{129,257},{257,385},{2,130},{1... | collective-permute-start | bytes 24584 | tf_op jit(solution)/shard_map/ppermute | solution.py:319
Sparse Core Ops, SparseCore 0:
  22.4 106.8 all-gather.1

commit v3 on v2

--- a/solution.py
+++ b/solution.py
@@ -217,9 +217,9 @@
 ):
     next_ref, score_ref = others[-2:]
     earlier = (len(others) - 2) // 2
-    width = state_ref.shape[1]
+    width = state_ref.shape[2]
     state, score = section_step(
-        state_ref[...],
+        state_ref[0],
         key_ref,
         value_ref,
         lambda: weight_ref[:, 2 * width : 3 * width],
@@ -251,7 +251,9 @@
     own = jnp.concatenate(
         [w_pair[0], w_ask[0], w_back[0], w_lift[0].reshape(depth, emb)], axis=1
     )
-    near = lax.all_gather(own, "y", axis=0, tiled=True)
+    even, odd = [[0, 1], [2, 3]], [[1, 2], [0, 3]]
+    near = lax.all_gather(own, "y", axis=0, tiled=True, axis_index_groups=even)
+    near = lax.all_gather(near, "y", axis=0, tiled=True, axis_index_groups=odd)
     gathered = lax.all_gather(near, ("z", "core"), axis=0, tiled=True)
     gathered = gathered.reshape(zs, cores, ys, depth, own.shape[1])
 
@@ -316,8 +318,8 @@
 
     states, scores = [leaving], [score]
     for step in range(1, segment_count):
-        entering = lax.ppermute(
-            leaving, "segment", [(i, i + 1) for i in range(segment_count - 1)]
+        entering = lax.all_gather(
+            leaving, "segment", axis=0, axis_index_groups=even if step % 2 else odd
         )
         earlier = (*states, *scores) if step + 1 == segment_count else ()
         leaving, score = pl.pallas_call(

time: 166 us -> 162 us (0.976)
  blocking collectives: 91.8 us -> 105 us
  waiting for transfers between devices: 34.5 us -> 22.2 us
  starting transfers between devices: 3.91 us -> 0.04 us
    all_gather x1 -> x5, blocking collectives: 13.5 us -> 26.3 us  [the longest x3 14.3 us: per_device(): lax.all_gather(leaving, 'segment', axis=0, axis_index_groups=even if step...]
    ppermute x3 -> x0, waiting for transfers between devices: 12.7 us -> none  [per_device(): lax.ppermute(leaving, 'segment', [(i, i + 1) for i in range(segment_count...]
    ppermute x3 -> x0, starting transfers between devices: 3.87 us -> none  [per_device(): lax.ppermute(leaving, 'segment', [(i, i + 1) for i in range(segment_count...]
  transfers between devices with their start and end apart: 4 -> 1, of which waited for: 4 -> 1; matrix products, arithmetic and copies ran while one was open for 0% -> 0% of each run, Pallas kernels for 2% -> 2%
where the time goes in v3:
time: 162 us
  blocking collectives  105 us (65%)
  waiting for transfers between devices  22.2 us (14%)
  Pallas kernels  15.4 us (10%)
  between operations  14.1 us (9%)
  local copies, waits for them, and re-layouts  4.64 us (3%)
    all_to_all x1, blocking collectives, per_device(): lax.all_to_all(found, SHARD, split_axis=0, concat_axis=0, tiled=True)  44.1 us
    all_to_all x1, blocking collectives, per_device(): lax.all_to_all(request.reshape(shards, 1, CAP), SHARD, split_axis=0, conc...  34.4 us
    all_gather x1, waiting for transfers between devices, per_device(): gathered = lax.all_gather(near, ('z', 'core'), axis=0, tiled=True)  22.2 us
    all_gather x3, blocking collectives, per_device(): lax.all_gather(leaving, 'segment', axis=0, axis_index_groups=even if step...  14.3 us
    pallas_call x1, Pallas kernels, per_device(): pl.pallas_call(item_kernel, out_shape=(jax.ShapeDtypeStruct((users * item...  7.36 us
    all_gather x1, blocking collectives, per_device(): near = lax.all_gather(near, 'y', axis=0, tiled=True, axis_index_groups=odd)  7.04 us
    pallas_call x3, Pallas kernels, per_device(): pl.pallas_call(section_kernel, out_shape=section_shape, in_specs=[vmem()]...  5.01 us
    all_gather x1, blocking collectives, per_device(): near = lax.all_gather(own, 'y', axis=0, tiled=True, axis_index_groups=even)  4.97 us
  transfers between devices with their start and end apart: 1, of which 1 were waited for; matrix products, arithmetic and copies ran while one was open for 0% of the time, Pallas kernels for 2%

profile of v3, /device:TPU:6, one launch (start us, length us, event | category | flops | bytes accessed | tf_op | source)
XLA Modules:
  0.0 162.0 jit_solution(11625472464303053259)
XLA Ops:
  7.2 0.0 all-gather.8.cloned.1.call-start
  7.2 0.7 reshape_squeeze.3
  7.9 0.8 pad_maximum_fusion
  8.7 5.0 %all_gather.27 = bf16[16,4352]{1,0:T(8,128)(2,1)S(1)} all-gather(bf16[8,4352]{1,0:T(8,128)(2,1)S(1)} %pad_maximum_fusion), channel_id=1, replica_groups={{0,2},{4,6},{1,3},{5,7},{8,10},{12,14},{9,11},{13,15},{16,18},{20,22},{..., dimensions={0}, use_global_device_ids=true | all-gather | bytes 208896 | tf_op jit(solution)/shard_map/all_gather | solution.py:255
  13.7 7.0 %all_gather.28 = bf16[32,4352]{1,0:T(8,128)(2,1)} all-gather(bf16[16,4352]{1,0:T(8,128)(2,1)S(1)} %all_gather.27), channel_id=1, replica_groups={{2,4},{0,6},{3,5},{1,7},{10,12},{8,14},{11,13},{9,15},{18,20},{16,22},{..., dimensions={0}, use_global_device_ids=true | all-gather | bytes 417792 | tf_op jit(solution)/shard_map/all_gather | solution.py:256
  20.7 0.0 all-gather.8.cloned.1.call-update
  20.7 0.0 copy-start.3
  20.8 0.7 copy-done.3
  21.4 0.7 request.1
  22.1 34.4 %all_to_all.10 = s32[128,1,8]{2,1,0:T(1,128)S(1)} all-to-all(s32[128,1,8]{2,1,0:T(1,128)S(1)} %bitcast.21), channel_id=1, replica_groups=mesh['segment'=4,'z'=16,'y'=4,'core'=2] {'z','y','core'}, dimensions={0} | all-to-all | bytes 8192 | tf_op jit(solution)/shard_map/all_to_all | solution.py:271
  56.5 0.0 copy-start
  56.5 1.2 copy-done
  57.7 1.3 table.1
  59.1 44.1 %all_to_all.11 = bf16[128,8,256]{2,1,0:T(8,128)(2,1)S(1)} all-to-all(bf16[128,8,256]{2,1,0:T(8,128)(2,1)S(1)} %table.1), channel_id=1, replica_groups=mesh['segment'=4,'z'=16,'y'=4,'core'=2] {'z','y','core'}, dimensions={0} | all-to-all | bytes 1048576 | tf_op jit(solution)/shard_map/all_to_all | solution.py:282
  103.2 0.0 copy-start.1
  103.2 0.7 copy-done.1
  103.9 0.0 copy-start.2
  103.9 0.7 copy-done.2
  104.6 0.0 copy-start.4
  104.6 0.7 copy-done.4
  105.2 1.0 list.1
  106.3 22.2 %all-gather.8.cloned.1.call-done = bf16[1024,4352]{1,0:T(8,128)(2,1)} async-done(((bf16[32,4352]{1,0:T(8,128)(2,1)}), bf16[1024,4352]{1,0:T(8,128)(2,1)}) %all-gather.8.cloned.1.call-update) | async-done | bytes 8912912 | tf_op jit(solution)/shard_map/all_gather | solution.py:257
  128.5 7.4 %item.1 = (bf16[512,1024]{1,0:T(8,128)(2,1)S(1)}, bf16[512,1024]{1,0:T(8,128)(2,1)S(1)}, bf16[16,4,2,8,4352]{4,3,2,1,0:T(8,128)(2,1)S(1)}, bf16[4,1024]{1,0:T(4,128)(2,1)S(1)}, f32[1,512]{1,0:T(1,128)S(1)}) custom-call(bf16[16,2,4,8,4352]{4,3,2,1,0:T(8,128)(2,1)} %bitcast.26, bf16[512,256]{1,0:T(8,128)(2,1)S(1)} %get-tuple-element.21.listed_ref, ...), custom_call_target="tpu_custom_call" | custom-call | tf_op jit(solution)/shard_map/item/pallas_call | solution.py:303
  135.8 4.4 %all-gather.3.state_ref = bf16[2,4,1024]{2,1,0:T(4,128)(2,1)S(1)} all-gather(bf16[1,4,1024]{2,1,0:T(4,128)(2,1)S(1)} %bitcast.22), channel_id=2, replica_groups={{0,128},{256,384},{1,129},{257,385},{2,130},{258,386},{3,131},{259,387}..., dimensions={0}, use_global_device_ids=true | all-gather | bytes 24576 | tf_op jit(solution)/shard_map/all_gather | solution.py:321
  140.2 1.5 section.3
  141.7 5.6 %all-gather.4.state_ref = bf16[2,4,1024]{2,1,0:T(4,128)(2,1)S(1)} all-gather(bf16[1,4,1024]{2,1,0:T(4,128)(2,1)S(1)} %bitcast.23), channel_id=3, replica_groups={{128,256},{0,384},{129,257},{1,385},{130,258},{2,386},{131,259},{3,387}..., dimensions={0}, use_global_device_ids=true | all-gather | bytes 24576 | tf_op jit(solution)/shard_map/all_gather | solution.py:321
  147.2 1.5 section.4
  148.7 4.4 %all-gather.5.state_ref = bf16[2,4,1024]{2,1,0:T(4,128)(2,1)S(1)} all-gather(bf16[1,4,1024]{2,1,0:T(4,128)(2,1)S(1)} %bitcast.24), channel_id=4, replica_groups={{0,128},{256,384},{1,129},{257,385},{2,130},{258,386},{3,131},{259,387}..., dimensions={0}, use_global_device_ids=true | all-gather | bytes 24576 | tf_op jit(solution)/shard_map/all_gather | solution.py:321
  153.1 2.1 %section.5 = (bf16[4,1024]{1,0:T(4,128)(2,1)}, f32[1,512]{1,0:T(1,128)}) custom-call(bf16[2,4,1024]{2,1,0:T(4,128)(2,1)S(1)} %all-gather.5.state_ref, bf16[512,1024]{1,0:T(8,128)(2,1)S(1)} %get-tuple-element.26.key_ref, bf16[512,1024]{1,0:T(8,128)(2,1)S(1)} %get-tuple-element.27.value_ref, bf16[1024,4352]{1,0:T(8,128)(2,1)S(1)} %bitcast.18, ...), custom_call_target="tpu_custom_call" | custom-call | tf_op jit(solution)/shard_map/section/pallas_call | solution.py:325
Async XLA Ops:
  7.2 121.3 %all-gather.8.cloned.1.call-start = ((), (), s32[]{:S(2)}) async-start(), calls=%async_computation.2 | async-start | bytes 9191424 | tf_op jit(solution)/shard_map/all_gather | solution.py:257
  20.7 0.7 copy-start.3
  56.5 1.2 copy-start
  103.2 0.7 copy-start.1
  103.9 0.7 copy-start.2
  104.6 0.7 copy-start.4
Sparse Core Ops, SparseCore 0:
  20.9 107.5 all-gather.7

commit v4 on v3

--- a/solution.py
+++ b/solution.py
@@ -14,6 +14,7 @@
 F32 = jnp.float32
 BF16 = jnp.bfloat16
 SHARD = ("z", "y", "core")
+FROM_Z = (4, 0, -4, 8, 3, -1, -5, 7, 5, 1, -3, 9, 6, 2, -2, -6)
 
 
 def vmem():
@@ -138,7 +139,14 @@
 
 
 def item_kernel(
-    gathered_ref,
+    *refs,
+):
+    pieces, refs = refs[:10], refs[10:]
+    place_and_project(pieces, *refs)
+
+
+def place_and_project(
+    pieces,
     listed_ref,
     state_ref,
     gain_ref,
@@ -150,30 +158,29 @@
     score_ref,
     sems,
 ):
-    _, cores, ys, _, columns = gathered_ref.shape
-    depth, width = key_ref.shape[1], key_ref.shape[1]
+    zs, ys, cores, _, _ = weight_ref.shape
+    depth = width = key_ref.shape[1]
     emb = listed_ref.shape[1]
-    copies = []
-    for part, (first, size) in enumerate(
-        ((4 * width, emb), (0, 2 * width), (2 * width, 2 * width))
-    ):
-        mine = []
-        for core in range(cores):
-            for y in range(ys):
-                copy = pltpu.make_async_copy(
-                    gathered_ref.at[:, core, y, :, pl.ds(first, size)],
-                    weight_ref.at[:, y, core, :, pl.ds(first, size)],
-                    sems.at[part, core * ys + y],
-                )
-                copy.start()
-                mine.append(copy)
-        copies.append(mine)
+    z, y, core = (lax.axis_index(name) for name in SHARD)
+    half = zs // 2
+    for number, piece in enumerate(pieces):
+        kind, swapped = number % 5, number // 5
+        first = half if kind == 4 else 0
+        to_y = lax.rem(y + (0, ys - 1, 1, ys - 2, 2)[kind], ys)
+        to_core = lax.rem(core + swapped, cores)
+        for index in range(piece.shape[0]):
+            to_z = lax.rem(z + FROM_Z[first + index] + zs, zs)
+            copy = pltpu.make_async_copy(
+                piece.at[index], weight_ref.at[to_z, to_y, to_core], sems.at[number]
+            )
+            copy.start()
 
     def weight(first, size):
         return weight_ref[:, :, :, :, first : first + size].reshape(depth, size)
 
-    for copy in copies[0]:
-        copy.wait()
+    for number, piece in enumerate(pieces):
+        whole = weight_ref.at[pl.ds(0, piece.shape[0]), 0, 0]
+        pltpu.make_async_copy(piece, whole, sems.at[number]).wait()
     listed = listed_ref[...]
     packed = weight(4 * width, emb)
     split = depth // emb
@@ -190,8 +197,6 @@
             jax.nn.silu(jnp.dot(listed, lift, preferred_element_type=F32)).astype(BF16)
         )
     lifted = jnp.concatenate(lifted, axis=1)
-    for copy in copies[1]:
-        copy.wait()
     block = 512
     for first in range(0, 2 * width, block):
         made = jnp.dot(lifted, weight(first, block), preferred_element_type=F32).astype(BF16)
@@ -199,8 +204,6 @@
             key_ref[:, first : first + block] = made
         else:
             value_ref[:, first - width : first - width + block] = made
-    for copy in copies[2]:
-        copy.wait()
     next_ref[...], score_ref[...] = section_step(
         state_ref[...],
         key_ref,
@@ -246,16 +249,14 @@
     items = item_ids.shape[2]
     shard_rows, emb = item_table.shape
     depth = w_ask.shape[1]
-    small, big = (pltpu.CompilerParams(vmem_limit_bytes=size << 20) for size in (12, 38))
+    small, big = (pltpu.CompilerParams(vmem_limit_bytes=size << 20) for size in (12, 24))
 
     own = jnp.concatenate(
         [w_pair[0], w_ask[0], w_back[0], w_lift[0].reshape(depth, emb)], axis=1
     )
-    even, odd = [[0, 1], [2, 3]], [[1, 2], [0, 3]]
-    near = lax.all_gather(own, "y", axis=0, tiled=True, axis_index_groups=even)
-    near = lax.all_gather(near, "y", axis=0, tiled=True, axis_index_groups=odd)
-    gathered = lax.all_gather(near, ("z", "core"), axis=0, tiled=True)
-    gathered = gathered.reshape(zs, cores, ys, depth, own.shape[1])
+    def moved(block, axis, distance):
+        size = lax.axis_size(axis)
+        return lax.ppermute(block, axis, [(i, (i + distance) % size) for i in range(size)])
 
     request, slots = pl.pallas_call(
         lambda *refs: request_kernel(shard_rows, *refs),
@@ -271,6 +272,25 @@
     arrived = lax.all_to_all(
         request.reshape(shards, 1, CAP), SHARD, split_axis=0, concat_axis=0, tiled=True
     )
+    own = own[None]
+    far = (moved(own, "z", -4), moved(own, "z", 4), moved(own, "z", 8))
+    far, arrived = lax.optimization_barrier((far, arrived))
+    far = jnp.concatenate([far[0], own, *far[1:]])
+    column = jnp.concatenate(
+        [
+            far,
+            moved(far, "z", 1),
+            moved(far, "z", -1),
+            moved(far[:2], "z", -2),
+            moved(far[1:3], "z", 2),
+        ]
+    )
+    half = zs // 2
+    below, above = moved(column, "y", 1), moved(column, "y", -1)
+    across = [moved(below[:half], "y", 1), moved(above[half:], "y", -1)]
+    pieces = [column, below, above, *across]
+    pieces = pieces + [moved(piece, "core", 1) for piece in pieces]
+
     found = pl.pallas_call(
         table_kernel,
         out_shape=jax.ShapeDtypeStruct((shards, CAP, emb), BF16),
@@ -305,21 +325,22 @@
         out_shape=(
             jax.ShapeDtypeStruct((users * items, width), BF16),
             jax.ShapeDtypeStruct((users * items, width), BF16),
-            jax.ShapeDtypeStruct((zs, ys, cores, depth, own.shape[1]), BF16),
+            jax.ShapeDtypeStruct((zs, ys, cores, depth, own.shape[2]), BF16),
         )
         + section_shape,
-        in_specs=[pl.BlockSpec(memory_space=pltpu.HBM)] + [vmem()] * 4,
+        in_specs=[pl.BlockSpec(memory_space=pl.ANY)] * len(pieces) + [vmem()] * 4,
         out_specs=(vmem(),) * 5,
-        scratch_shapes=[pltpu.SemaphoreType.DMA((3, cores * ys))],
+        scratch_shapes=[pltpu.SemaphoreType.DMA((len(pieces),))],
         compiler_params=big,
         name="item",
-    )(gathered, listed, entering, gains, length_row)
-    weights = weights.reshape(shards * depth, own.shape[1])
-
+    )(*pieces, listed, entering, gains, length_row)
+    weights = weights.reshape(shards * depth, own.shape[2])
+
+    even, odd = [[0, 1], [2, 3]], [[1, 2], [0, 3]]
     states, scores = [leaving], [score]
     for step in range(1, segment_count):
         entering = lax.all_gather(
-            leaving, "segment", axis=0, axis_index_groups=even if step % 2 else odd
+            leaving, "segment", axis=0, axis_index_groups=(even, odd)[step % 2 == 0]
         )
         earlier = (*states, *scores) if step + 1 == segment_count else ()
         leaving, score = pl.pallas_call(

time: 162 us -> 168 us (1.037)
  starting transfers between devices: 0.04 us -> 73.1 us
  blocking collectives: 105 us -> 38.5 us
  between operations: 14.1 us -> 0.99 us
  Pallas kernels: 15.4 us -> 21.4 us
  waiting for transfers between devices: 22.2 us -> 25.7 us
    ppermute x0 -> x16, starting transfers between devices: none -> 63 us  [moved(): lax.ppermute(block, axis, [(i, (i + distance) % size) for i in range(size)])]
    all_to_all x1 -> x0, blocking collectives: 44.1 us -> none  [per_device(): lax.all_to_all(found, SHARD, split_axis=0, concat_axis=0, tiled=True)]
    ppermute x0 -> x16, waiting for transfers between devices: none -> 25.7 us  [moved(): lax.ppermute(block, axis, [(i, (i + distance) % size) for i in range(size)])]
    all_gather x1 -> x0, waiting for transfers between devices: 22.2 us -> none  [per_device(): gathered = lax.all_gather(near, ('z', 'core'), axis=0, tiled=True)]
    all_gather x5 -> x3, blocking collectives: 26.3 us -> 14.3 us  [per_device(): lax.all_gather(leaving, 'segment', axis=0, axis_index_groups=(even, odd)[...]
    all_to_all x1, blocking collectives: 34.4 us -> 24.2 us  [per_device(): lax.all_to_all(request.reshape(shards, 1, CAP), SHARD, split_axis=0, conc...]
    all_to_all x0 -> x1, starting transfers between devices: none -> 10.2 us  [per_device(): lax.all_to_all(found, SHARD, split_axis=0, concat_axis=0, tiled=True)]
    pallas_call x1, Pallas kernels: 7.36 us -> 12.5 us  [per_device(): pl.pallas_call(item_kernel, out_shape=(jax.ShapeDtypeStruct((users * item...]
  transfers between devices with their start and end apart: 1 -> 17, of which waited for: 1 -> 5; matrix products, arithmetic and copies ran while one was open for 0% -> 3% of each run, Pallas kernels for 2% -> 2%
where the time goes in v4:
time: 168 us; the launch traced here: 167 us
  starting transfers between devices  73.1 us (44%)
  blocking collectives  38.5 us (23%)
  waiting for transfers between devices  25.7 us (15%)
  Pallas kernels  21.4 us (13%)
  local copies, waits for them, and re-layouts  6.19 us (4%)
    ppermute x16, starting transfers between devices, moved(): lax.ppermute(block, axis, [(i, (i + distance) % size) for i in range(size)])  63 us
    ppermute x16, waiting for transfers between devices, moved(): lax.ppermute(block, axis, [(i, (i + distance) % size) for i in range(size)])  25.7 us
    all_to_all x1, blocking collectives, per_device(): lax.all_to_all(request.reshape(shards, 1, CAP), SHARD, split_axis=0, conc...  24.2 us
    all_gather x3, blocking collectives, per_device(): lax.all_gather(leaving, 'segment', axis=0, axis_index_groups=(even, odd)[...  14.3 us
    pallas_call x1, Pallas kernels, per_device(): pl.pallas_call(item_kernel, out_shape=(jax.ShapeDtypeStruct((users * item...  12.5 us
    all_to_all x1, starting transfers between devices, per_device(): lax.all_to_all(found, SHARD, split_axis=0, concat_axis=0, tiled=True)  10.2 us
    pallas_call x3, Pallas kernels, per_device(): pl.pallas_call(section_kernel, out_shape=section_shape, in_specs=[vmem()]...  5.02 us
    unnamed x22, local copies, waits for them, and re-layouts  4.74 us
  transfers between devices with their start and end apart: 17, of which 5 were waited for; matrix products, arithmetic and copies ran while one was open for 3% of the time, Pallas kernels for 2%

profile of v4, /device:TPU:6, one launch (start us, length us, event | category | flops | bytes accessed | tf_op | source)
XLA Modules:
  0.0 167.4 jit_solution(1608635329338177048)
XLA Ops:
  0.6 0.0 copy-start.6
  0.6 0.0 copy-start.7
  0.7 0.0 copy-start.5
  0.7 0.7 reshape_squeeze.3
  1.4 0.8 maximum_bitcast_fusion
  2.2 15.7 %collective-permute-start.2 = (bf16[1,8,4352]{2,1,0:T(8,128)(2,1)S(1)}, bf16[1,8,4352]{2,1,0:T(8,128)(2,1)S(1)}, u32[]{:S(2)}, u32[]{:S(2)}) collective-permute-start(bf16[1,8,4352]{2,1,0:T(8,128)(2,1)S(1)} %maximum_bitcast_fusion), channel_id=1, source_target_pairs={{0,64},{8,72},{16,80},{24,88},{32,96},{40,104},{48,112},{56,120},{... | collective-permute-start | bytes 208904 | tf_op jit(solution)/shard_map/ppermute | solution.py:259
  17.9 4.3 %collective-permute-start.1 = (bf16[1,8,4352]{2,1,0:T(8,128)(2,1)S(1)}, bf16[1,8,4352]{2,1,0:T(8,128)(2,1)S(1)}, u32[]{:S(2)}, u32[]{:S(2)}) collective-permute-start(bf16[1,8,4352]{2,1,0:T(8,128)(2,1)S(1)} %maximum_bitcast_fusion), channel_id=1, source_target_pairs={{0,32},{8,40},{16,48},{24,56},{32,64},{40,72},{48,80},{56,88},{64,... | collective-permute-start | bytes 208904 | tf_op jit(solution)/shard_map/ppermute | solution.py:259
  22.2 5.5 %collective-permute-start = (bf16[1,8,4352]{2,1,0:T(8,128)(2,1)S(1)}, bf16[1,8,4352]{2,1,0:T(8,128)(2,1)S(1)}, u32[]{:S(2)}, u32[]{:S(2)}) collective-permute-start(bf16[1,8,4352]{2,1,0:T(8,128)(2,1)S(1)} %maximum_bitcast_fusion), channel_id=1, source_target_pairs={{0,96},{8,104},{16,112},{24,120},{32,0},{40,8},{48,16},{56,24},{64... | collective-permute-start | bytes 208904 | tf_op jit(solution)/shard_map/ppermute | solution.py:259
  27.7 0.0 copy-start.3
  27.7 0.7 copy-done.3
  28.3 0.7 request.1
  29.0 24.2 %all_to_all.10 = s32[128,1,8]{2,1,0:T(1,128)S(1)} all-to-all(s32[128,1,8]{2,1,0:T(1,128)S(1)} %bitcast.24), channel_id=1, replica_groups=mesh['segment'=4,'z'=16,'y'=4,'core'=2] {'z','y','core'}, dimensions={0} | all-to-all | bytes 8192 | tf_op jit(solution)/shard_map/all_to_all | solution.py:272
  53.2 0.0 collective-permute-done.2
  53.2 0.0 collective-permute-done.1
  53.2 0.0 collective-permute-done
  53.3 0.0 copy-start
  53.3 3.5 %collective-permute-start.4 = (bf16[4,8,4352]{2,1,0:T(8,128)(2,1)S(1)}, bf16[4,8,4352]{2,1,0:T(8,128)(2,1)S(1)}, u32[]{:S(2)}, u32[]{:S(2)}) collective-permute-start(bf16[4,8,4352]{2,1,0:T(8,128)(2,1)S(1)} %pad_maximum_fusion), channel_id=1, source_target_pairs={{0,120},{8,0},{16,8},{24,16},{32,24},{40,32},{48,40},{56,48},{64,5... | collective-permute-start | bytes 835592 | tf_op jit(solution)/shard_map/ppermute | solution.py:259
  56.8 2.5 %collective-permute-start.3 = (bf16[4,8,4352]{2,1,0:T(8,128)(2,1)S(1)}, bf16[4,8,4352]{2,1,0:T(8,128)(2,1)S(1)}, u32[]{:S(2)}, u32[]{:S(2)}) collective-permute-start(bf16[4,8,4352]{2,1,0:T(8,128)(2,1)S(1)} %pad_maximum_fusion), channel_id=1, source_target_pairs={{0,8},{8,16},{16,24},{24,32},{32,40},{40,48},{48,56},{56,64},{64,7... | collective-permute-start | bytes 835592 | tf_op jit(solution)/shard_map/ppermute | solution.py:259
  59.3 0.6 constant_dynamic-update-slice_fusion.7
  59.9 3.1 %collective-permute-start.6 = (bf16[2,8,4352]{2,1,0:T(8,128)(2,1)S(1)}, bf16[2,8,4352]{2,1,0:T(8,128)(2,1)S(1)}, u32[]{:S(2)}, u32[]{:S(2)}) collective-permute-start(bf16[2,8,4352]{2,1,0:T(8,128)(2,1)S(1)} %get-tuple-element.44), channel_id=1, source_target_pairs={{0,16},{8,24},{16,32},{24,40},{32,48},{40,56},{48,64},{56,72},{64,... | collective-permute-start | bytes 417800 | tf_op jit(solution)/shard_map/ppermute | solution.py:259
  63.0 4.9 %collective-permute-start.5 = (bf16[2,8,4352]{2,1,0:T(8,128)(2,1)S(1)}, bf16[2,8,4352]{2,1,0:T(8,128)(2,1)S(1)}, u32[]{:S(2)}, u32[]{:S(2)}) collective-permute-start(bf16[2,8,4352]{2,1,0:T(8,128)(2,1)S(1)} %get-tuple-element.45), channel_id=1, source_target_pairs={{0,112},{8,120},{16,0},{24,8},{32,16},{40,24},{48,32},{56,40},{64,... | collective-permute-start | bytes 417800 | tf_op jit(solution)/shard_map/ppermute | solution.py:259
  67.9 0.6 constant_dynamic-update-slice_fusion.6
  68.6 0.6 constant_dynamic-update-slice_fusion.5
  69.2 0.6 constant_dynamic-update-slice_fusion.4
  69.8 2.6 %collective-permute-done.3 = bf16[4,8,4352]{2,1,0:T(8,128)(2,1)S(1)} collective-permute-done((bf16[4,8,4352]{2,1,0:T(8,128)(2,1)S(1)}, bf16[4,8,4352]{2,1,0:T(8,128)(2,1)S(1)}, u32[]{:S(2)}, u32[]{:S(2)}) %collective-permute-start.3) | collective-permute-done | bytes 278560 | tf_op jit(solution)/shard_map/ppermute | solution.py:259
  72.4 0.7 constant_dynamic-update-slice_fusion.3
  73.1 0.0 collective-permute-done.4
  73.1 0.7 constant_dynamic-update-slice_fusion.2
  73.8 0.0 collective-permute-done.5
  73.8 0.7 constant_dynamic-update-slice_fusion.1
  74.5 0.0 collective-permute-done.6
  74.5 0.7 constant_dynamic-update-slice_fusion.refs_0_
  75.2 2.7 %collective-permute-start.8 = (bf16[16,8,4352]{2,1,0:T(8,128)(2,1)}, bf16[16,8,4352]{2,1,0:T(8,128)(2,1)S(1)}, u32[]{:S(2)}, u32[]{:S(2)}) collective-permute-start(bf16[16,8,4352]{2,1,0:T(8,128)(2,1)} %constant_dynamic-update-slice_fusion.refs_0_), channel_id=1, source_target_pairs={{0,6},{2,0},{4,2},{6,4},{1,7},{3,1},{5,3},{7,5},{8,14},{10,8},{12,... | collective-permute-start | bytes 3342344 | tf_op jit(solution)/shard_map/ppermute | solution.py:259
  77.8 3.2 %collective-permute-start.7 = (bf16[16,8,4352]{2,1,0:T(8,128)(2,1)}, bf16[16,8,4352]{2,1,0:T(8,128)(2,1)S(1)}, u32[]{:S(2)}, u32[]{:S(2)}) collective-permute-start(bf16[16,8,4352]{2,1,0:T(8,128)(2,1)} %constant_dynamic-update-slice_fusion.refs_0_), channel_id=1, source_target_pairs={{0,2},{2,4},{4,6},{6,0},{1,3},{3,5},{5,7},{7,1},{8,10},{10,12},{12... | collective-permute-start | bytes 3342344 | tf_op jit(solution)/shard_map/ppermute | solution.py:259
  81.0 2.1 %table.1 = bf16[128,8,256]{2,1,0:T(8,128)(2,1)} custom-call(s32[128,8]{1,0:T(8,128)S(1)} %bitcast.23, bf16[2048,256]{1,0:T(8,128)(2,1)S(1)} %copy-done), custom_call_target="tpu_custom_call" | custom-call | tf_op jit(solution)/shard_map/table/pallas_call | solution.py:294
  83.2 10.2 %all-to-all-start.1 = ((bf16[128,8,256]{2,1,0:T(8,128)(2,1)}), bf16[128,8,256]{2,1,0:T(8,128)(2,1)S(1)}, u32[]{:S(2)}, u32[]{:S(2)}) async-start(bf16[128,8,256]{2,1,0:T(8,128)(2,1)} %table.1), calls=%async_computation.1 | async-start | bytes 1048576 | tf_op jit(solution)/shard_map/all_to_all | solution.py:302
  93.3 0.0 copy-start.1
  93.3 0.0 copy-start.2
  93.4 0.0 copy-start.4
  93.4 2.1 %collective-permute-start.11 = (bf16[16,8,4352]{2,1,0:T(8,128)(2,1)}, bf16[16,8,4352]{2,1,0:T(8,128)(2,1)}, u32[]{:S(2)}, u32[]{:S(2)}) collective-permute-start(bf16[16,8,4352]{2,1,0:T(8,128)(2,1)} %constant_dynamic-update-slice_fusion.refs_0_), channel_id=1, source_target_pairs={{0,1},{1,0},{2,3},{3,2},{4,5},{5,4},{6,7},{7,6},{8,9},{9,8},{10,11... | collective-permute-start | bytes 3342344 | tf_op jit(solution)/shard_map/ppermute | solution.py:259
  95.4 7.7 %collective-permute-done.8.refs_2_ = bf16[16,8,4352]{2,1,0:T(8,128)(2,1)S(1)} collective-permute-done((bf16[16,8,4352]{2,1,0:T(8,128)(2,1)}, bf16[16,8,4352]{2,1,0:T(8,128)(2,1)S(1)}, u32[]{:S(2)}, u32[]{:S(2)}) %collective-permute-start.8) | collective-permute-done | bytes 1114144 | tf_op jit(solution)/shard_map/ppermute | solution.py:259
  103.2 5.5 %collective-permute-start.10 = (bf16[8,8,4352]{2,1,0:T(8,128)(2,1)S(1)}, bf16[8,8,4352]{2,1,0:T(8,128)(2,1)S(1)}, u32[]{:S(2)}, u32[]{:S(2)}) collective-permute-start(bf16[8,8,4352]{2,1,0:T(8,128)(2,1)S(1)} %slice.13), channel_id=1, source_target_pairs={{0,6},{2,0},{4,2},{6,4},{1,7},{3,1},{5,3},{7,5},{8,14},{10,8},{12,... | collective-permute-start | bytes 1671176 | tf_op jit(solution)/shard_map/ppermute | solution.py:259
  108.7 1.9 %collective-permute-start.13 = (bf16[16,8,4352]{2,1,0:T(8,128)(2,1)S(1)}, bf16[16,8,4352]{2,1,0:T(8,128)(2,1)}, u32[]{:S(2)}, u32[]{:S(2)}) collective-permute-start(bf16[16,8,4352]{2,1,0:T(8,128)(2,1)S(1)} %collective-permute-done.8.refs_2_), channel_id=1, source_target_pairs={{0,1},{1,0},{2,3},{3,2},{4,5},{5,4},{6,7},{7,6},{8,9},{9,8},{10,11... | collective-permute-start | bytes 3342344 | tf_op jit(solution)/shard_map/ppermute | solution.py:259
  110.6 0.0 collective-permute-done.7.refs_1_
  110.6 2.4 %collective-permute-start.12 = (bf16[16,8,4352]{2,1,0:T(8,128)(2,1)S(1)}, bf16[16,8,4352]{2,1,0:T(8,128)(2,1)}, u32[]{:S(2)}, u32[]{:S(2)}) collective-permute-start(bf16[16,8,4352]{2,1,0:T(8,128)(2,1)S(1)} %collective-permute-done.7.refs_1_), channel_id=1, source_target_pairs={{0,1},{1,0},{2,3},{3,2},{4,5},{5,4},{6,7},{7,6},{8,9},{9,8},{10,11... | collective-permute-start | bytes 3342344 | tf_op jit(solution)/shard_map/ppermute | solution.py:259
  113.1 1.9 %collective-permute-start.9 = (bf16[8,8,4352]{2,1,0:T(8,128)(2,1)S(1)}, bf16[8,8,4352]{2,1,0:T(8,128)(2,1)}, u32[]{:S(2)}, u32[]{:S(2)}) collective-permute-start(bf16[8,8,4352]{2,1,0:T(8,128)(2,1)S(1)} %slice.12), channel_id=1, source_target_pairs={{0,2},{2,4},{4,6},{6,0},{1,3},{3,5},{5,7},{7,1},{8,10},{10,12},{12... | collective-permute-start | bytes 1671176 | tf_op jit(solution)/shard_map/ppermute | solution.py:259
  115.0 6.6 %collective-permute-done.10.refs_4_ = bf16[8,8,4352]{2,1,0:T(8,128)(2,1)S(1)} collective-permute-done((bf16[8,8,4352]{2,1,0:T(8,128)(2,1)S(1)}, bf16[8,8,4352]{2,1,0:T(8,128)(2,1)S(1)}, u32[]{:S(2)}, u32[]{:S(2)}) %collective-permute-start.10) | collective-permute-done | bytes 557088 | tf_op jit(solution)/shard_map/ppermute | solution.py:259
  121.5 1.9 %collective-permute-start.15 = (bf16[8,8,4352]{2,1,0:T(8,128)(2,1)S(1)}, bf16[8,8,4352]{2,1,0:T(8,128)(2,1)}, u32[]{:S(2)}, u32[]{:S(2)}) collective-permute-start(bf16[8,8,4352]{2,1,0:T(8,128)(2,1)S(1)} %collective-permute-done.10.refs_4_), channel_id=1, source_target_pairs={{0,1},{1,0},{2,3},{3,2},{4,5},{5,4},{6,7},{7,6},{8,9},{9,8},{10,11... | collective-permute-start | bytes 1671176 | tf_op jit(solution)/shard_map/ppermute | solution.py:259
  123.5 7.9 %collective-permute-done.9.refs_3_ = bf16[8,8,4352]{2,1,0:T(8,128)(2,1)} collective-permute-done((bf16[8,8,4352]{2,1,0:T(8,128)(2,1)S(1)}, bf16[8,8,4352]{2,1,0:T(8,128)(2,1)}, u32[]{:S(2)}, u32[]{:S(2)}) %collective-permute-start.9) | collective-permute-done | bytes 557088 | tf_op jit(solution)/shard_map/ppermute | solution.py:259
  131.4 2.1 %collective-permute-start.14 = (bf16[8,8,4352]{2,1,0:T(8,128)(2,1)}, bf16[8,8,4352]{2,1,0:T(8,128)(2,1)}, u32[]{:S(2)}, u32[]{:S(2)}) collective-permute-start(bf16[8,8,4352]{2,1,0:T(8,128)(2,1)} %collective-permute-done.9.refs_3_), channel_id=1, source_target_pairs={{0,1},{1,0},{2,3},{3,2},{4,5},{5,4},{6,7},{7,6},{8,9},{9,8},{10,11... | collective-permute-start | bytes 1671176 | tf_op jit(solution)/shard_map/ppermute | solution.py:259
  133.5 0.0 all-to-all-done.1
  133.5 1.0 list.1
  134.6 0.0 collective-permute-done.11.refs_5_
  134.6 0.0 collective-permute-done.13.refs_7_
  134.6 0.0 collective-permute-done.12.refs_6_
  134.6 0.0 collective-permute-done.15.refs_9_
  134.6 1.0 collective-permute-done.14.refs_8_
  135.6 12.5 %item.1 = (bf16[512,1024]{1,0:T(8,128)(2,1)S(1)}, bf16[512,1024]{1,0:T(8,128)(2,1)S(1)}, bf16[16,4,2,8,4352]{4,3,2,1,0:T(8,128)(2,1)S(1)}, bf16[4,1024]{1,0:T(4,128)(2,1)S(1)}, f32[1,512]{1,0:T(1,128)S(1)}) custom-call(bf16[16,8,4352]{2,1,0:T(8,128)(2,1)} %constant_dynamic-update-slice_fusion.refs_0_, ...), custom_call_target="tpu_custom_call" | custom-call | tf_op jit(solution)/shard_map/item/pallas_call | solution.py:323
  148.1 4.4 %all-gather.3.state_ref = bf16[2,4,1024]{2,1,0:T(4,128)(2,1)S(1)} all-gather(bf16[1,4,1024]{2,1,0:T(4,128)(2,1)S(1)} %bitcast.25), channel_id=2, replica_groups={{0,128},{256,384},{1,129},{257,385},{2,130},{258,386},{3,131},{259,387}..., dimensions={0}, use_global_device_ids=true | all-gather | bytes 24576 | tf_op jit(solution)/shard_map/all_gather | solution.py:342
  152.5 1.5 section.3
  153.9 5.6 %all-gather.4.state_ref = bf16[2,4,1024]{2,1,0:T(4,128)(2,1)S(1)} all-gather(bf16[1,4,1024]{2,1,0:T(4,128)(2,1)S(1)} %bitcast.26), channel_id=3, replica_groups={{128,256},{0,384},{129,257},{1,385},{130,258},{2,386},{131,259},{3,387}..., dimensions={0}, use_global_device_ids=true | all-gather | bytes 24576 | tf_op jit(solution)/shard_map/all_gather | solution.py:342
  159.5 1.5 section.4
  161.0 4.4 %all-gather.5.state_ref = bf16[2,4,1024]{2,1,0:T(4,128)(2,1)S(1)} all-gather(bf16[1,4,1024]{2,1,0:T(4,128)(2,1)S(1)} %bitcast.27), channel_id=4, replica_groups={{0,128},{256,384},{1,129},{257,385},{2,130},{258,386},{3,131},{259,387}..., dimensions={0}, use_global_device_ids=true | all-gather | bytes 24576 | tf_op jit(solution)/shard_map/all_gather | solution.py:342
  165.3 2.1 %section.5 = (bf16[4,1024]{1,0:T(4,128)(2,1)}, f32[1,512]{1,0:T(1,128)}) custom-call(bf16[2,4,1024]{2,1,0:T(4,128)(2,1)S(1)} %all-gather.5.state_ref, bf16[512,1024]{1,0:T(8,128)(2,1)S(1)} %get-tuple-element.34.key_ref, bf16[512,1024]{1,0:T(8,128)(2,1)S(1)} %get-tuple-element.35.value_ref, bf16[1024,4352]{1,0:T(8,128)(2,1)S(1)} %bitcast.21, ...), custom_call_target="tpu_custom_call" | custom-call | tf_op jit(solution)/shard_map/section/pallas_call | solution.py:346
  (11 shorter events, 0.2 us)
Async XLA Ops:
  0.6 67.3 %copy-start.6 = (bf16[1,8,1024]{2,1,0:T(8,128)(2,1)S(1)}, bf16[1,8,1024]{2,1,0:T(8,128)(2,1)}, u32[]{:S(2)}) copy-start(bf16[1,8,1024]{2,1,0:T(8,128)(2,1)} %param.14) | copy-start | bytes 49156
  0.6 67.3 %copy-start.7 = (bf16[1,8,1024]{2,1,0:T(8,128)(2,1)S(1)}, bf16[1,8,1024]{2,1,0:T(8,128)(2,1)}, u32[]{:S(2)}) copy-start(bf16[1,8,1024]{2,1,0:T(8,128)(2,1)} %param.13) | copy-start | bytes 49156
  0.7 67.3 %copy-start.5 = (bf16[1,8,2048]{2,1,0:T(8,128)(2,1)S(1)}, bf16[1,8,2048]{2,1,0:T(8,128)(2,1)}, u32[]{:S(2)}) copy-start(bf16[1,8,2048]{2,1,0:T(8,128)(2,1)} %param.12) | copy-start | bytes 98308
  2.2 51.1 %collective-permute-start.2 = (bf16[1,8,4352]{2,1,0:T(8,128)(2,1)S(1)}, bf16[1,8,4352]{2,1,0:T(8,128)(2,1)S(1)}, u32[]{:S(2)}, u32[]{:S(2)}) collective-permute-start(bf16[1,8,4352]{2,1,0:T(8,128)(2,1)S(1)} %maximum_bitcast_fusion), channel_id=1, source_target_pairs={{0,64},{8,72},{16,80},{24,88},{32,96},{40,104},{48,112},{56,120},{... | collective-permute-start | bytes 208904 | tf_op jit(solution)/shard_map/ppermute | solution.py:259
  17.9 35.3 %collective-permute-start.1 = (bf16[1,8,4352]{2,1,0:T(8,128)(2,1)S(1)}, bf16[1,8,4352]{2,1,0:T(8,128)(2,1)S(1)}, u32[]{:S(2)}, u32[]{:S(2)}) collective-permute-start(bf16[1,8,4352]{2,1,0:T(8,128)(2,1)S(1)} %maximum_bitcast_fusion), channel_id=1, source_target_pairs={{0,32},{8,40},{16,48},{24,56},{32,64},{40,72},{48,80},{56,88},{64,... | collective-permute-start | bytes 208904 | tf_op jit(solution)/shard_map/ppermute | solution.py:259
  22.2 31.0 %collective-permute-start = (bf16[1,8,4352]{2,1,0:T(8,128)(2,1)S(1)}, bf16[1,8,4352]{2,1,0:T(8,128)(2,1)S(1)}, u32[]{:S(2)}, u32[]{:S(2)}) collective-permute-start(bf16[1,8,4352]{2,1,0:T(8,128)(2,1)S(1)} %maximum_bitcast_fusion), channel_id=1, source_target_pairs={{0,96},{8,104},{16,112},{24,120},{32,0},{40,8},{48,16},{56,24},{64... | collective-permute-start | bytes 208904 | tf_op jit(solution)/shard_map/ppermute | solution.py:259
  27.7 0.7 copy-start.3
  53.3 27.7 %copy-start = (bf16[2048,256]{1,0:T(8,128)(2,1)S(1)}, bf16[2048,256]{1,0:T(8,128)(2,1)}, u32[]{:S(2)}) copy-start(bf16[2048,256]{1,0:T(8,128)(2,1)} %table_ref.1) | copy-start | bytes 3145732
  53.3 19.8 %collective-permute-start.4 = (bf16[4,8,4352]{2,1,0:T(8,128)(2,1)S(1)}, bf16[4,8,4352]{2,1,0:T(8,128)(2,1)S(1)}, u32[]{:S(2)}, u32[]{:S(2)}) collective-permute-start(bf16[4,8,4352]{2,1,0:T(8,128)(2,1)S(1)} %pad_maximum_fusion), channel_id=1, source_target_pairs={{0,120},{8,0},{16,8},{24,16},{32,24},{40,32},{48,40},{56,48},{64,5... | collective-permute-start | bytes 835592 | tf_op jit(solution)/shard_map/ppermute | solution.py:259
  56.8 15.6 %collective-permute-start.3 = (bf16[4,8,4352]{2,1,0:T(8,128)(2,1)S(1)}, bf16[4,8,4352]{2,1,0:T(8,128)(2,1)S(1)}, u32[]{:S(2)}, u32[]{:S(2)}) collective-permute-start(bf16[4,8,4352]{2,1,0:T(8,128)(2,1)S(1)} %pad_maximum_fusion), channel_id=1, source_target_pairs={{0,8},{8,16},{16,24},{24,32},{32,40},{40,48},{48,56},{56,64},{64,7... | collective-permute-start | bytes 835592 | tf_op jit(solution)/shard_map/ppermute | solution.py:259
  59.9 14.6 %collective-permute-start.6 = (bf16[2,8,4352]{2,1,0:T(8,128)(2,1)S(1)}, bf16[2,8,4352]{2,1,0:T(8,128)(2,1)S(1)}, u32[]{:S(2)}, u32[]{:S(2)}) collective-permute-start(bf16[2,8,4352]{2,1,0:T(8,128)(2,1)S(1)} %get-tuple-element.44), channel_id=1, source_target_pairs={{0,16},{8,24},{16,32},{24,40},{32,48},{40,56},{48,64},{56,72},{64,... | collective-permute-start | bytes 417800 | tf_op jit(solution)/shard_map/ppermute | solution.py:259
  63.0 10.8 %collective-permute-start.5 = (bf16[2,8,4352]{2,1,0:T(8,128)(2,1)S(1)}, bf16[2,8,4352]{2,1,0:T(8,128)(2,1)S(1)}, u32[]{:S(2)}, u32[]{:S(2)}) collective-permute-start(bf16[2,8,4352]{2,1,0:T(8,128)(2,1)S(1)} %get-tuple-element.45), channel_id=1, source_target_pairs={{0,112},{8,120},{16,0},{24,8},{32,16},{40,24},{48,32},{56,40},{64,... | collective-permute-start | bytes 417800 | tf_op jit(solution)/shard_map/ppermute | solution.py:259
  75.2 28.0 %collective-permute-start.8 = (bf16[16,8,4352]{2,1,0:T(8,128)(2,1)}, bf16[16,8,4352]{2,1,0:T(8,128)(2,1)S(1)}, u32[]{:S(2)}, u32[]{:S(2)}) collective-permute-start(bf16[16,8,4352]{2,1,0:T(8,128)(2,1)} %constant_dynamic-update-slice_fusion.refs_0_), channel_id=1, source_target_pairs={{0,6},{2,0},{4,2},{6,4},{1,7},{3,1},{5,3},{7,5},{8,14},{10,8},{12,... | collective-permute-start | bytes 3342344 | tf_op jit(solution)/shard_map/ppermute | solution.py:259
  77.8 32.7 %collective-permute-start.7 = (bf16[16,8,4352]{2,1,0:T(8,128)(2,1)}, bf16[16,8,4352]{2,1,0:T(8,128)(2,1)S(1)}, u32[]{:S(2)}, u32[]{:S(2)}) collective-permute-start(bf16[16,8,4352]{2,1,0:T(8,128)(2,1)} %constant_dynamic-update-slice_fusion.refs_0_), channel_id=1, source_target_pairs={{0,2},{2,4},{4,6},{6,0},{1,3},{3,5},{5,7},{7,1},{8,10},{10,12},{12... | collective-permute-start | bytes 3342344 | tf_op jit(solution)/shard_map/ppermute | solution.py:259
  83.2 50.3 %all-to-all-start.1 = ((bf16[128,8,256]{2,1,0:T(8,128)(2,1)}), bf16[128,8,256]{2,1,0:T(8,128)(2,1)S(1)}, u32[]{:S(2)}, u32[]{:S(2)}) async-start(bf16[128,8,256]{2,1,0:T(8,128)(2,1)} %table.1), calls=%async_computation.1 | async-start | bytes 1048576 | tf_op jit(solution)/shard_map/all_to_all | solution.py:302
  93.3 40.2 %copy-start.1 = (bf16[4,1024]{1,0:T(4,128)(2,1)S(1)}, bf16[4,1024]{1,0:T(4,128)(2,1)}, u32[]{:S(2)}) copy-start(bf16[4,1024]{1,0:T(4,128)(2,1)} %state_ref.1) | copy-start | bytes 24580
  93.3 40.2 %copy-start.2 = (f32[1,1024]{1,0:T(1,128)S(1)}, f32[1,1024]{1,0:T(1,128)}, u32[]{:S(2)}) copy-start(f32[1,1024]{1,0:T(1,128)} %gain_ref.1) | copy-start | bytes 12292
  93.4 40.2 %copy-start.4 = (s32[1,4]{1,0:T(1,128)S(1)}, s32[1,4]{1,0:T(1,128)}, u32[]{:S(2)}) copy-start(s32[1,4]{1,0:T(1,128)} %count_ref.1) | copy-start | bytes 52
  93.4 41.2 %collective-permute-start.11 = (bf16[16,8,4352]{2,1,0:T(8,128)(2,1)}, bf16[16,8,4352]{2,1,0:T(8,128)(2,1)}, u32[]{:S(2)}, u32[]{:S(2)}) collective-permute-start(bf16[16,8,4352]{2,1,0:T(8,128)(2,1)} %constant_dynamic-update-slice_fusion.refs_0_), channel_id=1, source_target_pairs={{0,1},{1,0},{2,3},{3,2},{4,5},{5,4},{6,7},{7,6},{8,9},{9,8},{10,11... | collective-permute-start | bytes 3342344 | tf_op jit(solution)/shard_map/ppermute | solution.py:259
  103.2 18.4 %collective-permute-start.10 = (bf16[8,8,4352]{2,1,0:T(8,128)(2,1)S(1)}, bf16[8,8,4352]{2,1,0:T(8,128)(2,1)S(1)}, u32[]{:S(2)}, u32[]{:S(2)}) collective-permute-start(bf16[8,8,4352]{2,1,0:T(8,128)(2,1)S(1)} %slice.13), channel_id=1, source_target_pairs={{0,6},{2,0},{4,2},{6,4},{1,7},{3,1},{5,3},{7,5},{8,14},{10,8},{12,... | collective-permute-start | bytes 1671176 | tf_op jit(solution)/shard_map/ppermute | solution.py:259
  108.7 25.9 %collective-permute-start.13 = (bf16[16,8,4352]{2,1,0:T(8,128)(2,1)S(1)}, bf16[16,8,4352]{2,1,0:T(8,128)(2,1)}, u32[]{:S(2)}, u32[]{:S(2)}) collective-permute-start(bf16[16,8,4352]{2,1,0:T(8,128)(2,1)S(1)} %collective-permute-done.8.refs_2_), channel_id=1, source_target_pairs={{0,1},{1,0},{2,3},{3,2},{4,5},{5,4},{6,7},{7,6},{8,9},{9,8},{10,11... | collective-permute-start | bytes 3342344 | tf_op jit(solution)/shard_map/ppermute | solution.py:259
  110.6 23.9 %collective-permute-start.12 = (bf16[16,8,4352]{2,1,0:T(8,128)(2,1)S(1)}, bf16[16,8,4352]{2,1,0:T(8,128)(2,1)}, u32[]{:S(2)}, u32[]{:S(2)}) collective-permute-start(bf16[16,8,4352]{2,1,0:T(8,128)(2,1)S(1)} %collective-permute-done.7.refs_1_), channel_id=1, source_target_pairs={{0,1},{1,0},{2,3},{3,2},{4,5},{5,4},{6,7},{7,6},{8,9},{9,8},{10,11... | collective-permute-start | bytes 3342344 | tf_op jit(solution)/shard_map/ppermute | solution.py:259
  113.1 18.3 %collective-permute-start.9 = (bf16[8,8,4352]{2,1,0:T(8,128)(2,1)S(1)}, bf16[8,8,4352]{2,1,0:T(8,128)(2,1)}, u32[]{:S(2)}, u32[]{:S(2)}) collective-permute-start(bf16[8,8,4352]{2,1,0:T(8,128)(2,1)S(1)} %slice.12), channel_id=1, source_target_pairs={{0,2},{2,4},{4,6},{6,0},{1,3},{3,5},{5,7},{7,1},{8,10},{10,12},{12... | collective-permute-start | bytes 1671176 | tf_op jit(solution)/shard_map/ppermute | solution.py:259
  121.5 13.0 %collective-permute-start.15 = (bf16[8,8,4352]{2,1,0:T(8,128)(2,1)S(1)}, bf16[8,8,4352]{2,1,0:T(8,128)(2,1)}, u32[]{:S(2)}, u32[]{:S(2)}) collective-permute-start(bf16[8,8,4352]{2,1,0:T(8,128)(2,1)S(1)} %collective-permute-done.10.refs_4_), channel_id=1, source_target_pairs={{0,1},{1,0},{2,3},{3,2},{4,5},{5,4},{6,7},{7,6},{8,9},{9,8},{10,11... | collective-permute-start | bytes 1671176 | tf_op jit(solution)/shard_map/ppermute | solution.py:259
  131.4 4.2 %collective-permute-start.14 = (bf16[8,8,4352]{2,1,0:T(8,128)(2,1)}, bf16[8,8,4352]{2,1,0:T(8,128)(2,1)}, u32[]{:S(2)}, u32[]{:S(2)}) collective-permute-start(bf16[8,8,4352]{2,1,0:T(8,128)(2,1)} %collective-permute-done.9.refs_3_), channel_id=1, source_target_pairs={{0,1},{1,0},{2,3},{3,2},{4,5},{5,4},{6,7},{7,6},{8,9},{9,8},{10,11... | collective-permute-start | bytes 1671176 | tf_op jit(solution)/shard_map/ppermute | solution.py:259

commit v5 on v4

--- a/solution.py
+++ b/solution.py
@@ -138,15 +138,39 @@
     return (state.astype(F32) + update).astype(BF16), score
 
 
+def place(pieces, weight_ref, sems):
+    zs, ys, cores, _, _ = weight_ref.shape
+    z, y, core = (lax.axis_index(name) for name in SHARD)
+    for number, (piece, first, from_y, swapped) in enumerate(pieces):
+        to_y = lax.rem(y + from_y, ys)
+        to_core = lax.rem(core + swapped, cores)
+        for index in range(piece.shape[0]):
+            to_z = lax.rem(z + FROM_Z[first + index] + zs, zs)
+            pltpu.make_async_copy(
+                piece.at[index], weight_ref.at[to_z, to_y, to_core], sems.at[number]
+            ).start()
+
+
+def wait_placed(pieces, weight_ref, sems):
+    for number, (piece, *_) in enumerate(pieces):
+        whole = weight_ref.at[pl.ds(0, piece.shape[0]), 0, 0]
+        pltpu.make_async_copy(piece, whole, sems.at[number]).wait()
+
+
+def place_kernel(*refs):
+    *pieces, weight_ref, sems = refs
+    ys = weight_ref.shape[1]
+    kinds = [(piece, 0, (0, ys - 1, 1)[i % 3], i // 3) for i, piece in enumerate(pieces)]
+    place(kinds, weight_ref, sems)
+    wait_placed(kinds, weight_ref, sems)
+
+
 def item_kernel(
-    *refs,
-):
-    pieces, refs = refs[:10], refs[10:]
-    place_and_project(pieces, *refs)
-
-
-def place_and_project(
-    pieces,
+    low_ref,
+    high_ref,
+    low_swapped_ref,
+    high_swapped_ref,
+    placed_ref,
     listed_ref,
     state_ref,
     gain_ref,
@@ -158,29 +182,18 @@
     score_ref,
     sems,
 ):
-    zs, ys, cores, _, _ = weight_ref.shape
+    del placed_ref
+    zs = weight_ref.shape[0]
     depth = width = key_ref.shape[1]
     emb = listed_ref.shape[1]
-    z, y, core = (lax.axis_index(name) for name in SHARD)
-    half = zs // 2
-    for number, piece in enumerate(pieces):
-        kind, swapped = number % 5, number // 5
-        first = half if kind == 4 else 0
-        to_y = lax.rem(y + (0, ys - 1, 1, ys - 2, 2)[kind], ys)
-        to_core = lax.rem(core + swapped, cores)
-        for index in range(piece.shape[0]):
-            to_z = lax.rem(z + FROM_Z[first + index] + zs, zs)
-            copy = pltpu.make_async_copy(
-                piece.at[index], weight_ref.at[to_z, to_y, to_core], sems.at[number]
-            )
-            copy.start()
+    pieces = (low_ref, high_ref, low_swapped_ref, high_swapped_ref)
+    kinds = [(piece, i % 2 * (zs // 2), 2, i // 2) for i, piece in enumerate(pieces)]
+    place(kinds, weight_ref, sems)
 
     def weight(first, size):
         return weight_ref[:, :, :, :, first : first + size].reshape(depth, size)
 
-    for number, piece in enumerate(pieces):
-        whole = weight_ref.at[pl.ds(0, piece.shape[0]), 0, 0]
-        pltpu.make_async_copy(piece, whole, sems.at[number]).wait()
+    wait_placed(kinds, weight_ref, sems)
     listed = listed_ref[...]
     packed = weight(4 * width, emb)
     split = depth // emb
@@ -273,24 +286,21 @@
         request.reshape(shards, 1, CAP), SHARD, split_axis=0, concat_axis=0, tiled=True
     )
     own = own[None]
-    far = (moved(own, "z", -4), moved(own, "z", 4), moved(own, "z", 8))
-    far, arrived = lax.optimization_barrier((far, arrived))
-    far = jnp.concatenate([far[0], own, *far[1:]])
-    column = jnp.concatenate(
-        [
-            far,
-            moved(far, "z", 1),
-            moved(far, "z", -1),
-            moved(far[:2], "z", -2),
-            moved(far[1:3], "z", 2),
-        ]
-    )
+    far = jnp.concatenate([moved(own, "z", -4), own, moved(own, "z", 4), moved(own, "z", 8)])
+    near = (
+        moved(far, "z", 1),
+        moved(far, "z", -1),
+        moved(far[:2], "z", -2),
+        moved(far[1:3], "z", 2),
+    )
+    near, arrived = lax.optimization_barrier((near, arrived))
+    column = jnp.concatenate([far, *near])
     half = zs // 2
     below, above = moved(column, "y", 1), moved(column, "y", -1)
-    across = [moved(below[:half], "y", 1), moved(above[half:], "y", -1)]
-    pieces = [column, below, above, *across]
-    pieces = pieces + [moved(piece, "core", 1) for piece in pieces]
-
+    across = (moved(below[:half], "y", 1), moved(above[half:], "y", -1))
+    both = lax.optimization_barrier((below, above))
+    early = [column, below, above]
+    early = early + [moved(piece, "core", 1) for piece in (column, *both)]
     found = pl.pallas_call(
         table_kernel,
         out_shape=jax.ShapeDtypeStruct((shards, CAP, emb), BF16),
@@ -300,6 +310,20 @@
         name="table",
     )(arrived.reshape(shards, CAP), item_table)
     returned = lax.all_to_all(found, SHARD, split_axis=0, concat_axis=0, tiled=True)
+
+    early, returned = lax.optimization_barrier((early, returned))
+    weights = pl.pallas_call(
+        place_kernel,
+        out_shape=jax.ShapeDtypeStruct((zs, ys, cores, depth, own.shape[2]), BF16),
+        in_specs=[pl.BlockSpec(memory_space=pl.ANY)] * len(early),
+        out_specs=vmem(),
+        scratch_shapes=[pltpu.SemaphoreType.DMA((len(early),))],
+        compiler_params=small,
+        cost_estimate=pl.CostEstimate(flops=0, bytes_accessed=14_000_000, transcendentals=0),
+        name="place",
+    )(*early)
+    across, weights = lax.optimization_barrier((across, weights))
+    late = [*across, *(moved(piece, "core", 1) for piece in across)]
 
     smem = pl.BlockSpec(memory_space=pltpu.SMEM)
     listed, entering, gains, length_row = pl.pallas_call(
@@ -328,12 +352,13 @@
             jax.ShapeDtypeStruct((zs, ys, cores, depth, own.shape[2]), BF16),
         )
         + section_shape,
-        in_specs=[pl.BlockSpec(memory_space=pl.ANY)] * len(pieces) + [vmem()] * 4,
+        in_specs=[pl.BlockSpec(memory_space=pl.ANY)] * 4 + [vmem()] * 5,
         out_specs=(vmem(),) * 5,
-        scratch_shapes=[pltpu.SemaphoreType.DMA((len(pieces),))],
+        scratch_shapes=[pltpu.SemaphoreType.DMA((len(late),))],
+        input_output_aliases={4: 2},
         compiler_params=big,
         name="item",
-    )(*pieces, listed, entering, gains, length_row)
+    )(*late, weights, listed, entering, gains, length_row)
     weights = weights.reshape(shards * depth, own.shape[2])
 
     even, odd = [[0, 1], [2, 3]], [[1, 2], [0, 3]]

time: 168 us -> 163 us (0.970); the launches traced: 167 us -> 160 us
  blocking collectives: 38.5 us -> 14.3 us
  starting transfers between devices: 73.1 us -> 88.4 us
  waiting for transfers between devices: 25.7 us -> 20.8 us
  local copies, waits for them, and re-layouts: 6.19 us -> 10 us
  Pallas kernels: 21.4 us -> 24.3 us
    all_to_all x1 -> x0, blocking collectives: 24.2 us -> none  [per_device(): lax.all_to_all(request.reshape(shards, 1, CAP), SHARD, split_axis=0, conc...]
    ppermute x16, waiting for transfers between devices: 25.7 us -> 12.6 us  [moved(): lax.ppermute(block, axis, [(i, (i + distance) % size) for i in range(size)])]
    all_to_all x0 -> x1, starting transfers between devices: none -> 9.89 us  [per_device(): lax.all_to_all(request.reshape(shards, 1, CAP), SHARD, split_axis=0, conc...]
    all_to_all x1, waiting for transfers between devices: 0.01 us -> 8.24 us  [per_device(): lax.all_to_all(found, SHARD, split_axis=0, concat_axis=0, tiled=True)]
    pallas_call x0 -> x1, Pallas kernels: none -> 6.72 us  [per_device(): pl.pallas_call(place_kernel, out_shape=jax.ShapeDtypeStruct((zs, ys, core...]
    all_to_all x1, starting transfers between devices: 10.2 us -> 15 us  [per_device(): lax.all_to_all(found, SHARD, split_axis=0, concat_axis=0, tiled=True)]
    pallas_call x1, Pallas kernels: 12.5 us -> 8.15 us  [per_device(): pl.pallas_call(item_kernel, out_shape=(jax.ShapeDtypeStruct((users * item...]
    unnamed x22 -> x26, local copies, waits for them, and re-layouts: 4.74 us -> 6.98 us
  transfers between devices with their start and end apart: 17 -> 18, of which waited for: 5 -> 6; matrix products, arithmetic and copies ran while one was open for 3% -> 3% of each run, Pallas kernels for 2% -> 7%
where the time goes in v5:
time: 163 us; the launch traced here: 160 us
  starting transfers between devices  88.4 us (54%)
  Pallas kernels  24.3 us (15%)
  waiting for transfers between devices  20.8 us (13%)
  blocking collectives  14.3 us (9%)
  local copies, waits for them, and re-layouts  10 us (6%)
    ppermute x16, starting transfers between devices, moved(): lax.ppermute(block, axis, [(i, (i + distance) % size) for i in range(size)])  63.5 us
    all_to_all x1, starting transfers between devices, per_device(): lax.all_to_all(found, SHARD, split_axis=0, concat_axis=0, tiled=True)  15 us
    all_gather x3, blocking collectives, per_device(): lax.all_gather(leaving, 'segment', axis=0, axis_index_groups=(even, odd)[...  14.3 us
    ppermute x16, waiting for transfers between devices, moved(): lax.ppermute(block, axis, [(i, (i + distance) % size) for i in range(size)])  12.6 us
    all_to_all x1, starting transfers between devices, per_device(): lax.all_to_all(request.reshape(shards, 1, CAP), SHARD, split_axis=0, conc...  9.89 us
    all_to_all x1, waiting for transfers between devices, per_device(): lax.all_to_all(found, SHARD, split_axis=0, concat_axis=0, tiled=True)  8.24 us
    pallas_call x1, Pallas kernels, per_device(): pl.pallas_call(item_kernel, out_shape=(jax.ShapeDtypeStruct((users * item...  8.15 us
    unnamed x26, local copies, waits for them, and re-layouts  6.98 us
  transfers between devices with their start and end apart: 18, of which 6 were waited for; matrix products, arithmetic and copies ran while one was open for 3% of the time, Pallas kernels for 7%

profile of v5, /device:TPU:6, one launch (start us, length us, event | category | flops | bytes accessed | tf_op | source)
XLA Modules:
  0.0 160.4 jit_solution(14319372825675479776)
XLA Ops:
  0.6 0.0 copy-start.8
  0.6 0.0 copy-start.9
  0.7 0.0 copy-start.7
  0.7 0.7 reshape_squeeze.3
  1.4 0.8 maximum_bitcast_fusion
  2.2 15.7 %collective-permute-start.2 = (bf16[1,8,4352]{2,1,0:T(8,128)(2,1)S(1)}, bf16[1,8,4352]{2,1,0:T(8,128)(2,1)S(1)}, u32[]{:S(2)}, u32[]{:S(2)}) collective-permute-start(bf16[1,8,4352]{2,1,0:T(8,128)(2,1)S(1)} %maximum_bitcast_fusion), channel_id=1, source_target_pairs={{0,64},{8,72},{16,80},{24,88},{32,96},{40,104},{48,112},{56,120},{... | collective-permute-start | bytes 208904 | tf_op jit(solution)/shard_map/ppermute | solution.py:272
  17.9 4.3 %collective-permute-start.1 = (bf16[1,8,4352]{2,1,0:T(8,128)(2,1)S(1)}, bf16[1,8,4352]{2,1,0:T(8,128)(2,1)S(1)}, u32[]{:S(2)}, u32[]{:S(2)}) collective-permute-start(bf16[1,8,4352]{2,1,0:T(8,128)(2,1)S(1)} %maximum_bitcast_fusion), channel_id=1, source_target_pairs={{0,32},{8,40},{16,48},{24,56},{32,64},{40,72},{48,80},{56,88},{64,... | collective-permute-start | bytes 208904 | tf_op jit(solution)/shard_map/ppermute | solution.py:272
  22.2 5.5 %collective-permute-start = (bf16[1,8,4352]{2,1,0:T(8,128)(2,1)S(1)}, bf16[1,8,4352]{2,1,0:T(8,128)(2,1)S(1)}, u32[]{:S(2)}, u32[]{:S(2)}) collective-permute-start(bf16[1,8,4352]{2,1,0:T(8,128)(2,1)S(1)} %maximum_bitcast_fusion), channel_id=1, source_target_pairs={{0,96},{8,104},{16,112},{24,120},{32,0},{40,8},{48,16},{56,24},{64... | collective-permute-start | bytes 208904 | tf_op jit(solution)/shard_map/ppermute | solution.py:272
  27.7 0.0 copy-start.5
  27.7 0.7 copy-done.5
  28.3 1.3 request.1
  29.7 9.9 %all-to-all-start = ((s32[128,1,8]{2,1,0:T(1,128)}), s32[128,1,8]{2,1,0:T(1,128)S(1)}, u32[]{:S(2)}, u32[]{:S(2)}) async-start(s32[128,1,8]{2,1,0:T(1,128)} %bitcast.6), calls=%async_computation | async-start | bytes 131072 | tf_op jit(solution)/shard_map/all_to_all | solution.py:285
  39.5 0.0 collective-permute-done.2
  39.6 0.0 collective-permute-done.1
  39.6 0.0 collective-permute-done
  39.6 5.0 %collective-permute-start.4 = (bf16[4,8,4352]{2,1,0:T(8,128)(2,1)S(1)}, bf16[4,8,4352]{2,1,0:T(8,128)(2,1)S(1)}, u32[]{:S(2)}, u32[]{:S(2)}) collective-permute-start(bf16[4,8,4352]{2,1,0:T(8,128)(2,1)S(1)} %pad_maximum_fusion), channel_id=1, source_target_pairs={{0,120},{8,0},{16,8},{24,16},{32,24},{40,32},{48,40},{56,48},{64,5... | collective-permute-start | bytes 835592 | tf_op jit(solution)/shard_map/ppermute | solution.py:272
  44.6 1.9 %collective-permute-start.3 = (bf16[4,8,4352]{2,1,0:T(8,128)(2,1)S(1)}, bf16[4,8,4352]{2,1,0:T(8,128)(2,1)S(1)}, u32[]{:S(2)}, u32[]{:S(2)}) collective-permute-start(bf16[4,8,4352]{2,1,0:T(8,128)(2,1)S(1)} %pad_maximum_fusion), channel_id=1, source_target_pairs={{0,8},{8,16},{16,24},{24,32},{32,40},{40,48},{48,56},{56,64},{64,7... | collective-permute-start | bytes 835592 | tf_op jit(solution)/shard_map/ppermute | solution.py:272
  46.6 2.9 %collective-permute-start.6 = (bf16[2,8,4352]{2,1,0:T(8,128)(2,1)S(1)}, bf16[2,8,4352]{2,1,0:T(8,128)(2,1)S(1)}, u32[]{:S(2)}, u32[]{:S(2)}) collective-permute-start(bf16[2,8,4352]{2,1,0:T(8,128)(2,1)S(1)} %get-tuple-element.70), channel_id=1, source_target_pairs={{0,16},{8,24},{16,32},{24,40},{32,48},{40,56},{48,64},{56,72},{64,... | collective-permute-start | bytes 417800 | tf_op jit(solution)/shard_map/ppermute | solution.py:272
  49.5 0.0 copy-start.2
  49.5 5.2 %collective-permute-start.5 = (bf16[2,8,4352]{2,1,0:T(8,128)(2,1)S(1)}, bf16[2,8,4352]{2,1,0:T(8,128)(2,1)S(1)}, u32[]{:S(2)}, u32[]{:S(2)}) collective-permute-start(bf16[2,8,4352]{2,1,0:T(8,128)(2,1)S(1)} %get-tuple-element.71), channel_id=1, source_target_pairs={{0,112},{8,120},{16,0},{24,8},{32,16},{40,24},{48,32},{56,40},{64,... | collective-permute-start | bytes 417800 | tf_op jit(solution)/shard_map/ppermute | solution.py:272
  54.7 0.6 constant_dynamic-update-slice_fusion.7
  55.3 0.6 constant_dynamic-update-slice_fusion.6
  55.9 0.6 constant_dynamic-update-slice_fusion.5
  56.6 0.6 constant_dynamic-update-slice_fusion.4
  57.2 3.6 %collective-permute-done.6 = bf16[2,8,4352]{2,1,0:T(8,128)(2,1)S(1)} collective-permute-done((bf16[2,8,4352]{2,1,0:T(8,128)(2,1)S(1)}, bf16[2,8,4352]{2,1,0:T(8,128)(2,1)S(1)}, u32[]{:S(2)}, u32[]{:S(2)}) %collective-permute-start.6) | collective-permute-done | bytes 139296 | tf_op jit(solution)/shard_map/ppermute | solution.py:272
  60.8 0.5 collective-permute-done.5
  61.4 0.7 constant_dynamic-update-slice_fusion.3
  62.1 0.7 constant_dynamic-update-slice_fusion.2
  62.8 0.7 constant_dynamic-update-slice_fusion.1
  63.5 0.7 constant_dynamic-update-slice_fusion.refs_0_
  64.2 4.6 %collective-permute-start.9 = (bf16[16,8,4352]{2,1,0:T(8,128)(2,1)}, bf16[16,8,4352]{2,1,0:T(8,128)(2,1)S(1)}, u32[]{:S(2)}, u32[]{:S(2)}) collective-permute-start(bf16[16,8,4352]{2,1,0:T(8,128)(2,1)} %constant_dynamic-update-slice_fusion.refs_0_), channel_id=1, source_target_pairs={{0,6},{2,0},{4,2},{6,4},{1,7},{3,1},{5,3},{7,5},{8,14},{10,8},{12,... | collective-permute-start | bytes 3342344 | tf_op jit(solution)/shard_map/ppermute | solution.py:272
  68.8 1.9 %collective-permute-start.7 = (bf16[16,8,4352]{2,1,0:T(8,128)(2,1)}, bf16[16,8,4352]{2,1,0:T(8,128)(2,1)S(1)}, u32[]{:S(2)}, u32[]{:S(2)}) collective-permute-start(bf16[16,8,4352]{2,1,0:T(8,128)(2,1)} %constant_dynamic-update-slice_fusion.refs_0_), channel_id=1, source_target_pairs={{0,2},{2,4},{4,6},{6,0},{1,3},{3,5},{5,7},{7,1},{8,10},{10,12},{12... | collective-permute-start | bytes 3342344 | tf_op jit(solution)/shard_map/ppermute | solution.py:272
  70.7 2.1 %table.1 = bf16[128,8,256]{2,1,0:T(8,128)(2,1)} custom-call(s32[128,8]{1,0:T(8,128)S(1)} %bitcast.23, bf16[2048,256]{1,0:T(8,128)(2,1)S(1)} %copy-done.2), custom_call_target="tpu_custom_call" | custom-call | tf_op jit(solution)/shard_map/table/pallas_call | solution.py:304
  72.8 15.0 %all-to-all-start.1 = ((bf16[128,8,256]{2,1,0:T(8,128)(2,1)}), bf16[128,8,256]{2,1,0:T(8,128)(2,1)S(1)}, u32[]{:S(2)}, u32[]{:S(2)}) async-start(bf16[128,8,256]{2,1,0:T(8,128)(2,1)} %table.1), calls=%async_computation.1 | async-start | bytes 1048576 | tf_op jit(solution)/shard_map/all_to_all | solution.py:312
  87.8 1.9 %collective-permute-start.11 = (bf16[16,8,4352]{2,1,0:T(8,128)(2,1)}, bf16[16,8,4352]{2,1,0:T(8,128)(2,1)S(1)}, u32[]{:S(2)}, u32[]{:S(2)}) collective-permute-start(bf16[16,8,4352]{2,1,0:T(8,128)(2,1)} %constant_dynamic-update-slice_fusion.refs_0_), channel_id=1, source_target_pairs={{0,1},{1,0},{2,3},{3,2},{4,5},{5,4},{6,7},{7,6},{8,9},{9,8},{10,11... | collective-permute-start | bytes 3342344 | tf_op jit(solution)/shard_map/ppermute | solution.py:272
  89.8 2.2 %collective-permute-done.9.refs_2_ = bf16[16,8,4352]{2,1,0:T(8,128)(2,1)S(1)} collective-permute-done((bf16[16,8,4352]{2,1,0:T(8,128)(2,1)}, bf16[16,8,4352]{2,1,0:T(8,128)(2,1)S(1)}, u32[]{:S(2)}, u32[]{:S(2)}) %collective-permute-start.9) | collective-permute-done | bytes 1114144 | tf_op jit(solution)/shard_map/ppermute | solution.py:272
  92.0 5.8 %collective-permute-done.7.refs_1_ = bf16[16,8,4352]{2,1,0:T(8,128)(2,1)S(1)} collective-permute-done((bf16[16,8,4352]{2,1,0:T(8,128)(2,1)}, bf16[16,8,4352]{2,1,0:T(8,128)(2,1)S(1)}, u32[]{:S(2)}, u32[]{:S(2)}) %collective-permute-start.7) | collective-permute-done | bytes 1114144 | tf_op jit(solution)/shard_map/ppermute | solution.py:272
  97.8 1.9 %collective-permute-start.12 = (bf16[16,8,4352]{2,1,0:T(8,128)(2,1)S(1)}, bf16[16,8,4352]{2,1,0:T(8,128)(2,1)}, u32[]{:S(2)}, u32[]{:S(2)}) collective-permute-start(bf16[16,8,4352]{2,1,0:T(8,128)(2,1)S(1)} %collective-permute-done.7.refs_1_), channel_id=1, source_target_pairs={{0,1},{1,0},{2,3},{3,2},{4,5},{5,4},{6,7},{7,6},{8,9},{9,8},{10,11... | collective-permute-start | bytes 3342344 | tf_op jit(solution)/shard_map/ppermute | solution.py:272
  99.7 2.4 %collective-permute-start.13 = (bf16[16,8,4352]{2,1,0:T(8,128)(2,1)S(1)}, bf16[16,8,4352]{2,1,0:T(8,128)(2,1)}, u32[]{:S(2)}, u32[]{:S(2)}) collective-permute-start(bf16[16,8,4352]{2,1,0:T(8,128)(2,1)S(1)} %collective-permute-done.9.refs_2_), channel_id=1, source_target_pairs={{0,1},{1,0},{2,3},{3,2},{4,5},{5,4},{6,7},{7,6},{8,9},{9,8},{10,11... | collective-permute-start | bytes 3342344 | tf_op jit(solution)/shard_map/ppermute | solution.py:272
  102.1 0.9 slice.13
  103.0 1.9 %collective-permute-start.10 = (bf16[8,8,4352]{2,1,0:T(8,128)(2,1)}, bf16[8,8,4352]{2,1,0:T(8,128)(2,1)S(1)}, u32[]{:S(2)}, u32[]{:S(2)}) collective-permute-start(bf16[8,8,4352]{2,1,0:T(8,128)(2,1)} %slice.13), channel_id=1, source_target_pairs={{0,6},{2,0},{4,2},{6,4},{1,7},{3,1},{5,3},{7,5},{8,14},{10,8},{12,... | collective-permute-start | bytes 1671176 | tf_op jit(solution)/shard_map/ppermute | solution.py:272
  104.9 0.0 copy-start.3
  104.9 0.0 copy-start.4
  104.9 0.0 copy-start.6
  105.0 0.8 slice.12
  105.8 3.9 %collective-permute-start.8 = (bf16[8,8,4352]{2,1,0:T(8,128)(2,1)}, bf16[8,8,4352]{2,1,0:T(8,128)(2,1)}, u32[]{:S(2)}, u32[]{:S(2)}) collective-permute-start(bf16[8,8,4352]{2,1,0:T(8,128)(2,1)} %slice.12), channel_id=1, source_target_pairs={{0,2},{2,4},{4,6},{6,0},{1,3},{3,5},{5,7},{7,1},{8,10},{10,12},{12... | collective-permute-start | bytes 1671176 | tf_op jit(solution)/shard_map/ppermute | solution.py:272
  109.7 0.0 collective-permute-done.11.refs_3_
  109.7 1.0 copy-done
  110.7 8.2 %all-to-all-done.1 = bf16[128,8,256]{2,1,0:T(8,128)(2,1)S(1)} async-done(((bf16[128,8,256]{2,1,0:T(8,128)(2,1)}), bf16[128,8,256]{2,1,0:T(8,128)(2,1)S(1)}, u32[]{:S(2)}, u32[]{:S(2)}) %all-to-all-start.1) | async-done | bytes 524320 | tf_op jit(solution)/shard_map/all_to_all | solution.py:312
  119.0 1.2 copy-done.1
  120.2 6.7 %place.1.placed_ref = bf16[16,4,2,8,4352]{4,3,2,1,0:T(8,128)(2,1)S(1)} custom-call(bf16[16,8,4352]{2,1,0:T(8,128)(2,1)} %constant_dynamic-update-slice_fusion.refs_0_, bf16[16,8,4352]{2,1,0:T(8,128)(2,1)S(1)} %collective-permute-done.7.refs_1_, bf16[16,8,4352]{2,1,0:T(8,128)(2,1)S(1)} %collective-permute-done.9.refs_2_, bf16[16,8,4352]{2,1,0:T(8,128)(2,1)S(1)} %copy-done.1, ...), custom_call_target="tpu_custom_call" | custom-call | bytes 14000000 | tf_op jit(solution)/shard_map/place/pallas_call | solution.py:315
  126.9 0.0 collective-permute-done.10.high_ref
  127.0 1.9 %collective-permute-start.14 = (bf16[8,8,4352]{2,1,0:T(8,128)(2,1)}, bf16[8,8,4352]{2,1,0:T(8,128)(2,1)S(1)}, u32[]{:S(2)}, u32[]{:S(2)}) collective-permute-start(bf16[8,8,4352]{2,1,0:T(8,128)(2,1)} %collective-permute-done.8.low_ref), channel_id=1, source_target_pairs={{0,1},{1,0},{2,3},{3,2},{4,5},{5,4},{6,7},{7,6},{8,9},{9,8},{10,11... | collective-permute-start | bytes 1671176 | tf_op jit(solution)/shard_map/ppermute | solution.py:272
  128.9 2.6 %collective-permute-start.15 = (bf16[8,8,4352]{2,1,0:T(8,128)(2,1)S(1)}, bf16[8,8,4352]{2,1,0:T(8,128)(2,1)S(1)}, u32[]{:S(2)}, u32[]{:S(2)}) collective-permute-start(bf16[8,8,4352]{2,1,0:T(8,128)(2,1)S(1)} %collective-permute-done.10.high_ref), channel_id=1, source_target_pairs={{0,1},{1,0},{2,3},{3,2},{4,5},{5,4},{6,7},{7,6},{8,9},{9,8},{10,11... | collective-permute-start | bytes 1671176 | tf_op jit(solution)/shard_map/ppermute | solution.py:272
  131.5 1.0 list.1
  132.5 0.0 collective-permute-done.14.low_swapped_ref
  132.6 0.3 collective-permute-done.15.high_swapped_ref
  132.9 8.2 %item.1 = (bf16[512,1024]{1,0:T(8,128)(2,1)S(1)}, bf16[512,1024]{1,0:T(8,128)(2,1)S(1)}, bf16[16,4,2,8,4352]{4,3,2,1,0:T(8,128)(2,1)S(1)}, bf16[4,1024]{1,0:T(4,128)(2,1)S(1)}, f32[1,512]{1,0:T(1,128)S(1)}) custom-call(bf16[8,8,4352]{2,1,0:T(8,128)(2,1)} %collective-permute-done.8.low_ref, ...), custom_call_target="tpu_custom_call", output_to_operand_aliasing={{2}: (4, {})} | custom-call | tf_op jit(solution)/shard_map/item/pallas_call | solution.py:347
  141.0 4.4 %all-gather.3.state_ref = bf16[2,4,1024]{2,1,0:T(4,128)(2,1)S(1)} all-gather(bf16[1,4,1024]{2,1,0:T(4,128)(2,1)S(1)} %bitcast.24), channel_id=2, replica_groups={{0,128},{256,384},{1,129},{257,385},{2,130},{258,386},{3,131},{259,387}..., dimensions={0}, use_global_device_ids=true | all-gather | bytes 24576 | tf_op jit(solution)/shard_map/all_gather | solution.py:367
  145.4 1.5 section.3
  146.9 5.6 %all-gather.4.state_ref = bf16[2,4,1024]{2,1,0:T(4,128)(2,1)S(1)} all-gather(bf16[1,4,1024]{2,1,0:T(4,128)(2,1)S(1)} %bitcast.25), channel_id=3, replica_groups={{128,256},{0,384},{129,257},{1,385},{130,258},{2,386},{131,259},{3,387}..., dimensions={0}, use_global_device_ids=true | all-gather | bytes 24576 | tf_op jit(solution)/shard_map/all_gather | solution.py:367
  152.4 1.5 section.4
  153.9 4.4 %all-gather.5.state_ref = bf16[2,4,1024]{2,1,0:T(4,128)(2,1)S(1)} all-gather(bf16[1,4,1024]{2,1,0:T(4,128)(2,1)S(1)} %bitcast.26), channel_id=4, replica_groups={{0,128},{256,384},{1,129},{257,385},{2,130},{258,386},{3,131},{259,387}..., dimensions={0}, use_global_device_ids=true | all-gather | bytes 24576 | tf_op jit(solution)/shard_map/all_gather | solution.py:367
  158.3 2.1 %section.5 = (bf16[4,1024]{1,0:T(4,128)(2,1)}, f32[1,512]{1,0:T(1,128)}) custom-call(bf16[2,4,1024]{2,1,0:T(4,128)(2,1)S(1)} %all-gather.5.state_ref, bf16[512,1024]{1,0:T(8,128)(2,1)S(1)} %get-tuple-element.60.key_ref, bf16[512,1024]{1,0:T(8,128)(2,1)S(1)} %get-tuple-element.61.value_ref, bf16[1024,4352]{1,0:T(8,128)(2,1)S(1)} %bitcast.21, ...), custom_call_target="tpu_custom_call" | custom-call | tf_op jit(solution)/shard_map/section/pallas_call | solution.py:371
  (17 shorter events, 0.1 us)
Async XLA Ops:
  0.6 54.7 %copy-start.8 = (bf16[1,8,1024]{2,1,0:T(8,128)(2,1)S(1)}, bf16[1,8,1024]{2,1,0:T(8,128)(2,1)}, u32[]{:S(2)}) copy-start(bf16[1,8,1024]{2,1,0:T(8,128)(2,1)} %param.14) | copy-start | bytes 49156
  0.6 54.7 %copy-start.9 = (bf16[1,8,1024]{2,1,0:T(8,128)(2,1)S(1)}, bf16[1,8,1024]{2,1,0:T(8,128)(2,1)}, u32[]{:S(2)}) copy-start(bf16[1,8,1024]{2,1,0:T(8,128)(2,1)} %param.13) | copy-start | bytes 49156
  0.7 54.6 %copy-start.7 = (bf16[1,8,2048]{2,1,0:T(8,128)(2,1)S(1)}, bf16[1,8,2048]{2,1,0:T(8,128)(2,1)}, u32[]{:S(2)}) copy-start(bf16[1,8,2048]{2,1,0:T(8,128)(2,1)} %param.12) | copy-start | bytes 98308
  2.2 37.4 %collective-permute-start.2 = (bf16[1,8,4352]{2,1,0:T(8,128)(2,1)S(1)}, bf16[1,8,4352]{2,1,0:T(8,128)(2,1)S(1)}, u32[]{:S(2)}, u32[]{:S(2)}) collective-permute-start(bf16[1,8,4352]{2,1,0:T(8,128)(2,1)S(1)} %maximum_bitcast_fusion), channel_id=1, source_target_pairs={{0,64},{8,72},{16,80},{24,88},{32,96},{40,104},{48,112},{56,120},{... | collective-permute-start | bytes 208904 | tf_op jit(solution)/shard_map/ppermute | solution.py:272
  17.9 21.7 %collective-permute-start.1 = (bf16[1,8,4352]{2,1,0:T(8,128)(2,1)S(1)}, bf16[1,8,4352]{2,1,0:T(8,128)(2,1)S(1)}, u32[]{:S(2)}, u32[]{:S(2)}) collective-permute-start(bf16[1,8,4352]{2,1,0:T(8,128)(2,1)S(1)} %maximum_bitcast_fusion), channel_id=1, source_target_pairs={{0,32},{8,40},{16,48},{24,56},{32,64},{40,72},{48,80},{56,88},{64,... | collective-permute-start | bytes 208904 | tf_op jit(solution)/shard_map/ppermute | solution.py:272
  22.2 17.4 %collective-permute-start = (bf16[1,8,4352]{2,1,0:T(8,128)(2,1)S(1)}, bf16[1,8,4352]{2,1,0:T(8,128)(2,1)S(1)}, u32[]{:S(2)}, u32[]{:S(2)}) collective-permute-start(bf16[1,8,4352]{2,1,0:T(8,128)(2,1)S(1)} %maximum_bitcast_fusion), channel_id=1, source_target_pairs={{0,96},{8,104},{16,112},{24,120},{32,0},{40,8},{48,16},{56,24},{64... | collective-permute-start | bytes 208904 | tf_op jit(solution)/shard_map/ppermute | solution.py:272
  27.7 0.7 copy-start.5
  29.7 27.5 %all-to-all-start = ((s32[128,1,8]{2,1,0:T(1,128)}), s32[128,1,8]{2,1,0:T(1,128)S(1)}, u32[]{:S(2)}, u32[]{:S(2)}) async-start(s32[128,1,8]{2,1,0:T(1,128)} %bitcast.6), calls=%async_computation | async-start | bytes 131072 | tf_op jit(solution)/shard_map/all_to_all | solution.py:285
  39.6 21.7 %collective-permute-start.4 = (bf16[4,8,4352]{2,1,0:T(8,128)(2,1)S(1)}, bf16[4,8,4352]{2,1,0:T(8,128)(2,1)S(1)}, u32[]{:S(2)}, u32[]{:S(2)}) collective-permute-start(bf16[4,8,4352]{2,1,0:T(8,128)(2,1)S(1)} %pad_maximum_fusion), channel_id=1, source_target_pairs={{0,120},{8,0},{16,8},{24,16},{32,24},{40,32},{48,40},{56,48},{64,5... | collective-permute-start | bytes 835592 | tf_op jit(solution)/shard_map/ppermute | solution.py:272
  44.6 16.8 %collective-permute-start.3 = (bf16[4,8,4352]{2,1,0:T(8,128)(2,1)S(1)}, bf16[4,8,4352]{2,1,0:T(8,128)(2,1)S(1)}, u32[]{:S(2)}, u32[]{:S(2)}) collective-permute-start(bf16[4,8,4352]{2,1,0:T(8,128)(2,1)S(1)} %pad_maximum_fusion), channel_id=1, source_target_pairs={{0,8},{8,16},{16,24},{24,32},{32,40},{40,48},{48,56},{56,64},{64,7... | collective-permute-start | bytes 835592 | tf_op jit(solution)/shard_map/ppermute | solution.py:272
  46.6 14.3 %collective-permute-start.6 = (bf16[2,8,4352]{2,1,0:T(8,128)(2,1)S(1)}, bf16[2,8,4352]{2,1,0:T(8,128)(2,1)S(1)}, u32[]{:S(2)}, u32[]{:S(2)}) collective-permute-start(bf16[2,8,4352]{2,1,0:T(8,128)(2,1)S(1)} %get-tuple-element.70), channel_id=1, source_target_pairs={{0,16},{8,24},{16,32},{24,40},{32,48},{40,56},{48,64},{56,72},{64,... | collective-permute-start | bytes 417800 | tf_op jit(solution)/shard_map/ppermute | solution.py:272
  49.5 21.2 %copy-start.2 = (bf16[2048,256]{1,0:T(8,128)(2,1)S(1)}, bf16[2048,256]{1,0:T(8,128)(2,1)}, u32[]{:S(2)}) copy-start(bf16[2048,256]{1,0:T(8,128)(2,1)} %table_ref.1) | copy-start | bytes 3145732
  49.5 11.9 %collective-permute-start.5 = (bf16[2,8,4352]{2,1,0:T(8,128)(2,1)S(1)}, bf16[2,8,4352]{2,1,0:T(8,128)(2,1)S(1)}, u32[]{:S(2)}, u32[]{:S(2)}) collective-permute-start(bf16[2,8,4352]{2,1,0:T(8,128)(2,1)S(1)} %get-tuple-element.71), channel_id=1, source_target_pairs={{0,112},{8,120},{16,0},{24,8},{32,16},{40,24},{48,32},{56,40},{64,... | collective-permute-start | bytes 417800 | tf_op jit(solution)/shard_map/ppermute | solution.py:272
  64.2 27.8 %collective-permute-start.9 = (bf16[16,8,4352]{2,1,0:T(8,128)(2,1)}, bf16[16,8,4352]{2,1,0:T(8,128)(2,1)S(1)}, u32[]{:S(2)}, u32[]{:S(2)}) collective-permute-start(bf16[16,8,4352]{2,1,0:T(8,128)(2,1)} %constant_dynamic-update-slice_fusion.refs_0_), channel_id=1, source_target_pairs={{0,6},{2,0},{4,2},{6,4},{1,7},{3,1},{5,3},{7,5},{8,14},{10,8},{12,... | collective-permute-start | bytes 3342344 | tf_op jit(solution)/shard_map/ppermute | solution.py:272
  68.8 29.0 %collective-permute-start.7 = (bf16[16,8,4352]{2,1,0:T(8,128)(2,1)}, bf16[16,8,4352]{2,1,0:T(8,128)(2,1)S(1)}, u32[]{:S(2)}, u32[]{:S(2)}) collective-permute-start(bf16[16,8,4352]{2,1,0:T(8,128)(2,1)} %constant_dynamic-update-slice_fusion.refs_0_), channel_id=1, source_target_pairs={{0,2},{2,4},{4,6},{6,0},{1,3},{3,5},{5,7},{7,1},{8,10},{10,12},{12... | collective-permute-start | bytes 3342344 | tf_op jit(solution)/shard_map/ppermute | solution.py:272
  72.8 46.1 %all-to-all-start.1 = ((bf16[128,8,256]{2,1,0:T(8,128)(2,1)}), bf16[128,8,256]{2,1,0:T(8,128)(2,1)S(1)}, u32[]{:S(2)}, u32[]{:S(2)}) async-start(bf16[128,8,256]{2,1,0:T(8,128)(2,1)} %table.1), calls=%async_computation.1 | async-start | bytes 1048576 | tf_op jit(solution)/shard_map/all_to_all | solution.py:312
  87.8 21.9 %collective-permute-start.11 = (bf16[16,8,4352]{2,1,0:T(8,128)(2,1)}, bf16[16,8,4352]{2,1,0:T(8,128)(2,1)S(1)}, u32[]{:S(2)}, u32[]{:S(2)}) collective-permute-start(bf16[16,8,4352]{2,1,0:T(8,128)(2,1)} %constant_dynamic-update-slice_fusion.refs_0_), channel_id=1, source_target_pairs={{0,1},{1,0},{2,3},{3,2},{4,5},{5,4},{6,7},{7,6},{8,9},{9,8},{10,11... | collective-permute-start | bytes 3342344 | tf_op jit(solution)/shard_map/ppermute | solution.py:272
  97.8 21.1 %collective-permute-start.12 = (bf16[16,8,4352]{2,1,0:T(8,128)(2,1)S(1)}, bf16[16,8,4352]{2,1,0:T(8,128)(2,1)}, u32[]{:S(2)}, u32[]{:S(2)}) collective-permute-start(bf16[16,8,4352]{2,1,0:T(8,128)(2,1)S(1)} %collective-permute-done.7.refs_1_), channel_id=1, source_target_pairs={{0,1},{1,0},{2,3},{3,2},{4,5},{5,4},{6,7},{7,6},{8,9},{9,8},{10,11... | collective-permute-start | bytes 3342344 | tf_op jit(solution)/shard_map/ppermute | solution.py:272
  99.7 19.2 %collective-permute-start.13 = (bf16[16,8,4352]{2,1,0:T(8,128)(2,1)S(1)}, bf16[16,8,4352]{2,1,0:T(8,128)(2,1)}, u32[]{:S(2)}, u32[]{:S(2)}) collective-permute-start(bf16[16,8,4352]{2,1,0:T(8,128)(2,1)S(1)} %collective-permute-done.9.refs_2_), channel_id=1, source_target_pairs={{0,1},{1,0},{2,3},{3,2},{4,5},{5,4},{6,7},{7,6},{8,9},{9,8},{10,11... | collective-permute-start | bytes 3342344 | tf_op jit(solution)/shard_map/ppermute | solution.py:272
  103.0 23.9 %collective-permute-start.10 = (bf16[8,8,4352]{2,1,0:T(8,128)(2,1)}, bf16[8,8,4352]{2,1,0:T(8,128)(2,1)S(1)}, u32[]{:S(2)}, u32[]{:S(2)}) collective-permute-start(bf16[8,8,4352]{2,1,0:T(8,128)(2,1)} %slice.13), channel_id=1, source_target_pairs={{0,6},{2,0},{4,2},{6,4},{1,7},{3,1},{5,3},{7,5},{8,14},{10,8},{12,... | collective-permute-start | bytes 1671176 | tf_op jit(solution)/shard_map/ppermute | solution.py:272
  104.9 26.6 %copy-start.3 = (bf16[4,1024]{1,0:T(4,128)(2,1)S(1)}, bf16[4,1024]{1,0:T(4,128)(2,1)}, u32[]{:S(2)}) copy-start(bf16[4,1024]{1,0:T(4,128)(2,1)} %state_ref.1) | copy-start | bytes 24580
  104.9 26.6 %copy-start.4 = (f32[1,1024]{1,0:T(1,128)S(1)}, f32[1,1024]{1,0:T(1,128)}, u32[]{:S(2)}) copy-start(f32[1,1024]{1,0:T(1,128)} %gain_ref.1) | copy-start | bytes 12292
  104.9 26.6 %copy-start.6 = (s32[1,4]{1,0:T(1,128)S(1)}, s32[1,4]{1,0:T(1,128)}, u32[]{:S(2)}) copy-start(s32[1,4]{1,0:T(1,128)} %count_ref.1) | copy-start | bytes 52
  105.8 21.2 %collective-permute-start.8 = (bf16[8,8,4352]{2,1,0:T(8,128)(2,1)}, bf16[8,8,4352]{2,1,0:T(8,128)(2,1)}, u32[]{:S(2)}, u32[]{:S(2)}) collective-permute-start(bf16[8,8,4352]{2,1,0:T(8,128)(2,1)} %slice.12), channel_id=1, source_target_pairs={{0,2},{2,4},{4,6},{6,0},{1,3},{3,5},{5,7},{7,1},{8,10},{10,12},{12... | collective-permute-start | bytes 1671176 | tf_op jit(solution)/shard_map/ppermute | solution.py:272
  109.7 1.0 copy-start
  119.0 1.2 copy-start.1
  127.0 5.6 %collective-permute-start.14 = (bf16[8,8,4352]{2,1,0:T(8,128)(2,1)}, bf16[8,8,4352]{2,1,0:T(8,128)(2,1)S(1)}, u32[]{:S(2)}, u32[]{:S(2)}) collective-permute-start(bf16[8,8,4352]{2,1,0:T(8,128)(2,1)} %collective-permute-done.8.low_ref), channel_id=1, source_target_pairs={{0,1},{1,0},{2,3},{3,2},{4,5},{5,4},{6,7},{7,6},{8,9},{9,8},{10,11... | collective-permute-start | bytes 1671176 | tf_op jit(solution)/shard_map/ppermute | solution.py:272
  128.9 4.0 %collective-permute-start.15 = (bf16[8,8,4352]{2,1,0:T(8,128)(2,1)S(1)}, bf16[8,8,4352]{2,1,0:T(8,128)(2,1)S(1)}, u32[]{:S(2)}, u32[]{:S(2)}) collective-permute-start(bf16[8,8,4352]{2,1,0:T(8,128)(2,1)S(1)} %collective-permute-done.10.high_ref), channel_id=1, source_target_pairs={{0,1},{1,0},{2,3},{3,2},{4,5},{5,4},{6,7},{7,6},{8,9},{9,8},{10,11... | collective-permute-start | bytes 1671176 | tf_op jit(solution)/shard_map/ppermute | solution.py:272

commit v6 on v5

--- a/solution.py
+++ b/solution.py
@@ -181,19 +181,48 @@
     next_ref,
     score_ref,
     sems,
+    load_sems,
 ):
-    del placed_ref
-    zs = weight_ref.shape[0]
+    zs, ys, cores, _, _ = weight_ref.shape
     depth = width = key_ref.shape[1]
     emb = listed_ref.shape[1]
-    pieces = (low_ref, high_ref, low_swapped_ref, high_swapped_ref)
-    kinds = [(piece, i % 2 * (zs // 2), 2, i // 2) for i, piece in enumerate(pieces)]
+    half = zs // 2
+    kinds = (
+        (low_ref, 0, 2, 0),
+        (high_ref, half, 2, 0),
+        (low_swapped_ref, 0, 2, 1),
+        (high_swapped_ref, half, 2, 1),
+    )
     place(kinds, weight_ref, sems)
+    y, core = lax.axis_index("y"), lax.axis_index("core")
+    copies = []
+    for part, (first, size) in enumerate(
+        ((4 * width, emb), (0, 2 * width), (2 * width, 2 * width))
+    ):
+        mine = []
+        for number, (from_y, from_core) in enumerate(
+            (from_y, from_core) for from_y in (0, 1, ys - 1) for from_core in range(cores)
+        ):
+            at = (
+                slice(None),
+                lax.rem(y + from_y, ys),
+                lax.rem(core + from_core, cores),
+                slice(None),
+                pl.ds(first, size),
+            )
+            copy = pltpu.make_async_copy(
+                placed_ref.at[at], weight_ref.at[at], load_sems.at[part, number]
+            )
+            copy.start()
+            mine.append(copy)
+        copies.append(mine)
 
     def weight(first, size):
         return weight_ref[:, :, :, :, first : first + size].reshape(depth, size)
 
     wait_placed(kinds, weight_ref, sems)
+    for copy in copies[0]:
+        copy.wait()
     listed = listed_ref[...]
     packed = weight(4 * width, emb)
     split = depth // emb
@@ -210,6 +239,8 @@
             jax.nn.silu(jnp.dot(listed, lift, preferred_element_type=F32)).astype(BF16)
         )
     lifted = jnp.concatenate(lifted, axis=1)
+    for copy in copies[1]:
+        copy.wait()
     block = 512
     for first in range(0, 2 * width, block):
         made = jnp.dot(lifted, weight(first, block), preferred_element_type=F32).astype(BF16)
@@ -217,6 +248,8 @@
             key_ref[:, first : first + block] = made
         else:
             value_ref[:, first - width : first - width + block] = made
+    for copy in copies[2]:
+        copy.wait()
     next_ref[...], score_ref[...] = section_step(
         state_ref[...],
         key_ref,
@@ -262,7 +295,7 @@
     items = item_ids.shape[2]
     shard_rows, emb = item_table.shape
     depth = w_ask.shape[1]
-    small, big = (pltpu.CompilerParams(vmem_limit_bytes=size << 20) for size in (12, 24))
+    small, big, wide = (pltpu.CompilerParams(vmem_limit_bytes=size << 20) for size in (12, 34, 54))
 
     own = jnp.concatenate(
         [w_pair[0], w_ask[0], w_back[0], w_lift[0].reshape(depth, emb)], axis=1
@@ -298,9 +331,8 @@
     half = zs // 2
     below, above = moved(column, "y", 1), moved(column, "y", -1)
     across = (moved(below[:half], "y", 1), moved(above[half:], "y", -1))
-    both = lax.optimization_barrier((below, above))
     early = [column, below, above]
-    early = early + [moved(piece, "core", 1) for piece in (column, *both)]
+    early = early + [moved(piece, "core", 1) for piece in early]
     found = pl.pallas_call(
         table_kernel,
         out_shape=jax.ShapeDtypeStruct((shards, CAP, emb), BF16),
@@ -311,14 +343,13 @@
     )(arrived.reshape(shards, CAP), item_table)
     returned = lax.all_to_all(found, SHARD, split_axis=0, concat_axis=0, tiled=True)
 
-    early, returned = lax.optimization_barrier((early, returned))
     weights = pl.pallas_call(
         place_kernel,
         out_shape=jax.ShapeDtypeStruct((zs, ys, cores, depth, own.shape[2]), BF16),
         in_specs=[pl.BlockSpec(memory_space=pl.ANY)] * len(early),
-        out_specs=vmem(),
+        out_specs=pl.BlockSpec(memory_space=pltpu.HBM),
         scratch_shapes=[pltpu.SemaphoreType.DMA((len(early),))],
-        compiler_params=small,
+        compiler_params=wide,
         cost_estimate=pl.CostEstimate(flops=0, bytes_accessed=14_000_000, transcendentals=0),
         name="place",
     )(*early)
@@ -352,10 +383,14 @@
             jax.ShapeDtypeStruct((zs, ys, cores, depth, own.shape[2]), BF16),
         )
         + section_shape,
-        in_specs=[pl.BlockSpec(memory_space=pl.ANY)] * 4 + [vmem()] * 5,
+        in_specs=[pl.BlockSpec(memory_space=pl.ANY)] * len(late)
+        + [pl.BlockSpec(memory_space=pltpu.HBM)]
+        + [vmem()] * 4,
         out_specs=(vmem(),) * 5,
-        scratch_shapes=[pltpu.SemaphoreType.DMA((len(late),))],
-        input_output_aliases={4: 2},
+        scratch_shapes=[
+            pltpu.SemaphoreType.DMA((len(late),)),
+            pltpu.SemaphoreType.DMA((3, 6)),
+        ],
         compiler_params=big,
         name="item",
     )(*late, weights, listed, entering, gains, length_row)

time: 163 us -> 351 us (2.15)
  Pallas kernels: 24.3 us -> 224 us
  waiting for transfers between devices: 20.8 us -> 10.7 us
    pallas_call x1, Pallas kernels: 6.72 us -> 204 us  [per_device(): pl.pallas_call(place_kernel, out_shape=jax.ShapeDtypeStruct((zs, ys, core...]
    all_to_all x1, waiting for transfers between devices: 8.24 us -> 0.01 us  [per_device(): lax.all_to_all(found, SHARD, split_axis=0, concat_axis=0, tiled=True)]
    unnamed x26 -> x30, local copies, waits for them, and re-layouts: 6.98 us -> 7.22 us
  transfers between devices with their start and end apart: 18 -> 18, of which waited for: 6 -> 5; matrix products, arithmetic and copies ran while one was open for 3% -> 1% of each run, Pallas kernels for 7% -> 60%
where the time goes in v6:
time: 351 us; the launch traced here: 349 us
  Pallas kernels  224 us (64%)
  starting transfers between devices  88 us (25%)
  blocking collectives  14.3 us (4%)
  waiting for transfers between devices  10.7 us (3%)
  local copies, waits for them, and re-layouts  9.72 us (3%)
    pallas_call x1, Pallas kernels, per_device(): pl.pallas_call(place_kernel, out_shape=jax.ShapeDtypeStruct((zs, ys, core...  204 us
    ppermute x16, starting transfers between devices, moved(): lax.ppermute(block, axis, [(i, (i + distance) % size) for i in range(size)])  63.2 us
    all_to_all x1, starting transfers between devices, per_device(): lax.all_to_all(found, SHARD, split_axis=0, concat_axis=0, tiled=True)  15 us
    all_gather x3, blocking collectives, per_device(): lax.all_gather(leaving, 'segment', axis=0, axis_index_groups=(even, odd)[...  14.3 us
    ppermute x16, waiting for transfers between devices, moved(): lax.ppermute(block, axis, [(i, (i + distance) % size) for i in range(size)])  10.7 us
    pallas_call x1, Pallas kernels, per_device(): pl.pallas_call(item_kernel, out_shape=(jax.ShapeDtypeStruct((users * item...  10.4 us
    all_to_all x1, starting transfers between devices, per_device(): lax.all_to_all(request.reshape(shards, 1, CAP), SHARD, split_axis=0, conc...  9.89 us
    unnamed x30, local copies, waits for them, and re-layouts  7.22 us
  transfers between devices with their start and end apart: 18, of which 5 were waited for; matrix products, arithmetic and copies ran while one was open for 1% of the time, Pallas kernels for 60%

profile of v6, /device:TPU:6, one launch (start us, length us, event | category | flops | bytes accessed | tf_op | source)
XLA Modules:
  0.0 348.8 jit_solution(14867206611354170297)
XLA Ops:
  0.6 0.0 copy-start.10
  0.6 0.0 copy-start.11
  0.7 0.0 copy-start.9
  0.7 0.7 reshape_squeeze.3
  1.4 0.8 maximum_bitcast_fusion
  2.2 15.7 %collective-permute-start.2 = (bf16[1,8,4352]{2,1,0:T(8,128)(2,1)S(1)}, bf16[1,8,4352]{2,1,0:T(8,128)(2,1)S(1)}, u32[]{:S(2)}, u32[]{:S(2)}) collective-permute-start(bf16[1,8,4352]{2,1,0:T(8,128)(2,1)S(1)} %maximum_bitcast_fusion), channel_id=1, source_target_pairs={{0,64},{8,72},{16,80},{24,88},{32,96},{40,104},{48,112},{56,120},{... | collective-permute-start | bytes 208904 | tf_op jit(solution)/shard_map/ppermute | solution.py:305
  17.9 4.3 %collective-permute-start.1 = (bf16[1,8,4352]{2,1,0:T(8,128)(2,1)S(1)}, bf16[1,8,4352]{2,1,0:T(8,128)(2,1)S(1)}, u32[]{:S(2)}, u32[]{:S(2)}) collective-permute-start(bf16[1,8,4352]{2,1,0:T(8,128)(2,1)S(1)} %maximum_bitcast_fusion), channel_id=1, source_target_pairs={{0,32},{8,40},{16,48},{24,56},{32,64},{40,72},{48,80},{56,88},{64,... | collective-permute-start | bytes 208904 | tf_op jit(solution)/shard_map/ppermute | solution.py:305
  22.2 5.5 %collective-permute-start = (bf16[1,8,4352]{2,1,0:T(8,128)(2,1)S(1)}, bf16[1,8,4352]{2,1,0:T(8,128)(2,1)S(1)}, u32[]{:S(2)}, u32[]{:S(2)}) collective-permute-start(bf16[1,8,4352]{2,1,0:T(8,128)(2,1)S(1)} %maximum_bitcast_fusion), channel_id=1, source_target_pairs={{0,96},{8,104},{16,112},{24,120},{32,0},{40,8},{48,16},{56,24},{64... | collective-permute-start | bytes 208904 | tf_op jit(solution)/shard_map/ppermute | solution.py:305
  27.7 0.0 copy-start.3
  27.7 0.7 copy-done.3
  28.3 1.3 request.1
  29.6 9.9 %all-to-all-start = ((s32[128,1,8]{2,1,0:T(1,128)}), s32[128,1,8]{2,1,0:T(1,128)S(1)}, u32[]{:S(2)}, u32[]{:S(2)}) async-start(s32[128,1,8]{2,1,0:T(1,128)} %bitcast.6), calls=%async_computation | async-start | bytes 131072 | tf_op jit(solution)/shard_map/all_to_all | solution.py:318
  39.5 0.0 collective-permute-done.2
  39.6 0.0 collective-permute-done.1
  39.6 5.0 %collective-permute-start.4 = (bf16[4,8,4352]{2,1,0:T(8,128)(2,1)S(1)}, bf16[4,8,4352]{2,1,0:T(8,128)(2,1)S(1)}, u32[]{:S(2)}, u32[]{:S(2)}) collective-permute-start(bf16[4,8,4352]{2,1,0:T(8,128)(2,1)S(1)} %pad_maximum_fusion), channel_id=1, source_target_pairs={{0,120},{8,0},{16,8},{24,16},{32,24},{40,32},{48,40},{56,48},{64,5... | collective-permute-start | bytes 835592 | tf_op jit(solution)/shard_map/ppermute | solution.py:305
  44.6 1.9 collective-permute-start.3
  46.5 2.9 collective-permute-start.6
  49.5 0.0 copy-start
  49.5 5.2 %collective-permute-start.5 = (bf16[2,8,4352]{2,1,0:T(8,128)(2,1)S(1)}, bf16[2,8,4352]{2,1,0:T(8,128)(2,1)S(1)}, u32[]{:S(2)}, u32[]{:S(2)}) collective-permute-start(bf16[2,8,4352]{2,1,0:T(8,128)(2,1)S(1)} %get-tuple-element.53), channel_id=1, source_target_pairs={{0,112},{8,120},{16,0},{24,8},{32,16},{40,24},{48,32},{56,40},{64,... | collective-permute-start | bytes 417800 | tf_op jit(solution)/shard_map/ppermute | solution.py:305
  54.7 0.6 constant_dynamic-update-slice_fusion.7
  55.3 0.6 constant_dynamic-update-slice_fusion.6
  55.9 0.6 constant_dynamic-update-slice_fusion.5
  56.6 0.6 constant_dynamic-update-slice_fusion.4
  57.2 0.0 all-to-all-done
  57.2 3.6 %collective-permute-done.6 = bf16[2,8,4352]{2,1,0:T(8,128)(2,1)S(1)} collective-permute-done((bf16[2,8,4352]{2,1,0:T(8,128)(2,1)S(1)}, bf16[2,8,4352]{2,1,0:T(8,128)(2,1)S(1)}, u32[]{:S(2)}, u32[]{:S(2)}) %collective-permute-start.6) | collective-permute-done | bytes 139296 | tf_op jit(solution)/shard_map/ppermute | solution.py:305
  60.8 0.5 collective-permute-done.5
  61.4 0.0 collective-permute-done.4
  61.4 0.0 collective-permute-done.3
  61.4 0.7 constant_dynamic-update-slice_fusion.3
  62.1 0.7 constant_dynamic-update-slice_fusion.2
  62.8 0.7 constant_dynamic-update-slice_fusion.1
  63.5 0.7 constant_dynamic-update-slice_fusion.refs_0_
  64.2 4.6 %collective-permute-start.9 = (bf16[16,8,4352]{2,1,0:T(8,128)(2,1)}, bf16[16,8,4352]{2,1,0:T(8,128)(2,1)S(1)}, u32[]{:S(2)}, u32[]{:S(2)}) collective-permute-start(bf16[16,8,4352]{2,1,0:T(8,128)(2,1)} %constant_dynamic-update-slice_fusion.refs_0_), channel_id=1, source_target_pairs={{0,6},{2,0},{4,2},{6,4},{1,7},{3,1},{5,3},{7,5},{8,14},{10,8},{12,... | collective-permute-start | bytes 3342344 | tf_op jit(solution)/shard_map/ppermute | solution.py:305
  68.8 1.9 collective-permute-start.7
  70.7 2.1 table.1
  72.8 15.0 %all-to-all-start.1 = ((bf16[128,8,256]{2,1,0:T(8,128)(2,1)}), bf16[128,8,256]{2,1,0:T(8,128)(2,1)S(1)}, u32[]{:S(2)}, u32[]{:S(2)}) async-start(bf16[128,8,256]{2,1,0:T(8,128)(2,1)} %table.1), calls=%async_computation.1 | async-start | bytes 1048576 | tf_op jit(solution)/shard_map/all_to_all | solution.py:344
  87.8 1.9 collective-permute-start.11
  89.8 2.2 collective-permute-done.9.refs_2_
  92.0 1.9 collective-permute-start.13
  93.9 4.0 %collective-permute-done.7.refs_1_ = bf16[16,8,4352]{2,1,0:T(8,128)(2,1)} collective-permute-done((bf16[16,8,4352]{2,1,0:T(8,128)(2,1)}, bf16[16,8,4352]{2,1,0:T(8,128)(2,1)}, u32[]{:S(2)}, u32[]{:S(2)}) %collective-permute-start.7) | collective-permute-done | bytes 1114144 | tf_op jit(solution)/shard_map/ppermute | solution.py:305
  97.9 1.9 collective-permute-start.12
  99.9 2.0 collective-permute-start.10
  101.9 1.1 slice.12
  103.0 0.0 copy-start.1
  103.0 0.0 copy-start.2
  103.0 0.0 copy-start.4
  103.0 4.0 %collective-permute-start.8 = (bf16[8,8,4352]{2,1,0:T(8,128)(2,1)S(1)}, bf16[8,8,4352]{2,1,0:T(8,128)(2,1)S(1)}, u32[]{:S(2)}, u32[]{:S(2)}) collective-permute-start(bf16[8,8,4352]{2,1,0:T(8,128)(2,1)S(1)} %slice.12), channel_id=1, source_target_pairs={{0,2},{2,4},{4,6},{6,0},{1,3},{3,5},{5,7},{7,1},{8,10},{10,12},{12... | collective-permute-start | bytes 1671176 | tf_op jit(solution)/shard_map/ppermute | solution.py:305
  107.0 0.0 collective-permute-done.11.refs_3_
  107.0 0.0 collective-permute-done.12.refs_4_
  107.0 1.0 copy-done.6
  108.0 0.4 copy-done.7
  108.4 1.1 copy-done.8
  109.5 203.7 %place.1.placed_ref = bf16[16,4,2,8,4352]{4,3,2,1,0:T(8,128)(2,1)} custom-call(bf16[16,8,4352]{2,1,0:T(8,128)(2,1)} %constant_dynamic-update-slice_fusion.refs_0_, bf16[16,8,4352]{2,1,0:T(8,128)(2,1)} %collective-permute-done.7.refs_1_, bf16[16,8,4352]{2,1,0:T(8,128)(2,1)} %copy-done.5, bf16[16,8,4352]{2,1,0:T(8,128)(2,1)} %copy-done.6, ...), custom_call_target="tpu_custom_call" | custom-call | bytes 14000000 | tf_op jit(solution)/shard_map/place/pallas_call | solution.py:346
  313.2 1.9 collective-permute-start.14
  315.1 2.6 collective-permute-start.15
  317.7 1.0 list.1
  318.8 0.3 collective-permute-done.15.high_swapped_ref
  319.1 10.4 %item.1 = (bf16[512,1024]{1,0:T(8,128)(2,1)S(1)}, bf16[512,1024]{1,0:T(8,128)(2,1)S(1)}, bf16[16,4,2,8,4352]{4,3,2,1,0:T(8,128)(2,1)S(1)}, bf16[4,1024]{1,0:T(4,128)(2,1)S(1)}, f32[1,512]{1,0:T(1,128)S(1)}) custom-call(bf16[8,8,4352]{2,1,0:T(8,128)(2,1)S(1)} %collective-permute-done.8.low_ref, bf16[8,8,4352]{2,1,0:T(8,128)(2,1)S(1)} %collective-permute-done.10.high_ref, ...), custom_call_target="tpu_custom_call" | custom-call | tf_op jit(solution)/shard_map/item/pallas_call | solution.py:378
  329.5 4.4 %all-gather.3.state_ref = bf16[2,4,1024]{2,1,0:T(4,128)(2,1)S(1)} all-gather(bf16[1,4,1024]{2,1,0:T(4,128)(2,1)S(1)} %bitcast.24), channel_id=2, replica_groups={{0,128},{256,384},{1,129},{257,385},{2,130},{258,386},{3,131},{259,387}..., dimensions={0}, use_global_device_ids=true | all-gather | bytes 24576 | tf_op jit(solution)/shard_map/all_gather | solution.py:402
  333.8 1.5 section.3
  335.3 5.6 %all-gather.4.state_ref = bf16[2,4,1024]{2,1,0:T(4,128)(2,1)S(1)} all-gather(bf16[1,4,1024]{2,1,0:T(4,128)(2,1)S(1)} %bitcast.25), channel_id=3, replica_groups={{128,256},{0,384},{129,257},{1,385},{130,258},{2,386},{131,259},{3,387}..., dimensions={0}, use_global_device_ids=true | all-gather | bytes 24576 | tf_op jit(solution)/shard_map/all_gather | solution.py:402
  340.9 1.5 section.4
  342.4 4.4 %all-gather.5.state_ref = bf16[2,4,1024]{2,1,0:T(4,128)(2,1)S(1)} all-gather(bf16[1,4,1024]{2,1,0:T(4,128)(2,1)S(1)} %bitcast.26), channel_id=4, replica_groups={{0,128},{256,384},{1,129},{257,385},{2,130},{258,386},{3,131},{259,387}..., dimensions={0}, use_global_device_ids=true | all-gather | bytes 24576 | tf_op jit(solution)/shard_map/all_gather | solution.py:402
  346.7 2.1 section.5
  (21 shorter events, 0.1 us)
Async XLA Ops:
  0.6 54.7 %copy-start.10 = (bf16[1,8,1024]{2,1,0:T(8,128)(2,1)S(1)}, bf16[1,8,1024]{2,1,0:T(8,128)(2,1)}, u32[]{:S(2)}) copy-start(bf16[1,8,1024]{2,1,0:T(8,128)(2,1)} %param.14) | copy-start | bytes 49156
  0.6 54.7 %copy-start.11 = (bf16[1,8,1024]{2,1,0:T(8,128)(2,1)S(1)}, bf16[1,8,1024]{2,1,0:T(8,128)(2,1)}, u32[]{:S(2)}) copy-start(bf16[1,8,1024]{2,1,0:T(8,128)(2,1)} %param.13) | copy-start | bytes 49156
  0.7 54.7 %copy-start.9 = (bf16[1,8,2048]{2,1,0:T(8,128)(2,1)S(1)}, bf16[1,8,2048]{2,1,0:T(8,128)(2,1)}, u32[]{:S(2)}) copy-start(bf16[1,8,2048]{2,1,0:T(8,128)(2,1)} %param.12) | copy-start | bytes 98308
  2.2 37.4 %collective-permute-start.2 = (bf16[1,8,4352]{2,1,0:T(8,128)(2,1)S(1)}, bf16[1,8,4352]{2,1,0:T(8,128)(2,1)S(1)}, u32[]{:S(2)}, u32[]{:S(2)}) collective-permute-start(bf16[1,8,4352]{2,1,0:T(8,128)(2,1)S(1)} %maximum_bitcast_fusion), channel_id=1, source_target_pairs={{0,64},{8,72},{16,80},{24,88},{32,96},{40,104},{48,112},{56,120},{... | collective-permute-start | bytes 208904 | tf_op jit(solution)/shard_map/ppermute | solution.py:305
  17.9 21.7 %collective-permute-start.1 = (bf16[1,8,4352]{2,1,0:T(8,128)(2,1)S(1)}, bf16[1,8,4352]{2,1,0:T(8,128)(2,1)S(1)}, u32[]{:S(2)}, u32[]{:S(2)}) collective-permute-start(bf16[1,8,4352]{2,1,0:T(8,128)(2,1)S(1)} %maximum_bitcast_fusion), channel_id=1, source_target_pairs={{0,32},{8,40},{16,48},{24,56},{32,64},{40,72},{48,80},{56,88},{64,... | collective-permute-start | bytes 208904 | tf_op jit(solution)/shard_map/ppermute | solution.py:305
  22.2 17.4 %collective-permute-start = (bf16[1,8,4352]{2,1,0:T(8,128)(2,1)S(1)}, bf16[1,8,4352]{2,1,0:T(8,128)(2,1)S(1)}, u32[]{:S(2)}, u32[]{:S(2)}) collective-permute-start(bf16[1,8,4352]{2,1,0:T(8,128)(2,1)S(1)} %maximum_bitcast_fusion), channel_id=1, source_target_pairs={{0,96},{8,104},{16,112},{24,120},{32,0},{40,8},{48,16},{56,24},{64... | collective-permute-start | bytes 208904 | tf_op jit(solution)/shard_map/ppermute | solution.py:305
  27.7 0.7 copy-start.3
  29.6 27.6 %all-to-all-start = ((s32[128,1,8]{2,1,0:T(1,128)}), s32[128,1,8]{2,1,0:T(1,128)S(1)}, u32[]{:S(2)}, u32[]{:S(2)}) async-start(s32[128,1,8]{2,1,0:T(1,128)} %bitcast.6), calls=%async_computation | async-start | bytes 131072 | tf_op jit(solution)/shard_map/all_to_all | solution.py:318
  39.6 21.7 %collective-permute-start.4 = (bf16[4,8,4352]{2,1,0:T(8,128)(2,1)S(1)}, bf16[4,8,4352]{2,1,0:T(8,128)(2,1)S(1)}, u32[]{:S(2)}, u32[]{:S(2)}) collective-permute-start(bf16[4,8,4352]{2,1,0:T(8,128)(2,1)S(1)} %pad_maximum_fusion), channel_id=1, source_target_pairs={{0,120},{8,0},{16,8},{24,16},{32,24},{40,32},{48,40},{56,48},{64,5... | collective-permute-start | bytes 835592 | tf_op jit(solution)/shard_map/ppermute | solution.py:305
  44.6 16.8 %collective-permute-start.3 = (bf16[4,8,4352]{2,1,0:T(8,128)(2,1)S(1)}, bf16[4,8,4352]{2,1,0:T(8,128)(2,1)S(1)}, u32[]{:S(2)}, u32[]{:S(2)}) collective-permute-start(bf16[4,8,4352]{2,1,0:T(8,128)(2,1)S(1)} %pad_maximum_fusion), channel_id=1, source_target_pairs={{0,8},{8,16},{16,24},{24,32},{32,40},{40,48},{48,56},{56,64},{64,7... | collective-permute-start | bytes 835592 | tf_op jit(solution)/shard_map/ppermute | solution.py:305
  46.5 14.3 %collective-permute-start.6 = (bf16[2,8,4352]{2,1,0:T(8,128)(2,1)S(1)}, bf16[2,8,4352]{2,1,0:T(8,128)(2,1)S(1)}, u32[]{:S(2)}, u32[]{:S(2)}) collective-permute-start(bf16[2,8,4352]{2,1,0:T(8,128)(2,1)S(1)} %get-tuple-element.52), channel_id=1, source_target_pairs={{0,16},{8,24},{16,32},{24,40},{32,48},{40,56},{48,64},{56,72},{64,... | collective-permute-start | bytes 417800 | tf_op jit(solution)/shard_map/ppermute | solution.py:305
  49.5 21.2 %copy-start = (bf16[2048,256]{1,0:T(8,128)(2,1)S(1)}, bf16[2048,256]{1,0:T(8,128)(2,1)}, u32[]{:S(2)}) copy-start(bf16[2048,256]{1,0:T(8,128)(2,1)} %table_ref.1) | copy-start | bytes 3145732
  49.5 11.9 %collective-permute-start.5 = (bf16[2,8,4352]{2,1,0:T(8,128)(2,1)S(1)}, bf16[2,8,4352]{2,1,0:T(8,128)(2,1)S(1)}, u32[]{:S(2)}, u32[]{:S(2)}) collective-permute-start(bf16[2,8,4352]{2,1,0:T(8,128)(2,1)S(1)} %get-tuple-element.53), channel_id=1, source_target_pairs={{0,112},{8,120},{16,0},{24,8},{32,16},{40,24},{48,32},{56,40},{64,... | collective-permute-start | bytes 417800 | tf_op jit(solution)/shard_map/ppermute | solution.py:305
  64.2 27.8 %collective-permute-start.9 = (bf16[16,8,4352]{2,1,0:T(8,128)(2,1)}, bf16[16,8,4352]{2,1,0:T(8,128)(2,1)S(1)}, u32[]{:S(2)}, u32[]{:S(2)}) collective-permute-start(bf16[16,8,4352]{2,1,0:T(8,128)(2,1)} %constant_dynamic-update-slice_fusion.refs_0_), channel_id=1, source_target_pairs={{0,6},{2,0},{4,2},{6,4},{1,7},{3,1},{5,3},{7,5},{8,14},{10,8},{12,... | collective-permute-start | bytes 3342344 | tf_op jit(solution)/shard_map/ppermute | solution.py:305
  68.8 29.1 %collective-permute-start.7 = (bf16[16,8,4352]{2,1,0:T(8,128)(2,1)}, bf16[16,8,4352]{2,1,0:T(8,128)(2,1)}, u32[]{:S(2)}, u32[]{:S(2)}) collective-permute-start(bf16[16,8,4352]{2,1,0:T(8,128)(2,1)} %constant_dynamic-update-slice_fusion.refs_0_), channel_id=1, source_target_pairs={{0,2},{2,4},{4,6},{6,0},{1,3},{3,5},{5,7},{7,1},{8,10},{10,12},{12... | collective-permute-start | bytes 3342344 | tf_op jit(solution)/shard_map/ppermute | solution.py:305
  72.8 244.9 %all-to-all-start.1 = ((bf16[128,8,256]{2,1,0:T(8,128)(2,1)}), bf16[128,8,256]{2,1,0:T(8,128)(2,1)S(1)}, u32[]{:S(2)}, u32[]{:S(2)}) async-start(bf16[128,8,256]{2,1,0:T(8,128)(2,1)} %table.1), calls=%async_computation.1 | async-start | bytes 1048576 | tf_op jit(solution)/shard_map/all_to_all | solution.py:344
  87.8 19.2 %collective-permute-start.11 = (bf16[16,8,4352]{2,1,0:T(8,128)(2,1)}, bf16[16,8,4352]{2,1,0:T(8,128)(2,1)S(1)}, u32[]{:S(2)}, u32[]{:S(2)}) collective-permute-start(bf16[16,8,4352]{2,1,0:T(8,128)(2,1)} %constant_dynamic-update-slice_fusion.refs_0_), channel_id=1, source_target_pairs={{0,1},{1,0},{2,3},{3,2},{4,5},{5,4},{6,7},{7,6},{8,9},{9,8},{10,11... | collective-permute-start | bytes 3342344 | tf_op jit(solution)/shard_map/ppermute | solution.py:305
  92.0 11.0 %copy-start.5 = (bf16[16,8,4352]{2,1,0:T(8,128)(2,1)}, bf16[16,8,4352]{2,1,0:T(8,128)(2,1)S(1)}, u32[]{:S(2)}) copy-start(bf16[16,8,4352]{2,1,0:T(8,128)(2,1)S(1)} %collective-permute-done.9.refs_2_) | copy-start | bytes 3342340
  92.0 15.0 %collective-permute-start.13 = (bf16[16,8,4352]{2,1,0:T(8,128)(2,1)S(1)}, bf16[16,8,4352]{2,1,0:T(8,128)(2,1)S(1)}, u32[]{:S(2)}, u32[]{:S(2)}) collective-permute-start(bf16[16,8,4352]{2,1,0:T(8,128)(2,1)S(1)} %collective-permute-done.9.refs_2_), channel_id=1, source_target_pairs={{0,1},{1,0},{2,3},{3,2},{4,5},{5,4},{6,7},{7,6},{8,9},{9,8},{10,11... | collective-permute-start | bytes 3342344 | tf_op jit(solution)/shard_map/ppermute | solution.py:305
  97.9 9.1 %collective-permute-start.12 = (bf16[16,8,4352]{2,1,0:T(8,128)(2,1)}, bf16[16,8,4352]{2,1,0:T(8,128)(2,1)S(1)}, u32[]{:S(2)}, u32[]{:S(2)}) collective-permute-start(bf16[16,8,4352]{2,1,0:T(8,128)(2,1)} %collective-permute-done.7.refs_1_), channel_id=1, source_target_pairs={{0,1},{1,0},{2,3},{3,2},{4,5},{5,4},{6,7},{7,6},{8,9},{9,8},{10,11... | collective-permute-start | bytes 3342344 | tf_op jit(solution)/shard_map/ppermute | solution.py:305
  99.9 213.3 %collective-permute-start.10 = (bf16[8,8,4352]{2,1,0:T(8,128)(2,1)S(1)}, bf16[8,8,4352]{2,1,0:T(8,128)(2,1)S(1)}, u32[]{:S(2)}, u32[]{:S(2)}) collective-permute-start(bf16[8,8,4352]{2,1,0:T(8,128)(2,1)S(1)} %slice.13), channel_id=1, source_target_pairs={{0,6},{2,0},{4,2},{6,4},{1,7},{3,1},{5,3},{7,5},{8,14},{10,8},{12,... | collective-permute-start | bytes 1671176 | tf_op jit(solution)/shard_map/ppermute | solution.py:305
  103.0 214.8 %copy-start.1 = (bf16[4,1024]{1,0:T(4,128)(2,1)S(1)}, bf16[4,1024]{1,0:T(4,128)(2,1)}, u32[]{:S(2)}) copy-start(bf16[4,1024]{1,0:T(4,128)(2,1)} %state_ref.1) | copy-start | bytes 24580
  103.0 214.8 %copy-start.2 = (f32[1,1024]{1,0:T(1,128)S(1)}, f32[1,1024]{1,0:T(1,128)}, u32[]{:S(2)}) copy-start(f32[1,1024]{1,0:T(1,128)} %gain_ref.1) | copy-start | bytes 12292
  103.0 214.8 %copy-start.4 = (s32[1,4]{1,0:T(1,128)S(1)}, s32[1,4]{1,0:T(1,128)}, u32[]{:S(2)}) copy-start(s32[1,4]{1,0:T(1,128)} %count_ref.1) | copy-start | bytes 52
  103.0 210.2 %collective-permute-start.8 = (bf16[8,8,4352]{2,1,0:T(8,128)(2,1)S(1)}, bf16[8,8,4352]{2,1,0:T(8,128)(2,1)S(1)}, u32[]{:S(2)}, u32[]{:S(2)}) collective-permute-start(bf16[8,8,4352]{2,1,0:T(8,128)(2,1)S(1)} %slice.12), channel_id=1, source_target_pairs={{0,2},{2,4},{4,6},{6,0},{1,3},{3,5},{5,7},{7,1},{8,10},{10,12},{12... | collective-permute-start | bytes 1671176 | tf_op jit(solution)/shard_map/ppermute | solution.py:305
  107.0 1.0 copy-start.6
  107.0 1.4 copy-start.7
  108.4 1.1 copy-start.8
  313.2 5.6 %collective-permute-start.14 = (bf16[8,8,4352]{2,1,0:T(8,128)(2,1)S(1)}, bf16[8,8,4352]{2,1,0:T(8,128)(2,1)S(1)}, u32[]{:S(2)}, u32[]{:S(2)}) collective-permute-start(bf16[8,8,4352]{2,1,0:T(8,128)(2,1)S(1)} %collective-permute-done.8.low_ref), channel_id=1, source_target_pairs={{0,1},{1,0},{2,3},{3,2},{4,5},{5,4},{6,7},{7,6},{8,9},{9,8},{10,11... | collective-permute-start | bytes 1671176 | tf_op jit(solution)/shard_map/ppermute | solution.py:305
  315.1 4.0 %collective-permute-start.15 = (bf16[8,8,4352]{2,1,0:T(8,128)(2,1)S(1)}, bf16[8,8,4352]{2,1,0:T(8,128)(2,1)S(1)}, u32[]{:S(2)}, u32[]{:S(2)}) collective-permute-start(bf16[8,8,4352]{2,1,0:T(8,128)(2,1)S(1)} %collective-permute-done.10.high_ref), channel_id=1, source_target_pairs={{0,1},{1,0},{2,3},{3,2},{4,5},{5,4},{6,7},{7,6},{8,9},{9,8},{10,11... | collective-permute-start | bytes 1671176 | tf_op jit(solution)/shard_map/ppermute | solution.py:305

commit v7 on v6

--- a/solution.py
+++ b/solution.py
@@ -160,12 +160,14 @@
 def place_kernel(*refs):
     *pieces, weight_ref, sems = refs
     ys = weight_ref.shape[1]
-    kinds = [(piece, 0, (0, ys - 1, 1)[i % 3], i // 3) for i, piece in enumerate(pieces)]
+    parts = ((ys - 1, 0), (1, 0), (ys - 1, 1), (1, 1), (0, 1))
+    kinds = [(piece, 0, *part) for piece, part in zip(pieces, parts)]
     place(kinds, weight_ref, sems)
     wait_placed(kinds, weight_ref, sems)
 
 
 def item_kernel(
+    column_ref,
     low_ref,
     high_ref,
     low_swapped_ref,
@@ -188,6 +190,7 @@
     emb = listed_ref.shape[1]
     half = zs // 2
     kinds = (
+        (column_ref, 0, 0, 0),
         (low_ref, 0, 2, 0),
         (high_ref, half, 2, 0),
         (low_swapped_ref, 0, 2, 1),
@@ -201,7 +204,7 @@
     ):
         mine = []
         for number, (from_y, from_core) in enumerate(
-            (from_y, from_core) for from_y in (0, 1, ys - 1) for from_core in range(cores)
+            ((ys - 1, 0), (1, 0), (ys - 1, 1), (1, 1), (0, 1))
         ):
             at = (
                 slice(None),
@@ -295,7 +298,7 @@
     items = item_ids.shape[2]
     shard_rows, emb = item_table.shape
     depth = w_ask.shape[1]
-    small, big, wide = (pltpu.CompilerParams(vmem_limit_bytes=size << 20) for size in (12, 34, 54))
+    small, big, wide = (pltpu.CompilerParams(vmem_limit_bytes=size << 20) for size in (12, 34, 44))
 
     own = jnp.concatenate(
         [w_pair[0], w_ask[0], w_back[0], w_lift[0].reshape(depth, emb)], axis=1
@@ -331,8 +334,8 @@
     half = zs // 2
     below, above = moved(column, "y", 1), moved(column, "y", -1)
     across = (moved(below[:half], "y", 1), moved(above[half:], "y", -1))
-    early = [column, below, above]
-    early = early + [moved(piece, "core", 1) for piece in early]
+    early = [below, above]
+    early = early + [moved(piece, "core", 1) for piece in (below, above, column)]
     found = pl.pallas_call(
         table_kernel,
         out_shape=jax.ShapeDtypeStruct((shards, CAP, emb), BF16),
@@ -354,7 +357,7 @@
         name="place",
     )(*early)
     across, weights = lax.optimization_barrier((across, weights))
-    late = [*across, *(moved(piece, "core", 1) for piece in across)]
+    late = [column, *across, *(moved(piece, "core", 1) for piece in across)]
 
     smem = pl.BlockSpec(memory_space=pltpu.SMEM)
     listed, entering, gains, length_row = pl.pallas_call(
@@ -389,7 +392,7 @@
         out_specs=(vmem(),) * 5,
         scratch_shapes=[
             pltpu.SemaphoreType.DMA((len(late),)),
-            pltpu.SemaphoreType.DMA((3, 6)),
+            pltpu.SemaphoreType.DMA((3, 5)),
         ],
         compiler_params=big,
         name="item",

time: 351 us -> 159 us (0.45)
  Pallas kernels: 224 us -> 21.9 us
  waiting for transfers between devices: 10.7 us -> 24.4 us
  local copies, waits for them, and re-layouts: 9.72 us -> 6.19 us
    pallas_call x1, Pallas kernels: 204 us -> 2.51 us  [per_device(): pl.pallas_call(place_kernel, out_shape=jax.ShapeDtypeStruct((zs, ys, core...]
    ppermute x16, waiting for transfers between devices: 10.7 us -> 24.4 us  [moved(): lax.ppermute(block, axis, [(i, (i + distance) % size) for i in range(size)])]
    unnamed x30 -> x22, local copies, waits for them, and re-layouts: 7.22 us -> 4.73 us
  transfers between devices with their start and end apart: 18 -> 18, of which waited for: 5 -> 7; matrix products, arithmetic and copies ran while one was open for 1% -> 2% of each run, Pallas kernels for 60% -> 4%
where the time goes in v7:
time: 159 us; the launch traced here: 157 us
  starting transfers between devices  88 us (55%)
  waiting for transfers between devices  24.4 us (15%)
  Pallas kernels  21.9 us (14%)
  blocking collectives  14.3 us (9%)
  local copies, waits for them, and re-layouts  6.19 us (4%)
    ppermute x16, starting transfers between devices, moved(): lax.ppermute(block, axis, [(i, (i + distance) % size) for i in range(size)])  63.2 us
    ppermute x16, waiting for transfers between devices, moved(): lax.ppermute(block, axis, [(i, (i + distance) % size) for i in range(size)])  24.4 us
    all_to_all x1, starting transfers between devices, per_device(): lax.all_to_all(found, SHARD, split_axis=0, concat_axis=0, tiled=True)  15 us
    all_gather x3, blocking collectives, per_device(): lax.all_gather(leaving, 'segment', axis=0, axis_index_groups=(even, odd)[...  14.3 us
    pallas_call x1, Pallas kernels, per_device(): pl.pallas_call(item_kernel, out_shape=(jax.ShapeDtypeStruct((users * item...  9.9 us
    all_to_all x1, starting transfers between devices, per_device(): lax.all_to_all(request.reshape(shards, 1, CAP), SHARD, split_axis=0, conc...  9.89 us
    pallas_call x3, Pallas kernels, per_device(): pl.pallas_call(section_kernel, out_shape=section_shape, in_specs=[vmem()]...  5.02 us
    unnamed x22, local copies, waits for them, and re-layouts  4.73 us
  transfers between devices with their start and end apart: 18, of which 7 were waited for; matrix products, arithmetic and copies ran while one was open for 2% of the time, Pallas kernels for 4%

profile of v7, /device:TPU:6, one launch (start us, length us, event | category | flops | bytes accessed | tf_op | source)
XLA Modules:
  0.0 157.3 jit_solution(13691223374442026154)
XLA Ops:
  0.6 0.0 copy-start.6
  0.6 0.0 copy-start.7
  0.7 0.0 copy-start.5
  0.7 0.7 reshape_squeeze.3
  1.4 0.8 maximum_bitcast_fusion
  2.2 15.7 %collective-permute-start.2 = (bf16[1,8,4352]{2,1,0:T(8,128)(2,1)S(1)}, bf16[1,8,4352]{2,1,0:T(8,128)(2,1)S(1)}, u32[]{:S(2)}, u32[]{:S(2)}) collective-permute-start(bf16[1,8,4352]{2,1,0:T(8,128)(2,1)S(1)} %maximum_bitcast_fusion), channel_id=1, source_target_pairs={{0,64},{8,72},{16,80},{24,88},{32,96},{40,104},{48,112},{56,120},{... | collective-permute-start | bytes 208904 | tf_op jit(solution)/shard_map/ppermute | solution.py:308
  17.9 4.3 %collective-permute-start.1 = (bf16[1,8,4352]{2,1,0:T(8,128)(2,1)S(1)}, bf16[1,8,4352]{2,1,0:T(8,128)(2,1)S(1)}, u32[]{:S(2)}, u32[]{:S(2)}) collective-permute-start(bf16[1,8,4352]{2,1,0:T(8,128)(2,1)S(1)} %maximum_bitcast_fusion), channel_id=1, source_target_pairs={{0,32},{8,40},{16,48},{24,56},{32,64},{40,72},{48,80},{56,88},{64,... | collective-permute-start | bytes 208904 | tf_op jit(solution)/shard_map/ppermute | solution.py:308
  22.2 5.5 %collective-permute-start = (bf16[1,8,4352]{2,1,0:T(8,128)(2,1)S(1)}, bf16[1,8,4352]{2,1,0:T(8,128)(2,1)S(1)}, u32[]{:S(2)}, u32[]{:S(2)}) collective-permute-start(bf16[1,8,4352]{2,1,0:T(8,128)(2,1)S(1)} %maximum_bitcast_fusion), channel_id=1, source_target_pairs={{0,96},{8,104},{16,112},{24,120},{32,0},{40,8},{48,16},{56,24},{64... | collective-permute-start | bytes 208904 | tf_op jit(solution)/shard_map/ppermute | solution.py:308
  27.7 0.0 copy-start.3
  27.7 0.7 copy-done.3
  28.3 1.3 request.1
  29.6 9.9 %all-to-all-start = ((s32[128,1,8]{2,1,0:T(1,128)}), s32[128,1,8]{2,1,0:T(1,128)S(1)}, u32[]{:S(2)}, u32[]{:S(2)}) async-start(s32[128,1,8]{2,1,0:T(1,128)} %bitcast.6), calls=%async_computation | async-start | bytes 131072 | tf_op jit(solution)/shard_map/all_to_all | solution.py:321
  39.5 0.0 collective-permute-done.2
  39.6 0.0 collective-permute-done.1
  39.6 5.0 %collective-permute-start.4 = (bf16[4,8,4352]{2,1,0:T(8,128)(2,1)S(1)}, bf16[4,8,4352]{2,1,0:T(8,128)(2,1)S(1)}, u32[]{:S(2)}, u32[]{:S(2)}) collective-permute-start(bf16[4,8,4352]{2,1,0:T(8,128)(2,1)S(1)} %pad_maximum_fusion), channel_id=1, source_target_pairs={{0,120},{8,0},{16,8},{24,16},{32,24},{40,32},{48,40},{56,48},{64,5... | collective-permute-start | bytes 835592 | tf_op jit(solution)/shard_map/ppermute | solution.py:308
  44.6 1.9 %collective-permute-start.3 = (bf16[4,8,4352]{2,1,0:T(8,128)(2,1)S(1)}, bf16[4,8,4352]{2,1,0:T(8,128)(2,1)S(1)}, u32[]{:S(2)}, u32[]{:S(2)}) collective-permute-start(bf16[4,8,4352]{2,1,0:T(8,128)(2,1)S(1)} %pad_maximum_fusion), channel_id=1, source_target_pairs={{0,8},{8,16},{16,24},{24,32},{32,40},{40,48},{48,56},{56,64},{64,7... | collective-permute-start | bytes 835592 | tf_op jit(solution)/shard_map/ppermute | solution.py:308
  46.5 2.9 %collective-permute-start.6 = (bf16[2,8,4352]{2,1,0:T(8,128)(2,1)S(1)}, bf16[2,8,4352]{2,1,0:T(8,128)(2,1)S(1)}, u32[]{:S(2)}, u32[]{:S(2)}) collective-permute-start(bf16[2,8,4352]{2,1,0:T(8,128)(2,1)S(1)} %get-tuple-element.52), channel_id=1, source_target_pairs={{0,16},{8,24},{16,32},{24,40},{32,48},{40,56},{48,64},{56,72},{64,... | collective-permute-start | bytes 417800 | tf_op jit(solution)/shard_map/ppermute | solution.py:308
  49.5 0.0 copy-start
  49.5 5.2 %collective-permute-start.5 = (bf16[2,8,4352]{2,1,0:T(8,128)(2,1)S(1)}, bf16[2,8,4352]{2,1,0:T(8,128)(2,1)S(1)}, u32[]{:S(2)}, u32[]{:S(2)}) collective-permute-start(bf16[2,8,4352]{2,1,0:T(8,128)(2,1)S(1)} %get-tuple-element.53), channel_id=1, source_target_pairs={{0,112},{8,120},{16,0},{24,8},{32,16},{40,24},{48,32},{56,40},{64,... | collective-permute-start | bytes 417800 | tf_op jit(solution)/shard_map/ppermute | solution.py:308
  54.7 0.6 constant_dynamic-update-slice_fusion.7
  55.3 0.6 constant_dynamic-update-slice_fusion.6
  55.9 0.6 constant_dynamic-update-slice_fusion.5
  56.6 0.6 constant_dynamic-update-slice_fusion.4
  57.2 0.0 all-to-all-done
  57.2 3.6 %collective-permute-done.6 = bf16[2,8,4352]{2,1,0:T(8,128)(2,1)S(1)} collective-permute-done((bf16[2,8,4352]{2,1,0:T(8,128)(2,1)S(1)}, bf16[2,8,4352]{2,1,0:T(8,128)(2,1)S(1)}, u32[]{:S(2)}, u32[]{:S(2)}) %collective-permute-start.6) | collective-permute-done | bytes 139296 | tf_op jit(solution)/shard_map/ppermute | solution.py:308
  60.8 0.5 collective-permute-done.5
  61.4 0.0 collective-permute-done.4
  61.4 0.0 collective-permute-done.3
  61.4 0.7 constant_dynamic-update-slice_fusion.3
  62.1 0.7 constant_dynamic-update-slice_fusion.2
  62.8 0.7 constant_dynamic-update-slice_fusion.1
  63.5 0.7 constant_dynamic-update-slice_fusion.column_ref
  64.1 4.6 %collective-permute-start.9 = (bf16[16,8,4352]{2,1,0:T(8,128)(2,1)}, bf16[16,8,4352]{2,1,0:T(8,128)(2,1)S(1)}, u32[]{:S(2)}, u32[]{:S(2)}) collective-permute-start(bf16[16,8,4352]{2,1,0:T(8,128)(2,1)} %constant_dynamic-update-slice_fusion.column_ref), channel_id=1, source_target_pairs={{0,6},{2,0},{4,2},{6,4},{1,7},{3,1},{5,3},{7,5},{8,14},{10,8},{12,... | collective-permute-start | bytes 3342344 | tf_op jit(solution)/shard_map/ppermute | solution.py:308
  68.8 1.9 %collective-permute-start.7 = (bf16[16,8,4352]{2,1,0:T(8,128)(2,1)}, bf16[16,8,4352]{2,1,0:T(8,128)(2,1)S(1)}, u32[]{:S(2)}, u32[]{:S(2)}) collective-permute-start(bf16[16,8,4352]{2,1,0:T(8,128)(2,1)} %constant_dynamic-update-slice_fusion.column_ref), channel_id=1, source_target_pairs={{0,2},{2,4},{4,6},{6,0},{1,3},{3,5},{5,7},{7,1},{8,10},{10,12},{12... | collective-permute-start | bytes 3342344 | tf_op jit(solution)/shard_map/ppermute | solution.py:308
  70.7 2.1 %table.1 = bf16[128,8,256]{2,1,0:T(8,128)(2,1)} custom-call(s32[128,8]{1,0:T(8,128)S(1)} %bitcast.23, bf16[2048,256]{1,0:T(8,128)(2,1)S(1)} %copy-done), custom_call_target="tpu_custom_call" | custom-call | tf_op jit(solution)/shard_map/table/pallas_call | solution.py:339
  72.8 15.0 %all-to-all-start.1 = ((bf16[128,8,256]{2,1,0:T(8,128)(2,1)}), bf16[128,8,256]{2,1,0:T(8,128)(2,1)S(1)}, u32[]{:S(2)}, u32[]{:S(2)}) async-start(bf16[128,8,256]{2,1,0:T(8,128)(2,1)} %table.1), calls=%async_computation.1 | async-start | bytes 1048576 | tf_op jit(solution)/shard_map/all_to_all | solution.py:347
  87.8 1.9 %collective-permute-start.13 = (bf16[16,8,4352]{2,1,0:T(8,128)(2,1)}, bf16[16,8,4352]{2,1,0:T(8,128)(2,1)S(1)}, u32[]{:S(2)}, u32[]{:S(2)}) collective-permute-start(bf16[16,8,4352]{2,1,0:T(8,128)(2,1)} %constant_dynamic-update-slice_fusion.column_ref), channel_id=1, source_target_pairs={{0,1},{1,0},{2,3},{3,2},{4,5},{5,4},{6,7},{7,6},{8,9},{9,8},{10,11... | collective-permute-start | bytes 3342344 | tf_op jit(solution)/shard_map/ppermute | solution.py:308
  89.7 2.3 %collective-permute-done.9.refs_1_ = bf16[16,8,4352]{2,1,0:T(8,128)(2,1)S(1)} collective-permute-done((bf16[16,8,4352]{2,1,0:T(8,128)(2,1)}, bf16[16,8,4352]{2,1,0:T(8,128)(2,1)S(1)}, u32[]{:S(2)}, u32[]{:S(2)}) %collective-permute-start.9) | collective-permute-done | bytes 1114144 | tf_op jit(solution)/shard_map/ppermute | solution.py:308
  92.0 1.9 %collective-permute-start.12 = (bf16[16,8,4352]{2,1,0:T(8,128)(2,1)S(1)}, bf16[16,8,4352]{2,1,0:T(8,128)(2,1)S(1)}, u32[]{:S(2)}, u32[]{:S(2)}) collective-permute-start(bf16[16,8,4352]{2,1,0:T(8,128)(2,1)S(1)} %collective-permute-done.9.refs_1_), channel_id=1, source_target_pairs={{0,1},{1,0},{2,3},{3,2},{4,5},{5,4},{6,7},{7,6},{8,9},{9,8},{10,11... | collective-permute-start | bytes 3342344 | tf_op jit(solution)/shard_map/ppermute | solution.py:308
  93.9 3.9 %collective-permute-done.7.refs_0_ = bf16[16,8,4352]{2,1,0:T(8,128)(2,1)S(1)} collective-permute-done((bf16[16,8,4352]{2,1,0:T(8,128)(2,1)}, bf16[16,8,4352]{2,1,0:T(8,128)(2,1)S(1)}, u32[]{:S(2)}, u32[]{:S(2)}) %collective-permute-start.7) | collective-permute-done | bytes 1114144 | tf_op jit(solution)/shard_map/ppermute | solution.py:308
  97.8 1.9 %collective-permute-start.11 = (bf16[16,8,4352]{2,1,0:T(8,128)(2,1)S(1)}, bf16[16,8,4352]{2,1,0:T(8,128)(2,1)S(1)}, u32[]{:S(2)}, u32[]{:S(2)}) collective-permute-start(bf16[16,8,4352]{2,1,0:T(8,128)(2,1)S(1)} %collective-permute-done.7.refs_0_), channel_id=1, source_target_pairs={{0,1},{1,0},{2,3},{3,2},{4,5},{5,4},{6,7},{7,6},{8,9},{9,8},{10,11... | collective-permute-start | bytes 3342344 | tf_op jit(solution)/shard_map/ppermute | solution.py:308
  99.7 2.1 %collective-permute-start.10 = (bf16[8,8,4352]{2,1,0:T(8,128)(2,1)S(1)}, bf16[8,8,4352]{2,1,0:T(8,128)(2,1)S(1)}, u32[]{:S(2)}, u32[]{:S(2)}) collective-permute-start(bf16[8,8,4352]{2,1,0:T(8,128)(2,1)S(1)} %slice.13), channel_id=1, source_target_pairs={{0,6},{2,0},{4,2},{6,4},{1,7},{3,1},{5,3},{7,5},{8,14},{10,8},{12,... | collective-permute-start | bytes 1671176 | tf_op jit(solution)/shard_map/ppermute | solution.py:308
  101.9 0.0 copy-start.1
  101.9 0.0 copy-start.2
  101.9 0.0 copy-start.4
  101.9 3.9 %collective-permute-start.8 = (bf16[8,8,4352]{2,1,0:T(8,128)(2,1)S(1)}, bf16[8,8,4352]{2,1,0:T(8,128)(2,1)}, u32[]{:S(2)}, u32[]{:S(2)}) collective-permute-start(bf16[8,8,4352]{2,1,0:T(8,128)(2,1)S(1)} %slice.12), channel_id=1, source_target_pairs={{0,2},{2,4},{4,6},{6,0},{1,3},{3,5},{5,7},{7,1},{8,10},{10,12},{12... | collective-permute-start | bytes 1671176 | tf_op jit(solution)/shard_map/ppermute | solution.py:308
  105.8 0.0 collective-permute-done.13.refs_4_
  105.8 0.0 collective-permute-done.12.refs_3_
  105.9 2.5 %place.1.placed_ref = bf16[16,4,2,8,4352]{4,3,2,1,0:T(8,128)(2,1)} custom-call(bf16[16,8,4352]{2,1,0:T(8,128)(2,1)S(1)} %collective-permute-done.7.refs_0_, bf16[16,8,4352]{2,1,0:T(8,128)(2,1)S(1)} %collective-permute-done.9.refs_1_, bf16[16,8,4352]{2,1,0:T(8,128)(2,1)S(1)} %collective-permute-done.11.refs_2_, ...), custom_call_target="tpu_custom_call" | custom-call | bytes 14000000 | tf_op jit(solution)/shard_map/place/pallas_call | solution.py:349
  108.4 10.6 %collective-permute-done.10.high_ref = bf16[8,8,4352]{2,1,0:T(8,128)(2,1)S(1)} collective-permute-done((bf16[8,8,4352]{2,1,0:T(8,128)(2,1)S(1)}, bf16[8,8,4352]{2,1,0:T(8,128)(2,1)S(1)}, u32[]{:S(2)}, u32[]{:S(2)}) %collective-permute-start.10) | collective-permute-done | bytes 557088 | tf_op jit(solution)/shard_map/ppermute | solution.py:308
  118.9 3.2 %collective-permute-done.8.low_ref = bf16[8,8,4352]{2,1,0:T(8,128)(2,1)} collective-permute-done((bf16[8,8,4352]{2,1,0:T(8,128)(2,1)S(1)}, bf16[8,8,4352]{2,1,0:T(8,128)(2,1)}, u32[]{:S(2)}, u32[]{:S(2)}) %collective-permute-start.8) | collective-permute-done | bytes 557088 | tf_op jit(solution)/shard_map/ppermute | solution.py:308
  122.2 1.9 %collective-permute-start.14 = (bf16[8,8,4352]{2,1,0:T(8,128)(2,1)}, bf16[8,8,4352]{2,1,0:T(8,128)(2,1)S(1)}, u32[]{:S(2)}, u32[]{:S(2)}) collective-permute-start(bf16[8,8,4352]{2,1,0:T(8,128)(2,1)} %collective-permute-done.8.low_ref), channel_id=1, source_target_pairs={{0,1},{1,0},{2,3},{3,2},{4,5},{5,4},{6,7},{7,6},{8,9},{9,8},{10,11... | collective-permute-start | bytes 1671176 | tf_op jit(solution)/shard_map/ppermute | solution.py:308
  124.1 2.6 %collective-permute-start.15 = (bf16[8,8,4352]{2,1,0:T(8,128)(2,1)S(1)}, bf16[8,8,4352]{2,1,0:T(8,128)(2,1)S(1)}, u32[]{:S(2)}, u32[]{:S(2)}) collective-permute-start(bf16[8,8,4352]{2,1,0:T(8,128)(2,1)S(1)} %collective-permute-done.10.high_ref), channel_id=1, source_target_pairs={{0,1},{1,0},{2,3},{3,2},{4,5},{5,4},{6,7},{7,6},{8,9},{9,8},{10,11... | collective-permute-start | bytes 1671176 | tf_op jit(solution)/shard_map/ppermute | solution.py:308
  126.7 0.0 all-to-all-done.1
  126.7 1.0 list.1
  127.8 0.0 collective-permute-done.14.low_swapped_ref
  127.8 0.3 collective-permute-done.15.high_swapped_ref
  128.1 9.9 %item.1 = (bf16[512,1024]{1,0:T(8,128)(2,1)S(1)}, bf16[512,1024]{1,0:T(8,128)(2,1)S(1)}, bf16[16,4,2,8,4352]{4,3,2,1,0:T(8,128)(2,1)S(1)}, bf16[4,1024]{1,0:T(4,128)(2,1)S(1)}, f32[1,512]{1,0:T(1,128)S(1)}) custom-call(bf16[16,8,4352]{2,1,0:T(8,128)(2,1)} %constant_dynamic-update-slice_fusion.column_ref, bf16[8,8,4352]{2,1,0:T(8,128)(2,1)} %collective-permute-done.8.low_ref, ...), custom_call_target="tpu_custom_call" | custom-call | tf_op jit(solution)/shard_map/item/pallas_call | solution.py:381
  138.0 4.4 %all-gather.3.state_ref = bf16[2,4,1024]{2,1,0:T(4,128)(2,1)S(1)} all-gather(bf16[1,4,1024]{2,1,0:T(4,128)(2,1)S(1)} %bitcast.24), channel_id=2, replica_groups={{0,128},{256,384},{1,129},{257,385},{2,130},{258,386},{3,131},{259,387}..., dimensions={0}, use_global_device_ids=true | all-gather | bytes 24576 | tf_op jit(solution)/shard_map/all_gather | solution.py:405
  142.4 1.5 section.3
  143.8 5.6 %all-gather.4.state_ref = bf16[2,4,1024]{2,1,0:T(4,128)(2,1)S(1)} all-gather(bf16[1,4,1024]{2,1,0:T(4,128)(2,1)S(1)} %bitcast.25), channel_id=3, replica_groups={{128,256},{0,384},{129,257},{1,385},{130,258},{2,386},{131,259},{3,387}..., dimensions={0}, use_global_device_ids=true | all-gather | bytes 24576 | tf_op jit(solution)/shard_map/all_gather | solution.py:405
  149.4 1.5 section.4
  150.9 4.4 %all-gather.5.state_ref = bf16[2,4,1024]{2,1,0:T(4,128)(2,1)S(1)} all-gather(bf16[1,4,1024]{2,1,0:T(4,128)(2,1)S(1)} %bitcast.26), channel_id=4, replica_groups={{0,128},{256,384},{1,129},{257,385},{2,130},{258,386},{3,131},{259,387}..., dimensions={0}, use_global_device_ids=true | all-gather | bytes 24576 | tf_op jit(solution)/shard_map/all_gather | solution.py:405
  155.2 2.1 %section.5 = (bf16[4,1024]{1,0:T(4,128)(2,1)}, f32[1,512]{1,0:T(1,128)}) custom-call(bf16[2,4,1024]{2,1,0:T(4,128)(2,1)S(1)} %all-gather.5.state_ref, bf16[512,1024]{1,0:T(8,128)(2,1)S(1)} %get-tuple-element.42.key_ref, bf16[512,1024]{1,0:T(8,128)(2,1)S(1)} %get-tuple-element.43.value_ref, bf16[1024,4352]{1,0:T(8,128)(2,1)S(1)} %bitcast.21, ...), custom_call_target="tpu_custom_call" | custom-call | tf_op jit(solution)/shard_map/section/pallas_call | solution.py:409
  (13 shorter events, 0.2 us)
Async XLA Ops:
  0.6 54.7 %copy-start.6 = (bf16[1,8,1024]{2,1,0:T(8,128)(2,1)S(1)}, bf16[1,8,1024]{2,1,0:T(8,128)(2,1)}, u32[]{:S(2)}) copy-start(bf16[1,8,1024]{2,1,0:T(8,128)(2,1)} %param.14) | copy-start | bytes 49156
  0.6 54.7 %copy-start.7 = (bf16[1,8,1024]{2,1,0:T(8,128)(2,1)S(1)}, bf16[1,8,1024]{2,1,0:T(8,128)(2,1)}, u32[]{:S(2)}) copy-start(bf16[1,8,1024]{2,1,0:T(8,128)(2,1)} %param.13) | copy-start | bytes 49156
  0.7 54.6 %copy-start.5 = (bf16[1,8,2048]{2,1,0:T(8,128)(2,1)S(1)}, bf16[1,8,2048]{2,1,0:T(8,128)(2,1)}, u32[]{:S(2)}) copy-start(bf16[1,8,2048]{2,1,0:T(8,128)(2,1)} %param.12) | copy-start | bytes 98308
  2.2 37.4 %collective-permute-start.2 = (bf16[1,8,4352]{2,1,0:T(8,128)(2,1)S(1)}, bf16[1,8,4352]{2,1,0:T(8,128)(2,1)S(1)}, u32[]{:S(2)}, u32[]{:S(2)}) collective-permute-start(bf16[1,8,4352]{2,1,0:T(8,128)(2,1)S(1)} %maximum_bitcast_fusion), channel_id=1, source_target_pairs={{0,64},{8,72},{16,80},{24,88},{32,96},{40,104},{48,112},{56,120},{... | collective-permute-start | bytes 208904 | tf_op jit(solution)/shard_map/ppermute | solution.py:308
  17.9 21.7 %collective-permute-start.1 = (bf16[1,8,4352]{2,1,0:T(8,128)(2,1)S(1)}, bf16[1,8,4352]{2,1,0:T(8,128)(2,1)S(1)}, u32[]{:S(2)}, u32[]{:S(2)}) collective-permute-start(bf16[1,8,4352]{2,1,0:T(8,128)(2,1)S(1)} %maximum_bitcast_fusion), channel_id=1, source_target_pairs={{0,32},{8,40},{16,48},{24,56},{32,64},{40,72},{48,80},{56,88},{64,... | collective-permute-start | bytes 208904 | tf_op jit(solution)/shard_map/ppermute | solution.py:308
  22.2 17.4 %collective-permute-start = (bf16[1,8,4352]{2,1,0:T(8,128)(2,1)S(1)}, bf16[1,8,4352]{2,1,0:T(8,128)(2,1)S(1)}, u32[]{:S(2)}, u32[]{:S(2)}) collective-permute-start(bf16[1,8,4352]{2,1,0:T(8,128)(2,1)S(1)} %maximum_bitcast_fusion), channel_id=1, source_target_pairs={{0,96},{8,104},{16,112},{24,120},{32,0},{40,8},{48,16},{56,24},{64... | collective-permute-start | bytes 208904 | tf_op jit(solution)/shard_map/ppermute | solution.py:308
  27.7 0.7 copy-start.3
  29.6 27.5 %all-to-all-start = ((s32[128,1,8]{2,1,0:T(1,128)}), s32[128,1,8]{2,1,0:T(1,128)S(1)}, u32[]{:S(2)}, u32[]{:S(2)}) async-start(s32[128,1,8]{2,1,0:T(1,128)} %bitcast.6), calls=%async_computation | async-start | bytes 131072 | tf_op jit(solution)/shard_map/all_to_all | solution.py:321
  39.6 21.7 %collective-permute-start.4 = (bf16[4,8,4352]{2,1,0:T(8,128)(2,1)S(1)}, bf16[4,8,4352]{2,1,0:T(8,128)(2,1)S(1)}, u32[]{:S(2)}, u32[]{:S(2)}) collective-permute-start(bf16[4,8,4352]{2,1,0:T(8,128)(2,1)S(1)} %pad_maximum_fusion), channel_id=1, source_target_pairs={{0,120},{8,0},{16,8},{24,16},{32,24},{40,32},{48,40},{56,48},{64,5... | collective-permute-start | bytes 835592 | tf_op jit(solution)/shard_map/ppermute | solution.py:308
  44.6 16.8 %collective-permute-start.3 = (bf16[4,8,4352]{2,1,0:T(8,128)(2,1)S(1)}, bf16[4,8,4352]{2,1,0:T(8,128)(2,1)S(1)}, u32[]{:S(2)}, u32[]{:S(2)}) collective-permute-start(bf16[4,8,4352]{2,1,0:T(8,128)(2,1)S(1)} %pad_maximum_fusion), channel_id=1, source_target_pairs={{0,8},{8,16},{16,24},{24,32},{32,40},{40,48},{48,56},{56,64},{64,7... | collective-permute-start | bytes 835592 | tf_op jit(solution)/shard_map/ppermute | solution.py:308
  46.5 14.3 %collective-permute-start.6 = (bf16[2,8,4352]{2,1,0:T(8,128)(2,1)S(1)}, bf16[2,8,4352]{2,1,0:T(8,128)(2,1)S(1)}, u32[]{:S(2)}, u32[]{:S(2)}) collective-permute-start(bf16[2,8,4352]{2,1,0:T(8,128)(2,1)S(1)} %get-tuple-element.52), channel_id=1, source_target_pairs={{0,16},{8,24},{16,32},{24,40},{32,48},{40,56},{48,64},{56,72},{64,... | collective-permute-start | bytes 417800 | tf_op jit(solution)/shard_map/ppermute | solution.py:308
  49.5 21.2 %copy-start = (bf16[2048,256]{1,0:T(8,128)(2,1)S(1)}, bf16[2048,256]{1,0:T(8,128)(2,1)}, u32[]{:S(2)}) copy-start(bf16[2048,256]{1,0:T(8,128)(2,1)} %table_ref.1) | copy-start | bytes 3145732
  49.5 11.9 %collective-permute-start.5 = (bf16[2,8,4352]{2,1,0:T(8,128)(2,1)S(1)}, bf16[2,8,4352]{2,1,0:T(8,128)(2,1)S(1)}, u32[]{:S(2)}, u32[]{:S(2)}) collective-permute-start(bf16[2,8,4352]{2,1,0:T(8,128)(2,1)S(1)} %get-tuple-element.53), channel_id=1, source_target_pairs={{0,112},{8,120},{16,0},{24,8},{32,16},{40,24},{48,32},{56,40},{64,... | collective-permute-start | bytes 417800 | tf_op jit(solution)/shard_map/ppermute | solution.py:308
  64.1 27.8 %collective-permute-start.9 = (bf16[16,8,4352]{2,1,0:T(8,128)(2,1)}, bf16[16,8,4352]{2,1,0:T(8,128)(2,1)S(1)}, u32[]{:S(2)}, u32[]{:S(2)}) collective-permute-start(bf16[16,8,4352]{2,1,0:T(8,128)(2,1)} %constant_dynamic-update-slice_fusion.column_ref), channel_id=1, source_target_pairs={{0,6},{2,0},{4,2},{6,4},{1,7},{3,1},{5,3},{7,5},{8,14},{10,8},{12,... | collective-permute-start | bytes 3342344 | tf_op jit(solution)/shard_map/ppermute | solution.py:308
  68.8 29.0 %collective-permute-start.7 = (bf16[16,8,4352]{2,1,0:T(8,128)(2,1)}, bf16[16,8,4352]{2,1,0:T(8,128)(2,1)S(1)}, u32[]{:S(2)}, u32[]{:S(2)}) collective-permute-start(bf16[16,8,4352]{2,1,0:T(8,128)(2,1)} %constant_dynamic-update-slice_fusion.column_ref), channel_id=1, source_target_pairs={{0,2},{2,4},{4,6},{6,0},{1,3},{3,5},{5,7},{7,1},{8,10},{10,12},{12... | collective-permute-start | bytes 3342344 | tf_op jit(solution)/shard_map/ppermute | solution.py:308
  72.8 53.9 %all-to-all-start.1 = ((bf16[128,8,256]{2,1,0:T(8,128)(2,1)}), bf16[128,8,256]{2,1,0:T(8,128)(2,1)S(1)}, u32[]{:S(2)}, u32[]{:S(2)}) async-start(bf16[128,8,256]{2,1,0:T(8,128)(2,1)} %table.1), calls=%async_computation.1 | async-start | bytes 1048576 | tf_op jit(solution)/shard_map/all_to_all | solution.py:347
  87.8 18.0 %collective-permute-start.13 = (bf16[16,8,4352]{2,1,0:T(8,128)(2,1)}, bf16[16,8,4352]{2,1,0:T(8,128)(2,1)S(1)}, u32[]{:S(2)}, u32[]{:S(2)}) collective-permute-start(bf16[16,8,4352]{2,1,0:T(8,128)(2,1)} %constant_dynamic-update-slice_fusion.column_ref), channel_id=1, source_target_pairs={{0,1},{1,0},{2,3},{3,2},{4,5},{5,4},{6,7},{7,6},{8,9},{9,8},{10,11... | collective-permute-start | bytes 3342344 | tf_op jit(solution)/shard_map/ppermute | solution.py:308
  92.0 13.9 %collective-permute-start.12 = (bf16[16,8,4352]{2,1,0:T(8,128)(2,1)S(1)}, bf16[16,8,4352]{2,1,0:T(8,128)(2,1)S(1)}, u32[]{:S(2)}, u32[]{:S(2)}) collective-permute-start(bf16[16,8,4352]{2,1,0:T(8,128)(2,1)S(1)} %collective-permute-done.9.refs_1_), channel_id=1, source_target_pairs={{0,1},{1,0},{2,3},{3,2},{4,5},{5,4},{6,7},{7,6},{8,9},{9,8},{10,11... | collective-permute-start | bytes 3342344 | tf_op jit(solution)/shard_map/ppermute | solution.py:308
  97.8 8.1 %collective-permute-start.11 = (bf16[16,8,4352]{2,1,0:T(8,128)(2,1)S(1)}, bf16[16,8,4352]{2,1,0:T(8,128)(2,1)S(1)}, u32[]{:S(2)}, u32[]{:S(2)}) collective-permute-start(bf16[16,8,4352]{2,1,0:T(8,128)(2,1)S(1)} %collective-permute-done.7.refs_0_), channel_id=1, source_target_pairs={{0,1},{1,0},{2,3},{3,2},{4,5},{5,4},{6,7},{7,6},{8,9},{9,8},{10,11... | collective-permute-start | bytes 3342344 | tf_op jit(solution)/shard_map/ppermute | solution.py:308
  99.7 19.2 %collective-permute-start.10 = (bf16[8,8,4352]{2,1,0:T(8,128)(2,1)S(1)}, bf16[8,8,4352]{2,1,0:T(8,128)(2,1)S(1)}, u32[]{:S(2)}, u32[]{:S(2)}) collective-permute-start(bf16[8,8,4352]{2,1,0:T(8,128)(2,1)S(1)} %slice.13), channel_id=1, source_target_pairs={{0,6},{2,0},{4,2},{6,4},{1,7},{3,1},{5,3},{7,5},{8,14},{10,8},{12,... | collective-permute-start | bytes 1671176 | tf_op jit(solution)/shard_map/ppermute | solution.py:308
  101.9 24.8 %copy-start.1 = (bf16[4,1024]{1,0:T(4,128)(2,1)S(1)}, bf16[4,1024]{1,0:T(4,128)(2,1)}, u32[]{:S(2)}) copy-start(bf16[4,1024]{1,0:T(4,128)(2,1)} %state_ref.1) | copy-start | bytes 24580
  101.9 24.8 %copy-start.2 = (f32[1,1024]{1,0:T(1,128)S(1)}, f32[1,1024]{1,0:T(1,128)}, u32[]{:S(2)}) copy-start(f32[1,1024]{1,0:T(1,128)} %gain_ref.1) | copy-start | bytes 12292
  101.9 24.8 %copy-start.4 = (s32[1,4]{1,0:T(1,128)S(1)}, s32[1,4]{1,0:T(1,128)}, u32[]{:S(2)}) copy-start(s32[1,4]{1,0:T(1,128)} %count_ref.1) | copy-start | bytes 52
  101.9 20.2 %collective-permute-start.8 = (bf16[8,8,4352]{2,1,0:T(8,128)(2,1)S(1)}, bf16[8,8,4352]{2,1,0:T(8,128)(2,1)}, u32[]{:S(2)}, u32[]{:S(2)}) collective-permute-start(bf16[8,8,4352]{2,1,0:T(8,128)(2,1)S(1)} %slice.12), channel_id=1, source_target_pairs={{0,2},{2,4},{4,6},{6,0},{1,3},{3,5},{5,7},{7,1},{8,10},{10,12},{12... | collective-permute-start | bytes 1671176 | tf_op jit(solution)/shard_map/ppermute | solution.py:308
  122.2 5.6 %collective-permute-start.14 = (bf16[8,8,4352]{2,1,0:T(8,128)(2,1)}, bf16[8,8,4352]{2,1,0:T(8,128)(2,1)S(1)}, u32[]{:S(2)}, u32[]{:S(2)}) collective-permute-start(bf16[8,8,4352]{2,1,0:T(8,128)(2,1)} %collective-permute-done.8.low_ref), channel_id=1, source_target_pairs={{0,1},{1,0},{2,3},{3,2},{4,5},{5,4},{6,7},{7,6},{8,9},{9,8},{10,11... | collective-permute-start | bytes 1671176 | tf_op jit(solution)/shard_map/ppermute | solution.py:308
  124.1 4.0 %collective-permute-start.15 = (bf16[8,8,4352]{2,1,0:T(8,128)(2,1)S(1)}, bf16[8,8,4352]{2,1,0:T(8,128)(2,1)S(1)}, u32[]{:S(2)}, u32[]{:S(2)}) collective-permute-start(bf16[8,8,4352]{2,1,0:T(8,128)(2,1)S(1)} %collective-permute-done.10.high_ref), channel_id=1, source_target_pairs={{0,1},{1,0},{2,3},{3,2},{4,5},{5,4},{6,7},{7,6},{8,9},{9,8},{10,11... | collective-permute-start | bytes 1671176 | tf_op jit(solution)/shard_map/ppermute | solution.py:308

commit v8 on v7

--- a/solution.py
+++ b/solution.py
@@ -160,7 +160,7 @@
 def place_kernel(*refs):
     *pieces, weight_ref, sems = refs
     ys = weight_ref.shape[1]
-    parts = ((ys - 1, 0), (1, 0), (ys - 1, 1), (1, 1), (0, 1))
+    parts = ((ys - 1, 0), (1, 0), (0, 1))
     kinds = [(piece, 0, *part) for piece, part in zip(pieces, parts)]
     place(kinds, weight_ref, sems)
     wait_placed(kinds, weight_ref, sems)
@@ -168,6 +168,8 @@
 
 def item_kernel(
     column_ref,
+    below_ref,
+    above_ref,
     low_ref,
     high_ref,
     low_swapped_ref,
@@ -191,6 +193,8 @@
     half = zs // 2
     kinds = (
         (column_ref, 0, 0, 0),
+        (below_ref, 0, ys - 1, 1),
+        (above_ref, 0, 1, 1),
         (low_ref, 0, 2, 0),
         (high_ref, half, 2, 0),
         (low_swapped_ref, 0, 2, 1),
@@ -204,7 +208,7 @@
     ):
         mine = []
         for number, (from_y, from_core) in enumerate(
-            ((ys - 1, 0), (1, 0), (ys - 1, 1), (1, 1), (0, 1))
+            ((ys - 1, 0), (1, 0), (0, 1))
         ):
             at = (
                 slice(None),
@@ -335,7 +339,8 @@
     below, above = moved(column, "y", 1), moved(column, "y", -1)
     across = (moved(below[:half], "y", 1), moved(above[half:], "y", -1))
     early = [below, above]
-    early = early + [moved(piece, "core", 1) for piece in (below, above, column)]
+    early = early + [moved(column, "core", 1)]
+    swapped = (moved(below, "core", 1), moved(above, "core", 1))
     found = pl.pallas_call(
         table_kernel,
         out_shape=jax.ShapeDtypeStruct((shards, CAP, emb), BF16),
@@ -357,7 +362,7 @@
         name="place",
     )(*early)
     across, weights = lax.optimization_barrier((across, weights))
-    late = [column, *across, *(moved(piece, "core", 1) for piece in across)]
+    late = [column, *swapped, *across, *(moved(piece, "core", 1) for piece in across)]
 
     smem = pl.BlockSpec(memory_space=pltpu.SMEM)
     listed, entering, gains, length_row = pl.pallas_call(
@@ -392,7 +397,7 @@
         out_specs=(vmem(),) * 5,
         scratch_shapes=[
             pltpu.SemaphoreType.DMA((len(late),)),
-            pltpu.SemaphoreType.DMA((3, 5)),
+            pltpu.SemaphoreType.DMA((3, 3)),
         ],
         compiler_params=big,
         name="item",

time: 159 us -> 152 us (0.956)
  waiting for transfers between devices: 24.4 us -> 17 us
  starting transfers between devices: 88 us -> 90.1 us
  Pallas kernels: 21.9 us -> 20.2 us
    ppermute x16, waiting for transfers between devices: 24.4 us -> 16.9 us  [moved(): lax.ppermute(block, axis, [(i, (i + distance) % size) for i in range(size)])]
    ppermute x16, starting transfers between devices: 63.2 us -> 65.2 us  [moved(): lax.ppermute(block, axis, [(i, (i + distance) % size) for i in range(size)])]
where the time goes in v8:
time: 152 us; the launch traced here: 150 us
  starting transfers between devices  90.1 us (59%)
  Pallas kernels  20.2 us (13%)
  waiting for transfers between devices  17 us (11%)
  blocking collectives  14.3 us (9%)
  local copies, waits for them, and re-layouts  6.18 us (4%)
    ppermute x16, starting transfers between devices, moved(): lax.ppermute(block, axis, [(i, (i + distance) % size) for i in range(size)])  65.2 us
    ppermute x16, waiting for transfers between devices, moved(): lax.ppermute(block, axis, [(i, (i + distance) % size) for i in range(size)])  16.9 us
    all_to_all x1, starting transfers between devices, per_device(): lax.all_to_all(found, SHARD, split_axis=0, concat_axis=0, tiled=True)  15 us
    all_gather x3, blocking collectives, per_device(): lax.all_gather(leaving, 'segment', axis=0, axis_index_groups=(even, odd)[...  14.3 us
    all_to_all x1, starting transfers between devices, per_device(): lax.all_to_all(request.reshape(shards, 1, CAP), SHARD, split_axis=0, conc...  9.89 us
    pallas_call x1, Pallas kernels, per_device(): pl.pallas_call(item_kernel, out_shape=(jax.ShapeDtypeStruct((users * item...  8.86 us
    pallas_call x3, Pallas kernels, per_device(): pl.pallas_call(section_kernel, out_shape=section_shape, in_specs=[vmem()]...  5.01 us
    unnamed x22, local copies, waits for them, and re-layouts  4.73 us
  transfers between devices with their start and end apart: 18, of which 7 were waited for; matrix products, arithmetic and copies ran while one was open for 2% of the time, Pallas kernels for 4%

profile of v8, /device:TPU:6, one launch (start us, length us, event | category | flops | bytes accessed | tf_op | source)
XLA Modules:
  0.0 150.2 jit_solution(15787600559680310832)
XLA Ops:
  0.6 0.0 copy-start.6
  0.6 0.0 copy-start.7
  0.7 0.0 copy-start.5
  0.7 0.7 reshape_squeeze.3
  1.4 0.8 maximum_bitcast_fusion
  2.2 15.7 %collective-permute-start.2 = (bf16[1,8,4352]{2,1,0:T(8,128)(2,1)S(1)}, bf16[1,8,4352]{2,1,0:T(8,128)(2,1)S(1)}, u32[]{:S(2)}, u32[]{:S(2)}) collective-permute-start(bf16[1,8,4352]{2,1,0:T(8,128)(2,1)S(1)} %maximum_bitcast_fusion), channel_id=1, source_target_pairs={{0,64},{8,72},{16,80},{24,88},{32,96},{40,104},{48,112},{56,120},{... | collective-permute-start | bytes 208904 | tf_op jit(solution)/shard_map/ppermute | solution.py:312
  17.9 4.3 %collective-permute-start.1 = (bf16[1,8,4352]{2,1,0:T(8,128)(2,1)S(1)}, bf16[1,8,4352]{2,1,0:T(8,128)(2,1)S(1)}, u32[]{:S(2)}, u32[]{:S(2)}) collective-permute-start(bf16[1,8,4352]{2,1,0:T(8,128)(2,1)S(1)} %maximum_bitcast_fusion), channel_id=1, source_target_pairs={{0,32},{8,40},{16,48},{24,56},{32,64},{40,72},{48,80},{56,88},{64,... | collective-permute-start | bytes 208904 | tf_op jit(solution)/shard_map/ppermute | solution.py:312
  22.2 5.5 %collective-permute-start = (bf16[1,8,4352]{2,1,0:T(8,128)(2,1)S(1)}, bf16[1,8,4352]{2,1,0:T(8,128)(2,1)S(1)}, u32[]{:S(2)}, u32[]{:S(2)}) collective-permute-start(bf16[1,8,4352]{2,1,0:T(8,128)(2,1)S(1)} %maximum_bitcast_fusion), channel_id=1, source_target_pairs={{0,96},{8,104},{16,112},{24,120},{32,0},{40,8},{48,16},{56,24},{64... | collective-permute-start | bytes 208904 | tf_op jit(solution)/shard_map/ppermute | solution.py:312
  27.7 0.0 copy-start.3
  27.7 0.7 copy-done.3
  28.3 1.3 request.1
  29.6 9.9 %all-to-all-start = ((s32[128,1,8]{2,1,0:T(1,128)}), s32[128,1,8]{2,1,0:T(1,128)S(1)}, u32[]{:S(2)}, u32[]{:S(2)}) async-start(s32[128,1,8]{2,1,0:T(1,128)} %bitcast.6), calls=%async_computation | async-start | bytes 131072 | tf_op jit(solution)/shard_map/all_to_all | solution.py:325
  39.5 0.0 collective-permute-done.2
  39.6 0.0 collective-permute-done.1
  39.6 0.0 collective-permute-done
  39.6 5.0 %collective-permute-start.4 = (bf16[4,8,4352]{2,1,0:T(8,128)(2,1)S(1)}, bf16[4,8,4352]{2,1,0:T(8,128)(2,1)S(1)}, u32[]{:S(2)}, u32[]{:S(2)}) collective-permute-start(bf16[4,8,4352]{2,1,0:T(8,128)(2,1)S(1)} %pad_maximum_fusion), channel_id=1, source_target_pairs={{0,120},{8,0},{16,8},{24,16},{32,24},{40,32},{48,40},{56,48},{64,5... | collective-permute-start | bytes 835592 | tf_op jit(solution)/shard_map/ppermute | solution.py:312
  44.6 1.9 %collective-permute-start.3 = (bf16[4,8,4352]{2,1,0:T(8,128)(2,1)S(1)}, bf16[4,8,4352]{2,1,0:T(8,128)(2,1)S(1)}, u32[]{:S(2)}, u32[]{:S(2)}) collective-permute-start(bf16[4,8,4352]{2,1,0:T(8,128)(2,1)S(1)} %pad_maximum_fusion), channel_id=1, source_target_pairs={{0,8},{8,16},{16,24},{24,32},{32,40},{40,48},{48,56},{56,64},{64,7... | collective-permute-start | bytes 835592 | tf_op jit(solution)/shard_map/ppermute | solution.py:312
  46.5 2.9 %collective-permute-start.6 = (bf16[2,8,4352]{2,1,0:T(8,128)(2,1)S(1)}, bf16[2,8,4352]{2,1,0:T(8,128)(2,1)S(1)}, u32[]{:S(2)}, u32[]{:S(2)}) collective-permute-start(bf16[2,8,4352]{2,1,0:T(8,128)(2,1)S(1)} %get-tuple-element.52), channel_id=1, source_target_pairs={{0,16},{8,24},{16,32},{24,40},{32,48},{40,56},{48,64},{56,72},{64,... | collective-permute-start | bytes 417800 | tf_op jit(solution)/shard_map/ppermute | solution.py:312
  49.5 0.0 copy-start
  49.5 5.2 %collective-permute-start.5 = (bf16[2,8,4352]{2,1,0:T(8,128)(2,1)S(1)}, bf16[2,8,4352]{2,1,0:T(8,128)(2,1)S(1)}, u32[]{:S(2)}, u32[]{:S(2)}) collective-permute-start(bf16[2,8,4352]{2,1,0:T(8,128)(2,1)S(1)} %get-tuple-element.53), channel_id=1, source_target_pairs={{0,112},{8,120},{16,0},{24,8},{32,16},{40,24},{48,32},{56,40},{64,... | collective-permute-start | bytes 417800 | tf_op jit(solution)/shard_map/ppermute | solution.py:312
  54.7 0.6 constant_dynamic-update-slice_fusion.7
  55.3 0.6 constant_dynamic-update-slice_fusion.6
  55.9 0.6 constant_dynamic-update-slice_fusion.5
  56.5 0.6 constant_dynamic-update-slice_fusion.4
  57.2 0.0 all-to-all-done
  57.2 3.6 %collective-permute-done.6 = bf16[2,8,4352]{2,1,0:T(8,128)(2,1)S(1)} collective-permute-done((bf16[2,8,4352]{2,1,0:T(8,128)(2,1)S(1)}, bf16[2,8,4352]{2,1,0:T(8,128)(2,1)S(1)}, u32[]{:S(2)}, u32[]{:S(2)}) %collective-permute-start.6) | collective-permute-done | bytes 139296 | tf_op jit(solution)/shard_map/ppermute | solution.py:312
  60.8 0.5 collective-permute-done.5
  61.4 0.0 collective-permute-done.3
  61.4 0.7 constant_dynamic-update-slice_fusion.3
  62.1 0.7 constant_dynamic-update-slice_fusion.2
  62.8 0.7 constant_dynamic-update-slice_fusion.1
  63.5 0.7 constant_dynamic-update-slice_fusion.column_ref
  64.1 4.6 %collective-permute-start.9 = (bf16[16,8,4352]{2,1,0:T(8,128)(2,1)}, bf16[16,8,4352]{2,1,0:T(8,128)(2,1)S(1)}, u32[]{:S(2)}, u32[]{:S(2)}) collective-permute-start(bf16[16,8,4352]{2,1,0:T(8,128)(2,1)} %constant_dynamic-update-slice_fusion.column_ref), channel_id=1, source_target_pairs={{0,6},{2,0},{4,2},{6,4},{1,7},{3,1},{5,3},{7,5},{8,14},{10,8},{12,... | collective-permute-start | bytes 3342344 | tf_op jit(solution)/shard_map/ppermute | solution.py:312
  68.8 1.9 %collective-permute-start.7 = (bf16[16,8,4352]{2,1,0:T(8,128)(2,1)}, bf16[16,8,4352]{2,1,0:T(8,128)(2,1)S(1)}, u32[]{:S(2)}, u32[]{:S(2)}) collective-permute-start(bf16[16,8,4352]{2,1,0:T(8,128)(2,1)} %constant_dynamic-update-slice_fusion.column_ref), channel_id=1, source_target_pairs={{0,2},{2,4},{4,6},{6,0},{1,3},{3,5},{5,7},{7,1},{8,10},{10,12},{12... | collective-permute-start | bytes 3342344 | tf_op jit(solution)/shard_map/ppermute | solution.py:312
  70.7 2.1 %table.1 = bf16[128,8,256]{2,1,0:T(8,128)(2,1)} custom-call(s32[128,8]{1,0:T(8,128)S(1)} %bitcast.23, bf16[2048,256]{1,0:T(8,128)(2,1)S(1)} %copy-done), custom_call_target="tpu_custom_call" | custom-call | tf_op jit(solution)/shard_map/table/pallas_call | solution.py:344
  72.8 15.0 %all-to-all-start.1 = ((bf16[128,8,256]{2,1,0:T(8,128)(2,1)}), bf16[128,8,256]{2,1,0:T(8,128)(2,1)S(1)}, u32[]{:S(2)}, u32[]{:S(2)}) async-start(bf16[128,8,256]{2,1,0:T(8,128)(2,1)} %table.1), calls=%async_computation.1 | async-start | bytes 1048576 | tf_op jit(solution)/shard_map/all_to_all | solution.py:352
  87.8 1.9 %collective-permute-start.13 = (bf16[16,8,4352]{2,1,0:T(8,128)(2,1)}, bf16[16,8,4352]{2,1,0:T(8,128)(2,1)S(1)}, u32[]{:S(2)}, u32[]{:S(2)}) collective-permute-start(bf16[16,8,4352]{2,1,0:T(8,128)(2,1)} %constant_dynamic-update-slice_fusion.column_ref), channel_id=1, source_target_pairs={{0,1},{1,0},{2,3},{3,2},{4,5},{5,4},{6,7},{7,6},{8,9},{9,8},{10,11... | collective-permute-start | bytes 3342344 | tf_op jit(solution)/shard_map/ppermute | solution.py:312
  89.8 2.2 %collective-permute-done.9.refs_1_ = bf16[16,8,4352]{2,1,0:T(8,128)(2,1)S(1)} collective-permute-done((bf16[16,8,4352]{2,1,0:T(8,128)(2,1)}, bf16[16,8,4352]{2,1,0:T(8,128)(2,1)S(1)}, u32[]{:S(2)}, u32[]{:S(2)}) %collective-permute-start.9) | collective-permute-done | bytes 1114144 | tf_op jit(solution)/shard_map/ppermute | solution.py:312
  92.0 5.5 %collective-permute-start.12 = (bf16[8,8,4352]{2,1,0:T(8,128)(2,1)S(1)}, bf16[8,8,4352]{2,1,0:T(8,128)(2,1)S(1)}, u32[]{:S(2)}, u32[]{:S(2)}) collective-permute-start(bf16[8,8,4352]{2,1,0:T(8,128)(2,1)S(1)} %slice.13), channel_id=1, source_target_pairs={{0,6},{2,0},{4,2},{6,4},{1,7},{3,1},{5,3},{7,5},{8,14},{10,8},{12,... | collective-permute-start | bytes 1671176 | tf_op jit(solution)/shard_map/ppermute | solution.py:312
  97.5 0.3 collective-permute-done.7.refs_0_
  97.8 0.0 copy-start.1
  97.8 0.0 copy-start.2
  97.8 0.0 copy-start.4
  97.9 2.1 %collective-permute-start.11 = (bf16[8,8,4352]{2,1,0:T(8,128)(2,1)S(1)}, bf16[8,8,4352]{2,1,0:T(8,128)(2,1)}, u32[]{:S(2)}, u32[]{:S(2)}) collective-permute-start(bf16[8,8,4352]{2,1,0:T(8,128)(2,1)S(1)} %slice.12), channel_id=1, source_target_pairs={{0,2},{2,4},{4,6},{6,0},{1,3},{3,5},{5,7},{7,1},{8,10},{10,12},{12... | collective-permute-start | bytes 1671176 | tf_op jit(solution)/shard_map/ppermute | solution.py:312
  99.9 1.9 %collective-permute-start.10 = (bf16[16,8,4352]{2,1,0:T(8,128)(2,1)S(1)}, bf16[16,8,4352]{2,1,0:T(8,128)(2,1)}, u32[]{:S(2)}, u32[]{:S(2)}) collective-permute-start(bf16[16,8,4352]{2,1,0:T(8,128)(2,1)S(1)} %collective-permute-done.9.refs_1_), channel_id=1, source_target_pairs={{0,1},{1,0},{2,3},{3,2},{4,5},{5,4},{6,7},{7,6},{8,9},{9,8},{10,11... | collective-permute-start | bytes 3342344 | tf_op jit(solution)/shard_map/ppermute | solution.py:312
  101.9 2.4 %collective-permute-start.8 = (bf16[16,8,4352]{2,1,0:T(8,128)(2,1)S(1)}, bf16[16,8,4352]{2,1,0:T(8,128)(2,1)}, u32[]{:S(2)}, u32[]{:S(2)}) collective-permute-start(bf16[16,8,4352]{2,1,0:T(8,128)(2,1)S(1)} %collective-permute-done.7.refs_0_), channel_id=1, source_target_pairs={{0,1},{1,0},{2,3},{3,2},{4,5},{5,4},{6,7},{7,6},{8,9},{9,8},{10,11... | collective-permute-start | bytes 3342344 | tf_op jit(solution)/shard_map/ppermute | solution.py:312
  104.3 0.0 collective-permute-done.13.refs_2_
  104.3 1.8 %place.1.placed_ref = bf16[16,4,2,8,4352]{4,3,2,1,0:T(8,128)(2,1)} custom-call(bf16[16,8,4352]{2,1,0:T(8,128)(2,1)S(1)} %collective-permute-done.7.refs_0_, bf16[16,8,4352]{2,1,0:T(8,128)(2,1)S(1)} %collective-permute-done.9.refs_1_, bf16[16,8,4352]{2,1,0:T(8,128)(2,1)S(1)} %collective-permute-done.13.refs_2_), custom_call_target="tpu_custom_call" | custom-call | bytes 14000000 | tf_op jit(solution)/shard_map/place/pallas_call | solution.py:354
  106.1 4.6 %collective-permute-done.12.high_ref = bf16[8,8,4352]{2,1,0:T(8,128)(2,1)S(1)} collective-permute-done((bf16[8,8,4352]{2,1,0:T(8,128)(2,1)S(1)}, bf16[8,8,4352]{2,1,0:T(8,128)(2,1)S(1)}, u32[]{:S(2)}, u32[]{:S(2)}) %collective-permute-start.12) | collective-permute-done | bytes 557088 | tf_op jit(solution)/shard_map/ppermute | solution.py:312
  110.8 5.2 %collective-permute-done.11.low_ref = bf16[8,8,4352]{2,1,0:T(8,128)(2,1)} collective-permute-done((bf16[8,8,4352]{2,1,0:T(8,128)(2,1)S(1)}, bf16[8,8,4352]{2,1,0:T(8,128)(2,1)}, u32[]{:S(2)}, u32[]{:S(2)}) %collective-permute-start.11) | collective-permute-done | bytes 557088 | tf_op jit(solution)/shard_map/ppermute | solution.py:312
  116.0 1.9 %collective-permute-start.14 = (bf16[8,8,4352]{2,1,0:T(8,128)(2,1)}, bf16[8,8,4352]{2,1,0:T(8,128)(2,1)}, u32[]{:S(2)}, u32[]{:S(2)}) collective-permute-start(bf16[8,8,4352]{2,1,0:T(8,128)(2,1)} %collective-permute-done.11.low_ref), channel_id=1, source_target_pairs={{0,1},{1,0},{2,3},{3,2},{4,5},{5,4},{6,7},{7,6},{8,9},{9,8},{10,11... | collective-permute-start | bytes 1671176 | tf_op jit(solution)/shard_map/ppermute | solution.py:312
  117.9 2.6 %collective-permute-start.15 = (bf16[8,8,4352]{2,1,0:T(8,128)(2,1)S(1)}, bf16[8,8,4352]{2,1,0:T(8,128)(2,1)}, u32[]{:S(2)}, u32[]{:S(2)}) collective-permute-start(bf16[8,8,4352]{2,1,0:T(8,128)(2,1)S(1)} %collective-permute-done.12.high_ref), channel_id=1, source_target_pairs={{0,1},{1,0},{2,3},{3,2},{4,5},{5,4},{6,7},{7,6},{8,9},{9,8},{10,11... | collective-permute-start | bytes 1671176 | tf_op jit(solution)/shard_map/ppermute | solution.py:312
  120.5 0.0 all-to-all-done.1
  120.5 1.0 list.1
  121.6 0.0 collective-permute-done.8.below_ref
  121.6 0.0 collective-permute-done.14.low_swapped_ref
  121.6 0.4 collective-permute-done.15.high_swapped_ref
  122.0 8.9 %item.1 = (bf16[512,1024]{1,0:T(8,128)(2,1)S(1)}, bf16[512,1024]{1,0:T(8,128)(2,1)S(1)}, bf16[16,4,2,8,4352]{4,3,2,1,0:T(8,128)(2,1)S(1)}, bf16[4,1024]{1,0:T(4,128)(2,1)S(1)}, f32[1,512]{1,0:T(1,128)S(1)}) custom-call(bf16[16,8,4352]{2,1,0:T(8,128)(2,1)} %constant_dynamic-update-slice_fusion.column_ref, ...), custom_call_target="tpu_custom_call" | custom-call | tf_op jit(solution)/shard_map/item/pallas_call | solution.py:386
  130.9 4.4 %all-gather.3.state_ref = bf16[2,4,1024]{2,1,0:T(4,128)(2,1)S(1)} all-gather(bf16[1,4,1024]{2,1,0:T(4,128)(2,1)S(1)} %bitcast.24), channel_id=2, replica_groups={{0,128},{256,384},{1,129},{257,385},{2,130},{258,386},{3,131},{259,387}..., dimensions={0}, use_global_device_ids=true | all-gather | bytes 24576 | tf_op jit(solution)/shard_map/all_gather | solution.py:410
  135.2 1.5 section.3
  136.7 5.6 %all-gather.4.state_ref = bf16[2,4,1024]{2,1,0:T(4,128)(2,1)S(1)} all-gather(bf16[1,4,1024]{2,1,0:T(4,128)(2,1)S(1)} %bitcast.25), channel_id=3, replica_groups={{128,256},{0,384},{129,257},{1,385},{130,258},{2,386},{131,259},{3,387}..., dimensions={0}, use_global_device_ids=true | all-gather | bytes 24576 | tf_op jit(solution)/shard_map/all_gather | solution.py:410
  142.3 1.5 section.4
  143.7 4.4 %all-gather.5.state_ref = bf16[2,4,1024]{2,1,0:T(4,128)(2,1)S(1)} all-gather(bf16[1,4,1024]{2,1,0:T(4,128)(2,1)S(1)} %bitcast.26), channel_id=4, replica_groups={{0,128},{256,384},{1,129},{257,385},{2,130},{258,386},{3,131},{259,387}..., dimensions={0}, use_global_device_ids=true | all-gather | bytes 24576 | tf_op jit(solution)/shard_map/all_gather | solution.py:410
  148.1 2.1 %section.5 = (bf16[4,1024]{1,0:T(4,128)(2,1)}, f32[1,512]{1,0:T(1,128)}) custom-call(bf16[2,4,1024]{2,1,0:T(4,128)(2,1)S(1)} %all-gather.5.state_ref, bf16[512,1024]{1,0:T(8,128)(2,1)S(1)} %get-tuple-element.42.key_ref, bf16[512,1024]{1,0:T(8,128)(2,1)S(1)} %get-tuple-element.43.value_ref, bf16[1024,4352]{1,0:T(8,128)(2,1)S(1)} %bitcast.21, ...), custom_call_target="tpu_custom_call" | custom-call | tf_op jit(solution)/shard_map/section/pallas_call | solution.py:414
  (13 shorter events, 0.2 us)
Async XLA Ops:
  0.6 54.7 %copy-start.6 = (bf16[1,8,1024]{2,1,0:T(8,128)(2,1)S(1)}, bf16[1,8,1024]{2,1,0:T(8,128)(2,1)}, u32[]{:S(2)}) copy-start(bf16[1,8,1024]{2,1,0:T(8,128)(2,1)} %param.14) | copy-start | bytes 49156
  0.6 54.7 %copy-start.7 = (bf16[1,8,1024]{2,1,0:T(8,128)(2,1)S(1)}, bf16[1,8,1024]{2,1,0:T(8,128)(2,1)}, u32[]{:S(2)}) copy-start(bf16[1,8,1024]{2,1,0:T(8,128)(2,1)} %param.13) | copy-start | bytes 49156
  0.7 54.6 %copy-start.5 = (bf16[1,8,2048]{2,1,0:T(8,128)(2,1)S(1)}, bf16[1,8,2048]{2,1,0:T(8,128)(2,1)}, u32[]{:S(2)}) copy-start(bf16[1,8,2048]{2,1,0:T(8,128)(2,1)} %param.12) | copy-start | bytes 98308
  2.2 37.4 %collective-permute-start.2 = (bf16[1,8,4352]{2,1,0:T(8,128)(2,1)S(1)}, bf16[1,8,4352]{2,1,0:T(8,128)(2,1)S(1)}, u32[]{:S(2)}, u32[]{:S(2)}) collective-permute-start(bf16[1,8,4352]{2,1,0:T(8,128)(2,1)S(1)} %maximum_bitcast_fusion), channel_id=1, source_target_pairs={{0,64},{8,72},{16,80},{24,88},{32,96},{40,104},{48,112},{56,120},{... | collective-permute-start | bytes 208904 | tf_op jit(solution)/shard_map/ppermute | solution.py:312
  17.9 21.7 %collective-permute-start.1 = (bf16[1,8,4352]{2,1,0:T(8,128)(2,1)S(1)}, bf16[1,8,4352]{2,1,0:T(8,128)(2,1)S(1)}, u32[]{:S(2)}, u32[]{:S(2)}) collective-permute-start(bf16[1,8,4352]{2,1,0:T(8,128)(2,1)S(1)} %maximum_bitcast_fusion), channel_id=1, source_target_pairs={{0,32},{8,40},{16,48},{24,56},{32,64},{40,72},{48,80},{56,88},{64,... | collective-permute-start | bytes 208904 | tf_op jit(solution)/shard_map/ppermute | solution.py:312
  22.2 17.4 %collective-permute-start = (bf16[1,8,4352]{2,1,0:T(8,128)(2,1)S(1)}, bf16[1,8,4352]{2,1,0:T(8,128)(2,1)S(1)}, u32[]{:S(2)}, u32[]{:S(2)}) collective-permute-start(bf16[1,8,4352]{2,1,0:T(8,128)(2,1)S(1)} %maximum_bitcast_fusion), channel_id=1, source_target_pairs={{0,96},{8,104},{16,112},{24,120},{32,0},{40,8},{48,16},{56,24},{64... | collective-permute-start | bytes 208904 | tf_op jit(solution)/shard_map/ppermute | solution.py:312
  27.7 0.7 copy-start.3
  29.6 27.5 %all-to-all-start = ((s32[128,1,8]{2,1,0:T(1,128)}), s32[128,1,8]{2,1,0:T(1,128)S(1)}, u32[]{:S(2)}, u32[]{:S(2)}) async-start(s32[128,1,8]{2,1,0:T(1,128)} %bitcast.6), calls=%async_computation | async-start | bytes 131072 | tf_op jit(solution)/shard_map/all_to_all | solution.py:325
  39.6 21.7 %collective-permute-start.4 = (bf16[4,8,4352]{2,1,0:T(8,128)(2,1)S(1)}, bf16[4,8,4352]{2,1,0:T(8,128)(2,1)S(1)}, u32[]{:S(2)}, u32[]{:S(2)}) collective-permute-start(bf16[4,8,4352]{2,1,0:T(8,128)(2,1)S(1)} %pad_maximum_fusion), channel_id=1, source_target_pairs={{0,120},{8,0},{16,8},{24,16},{32,24},{40,32},{48,40},{56,48},{64,5... | collective-permute-start | bytes 835592 | tf_op jit(solution)/shard_map/ppermute | solution.py:312
  44.6 16.8 %collective-permute-start.3 = (bf16[4,8,4352]{2,1,0:T(8,128)(2,1)S(1)}, bf16[4,8,4352]{2,1,0:T(8,128)(2,1)S(1)}, u32[]{:S(2)}, u32[]{:S(2)}) collective-permute-start(bf16[4,8,4352]{2,1,0:T(8,128)(2,1)S(1)} %pad_maximum_fusion), channel_id=1, source_target_pairs={{0,8},{8,16},{16,24},{24,32},{32,40},{40,48},{48,56},{56,64},{64,7... | collective-permute-start | bytes 835592 | tf_op jit(solution)/shard_map/ppermute | solution.py:312
  46.5 14.3 %collective-permute-start.6 = (bf16[2,8,4352]{2,1,0:T(8,128)(2,1)S(1)}, bf16[2,8,4352]{2,1,0:T(8,128)(2,1)S(1)}, u32[]{:S(2)}, u32[]{:S(2)}) collective-permute-start(bf16[2,8,4352]{2,1,0:T(8,128)(2,1)S(1)} %get-tuple-element.52), channel_id=1, source_target_pairs={{0,16},{8,24},{16,32},{24,40},{32,48},{40,56},{48,64},{56,72},{64,... | collective-permute-start | bytes 417800 | tf_op jit(solution)/shard_map/ppermute | solution.py:312
  49.5 21.2 %copy-start = (bf16[2048,256]{1,0:T(8,128)(2,1)S(1)}, bf16[2048,256]{1,0:T(8,128)(2,1)}, u32[]{:S(2)}) copy-start(bf16[2048,256]{1,0:T(8,128)(2,1)} %table_ref.1) | copy-start | bytes 3145732
  49.5 11.9 %collective-permute-start.5 = (bf16[2,8,4352]{2,1,0:T(8,128)(2,1)S(1)}, bf16[2,8,4352]{2,1,0:T(8,128)(2,1)S(1)}, u32[]{:S(2)}, u32[]{:S(2)}) collective-permute-start(bf16[2,8,4352]{2,1,0:T(8,128)(2,1)S(1)} %get-tuple-element.53), channel_id=1, source_target_pairs={{0,112},{8,120},{16,0},{24,8},{32,16},{40,24},{48,32},{56,40},{64,... | collective-permute-start | bytes 417800 | tf_op jit(solution)/shard_map/ppermute | solution.py:312
  64.1 27.8 %collective-permute-start.9 = (bf16[16,8,4352]{2,1,0:T(8,128)(2,1)}, bf16[16,8,4352]{2,1,0:T(8,128)(2,1)S(1)}, u32[]{:S(2)}, u32[]{:S(2)}) collective-permute-start(bf16[16,8,4352]{2,1,0:T(8,128)(2,1)} %constant_dynamic-update-slice_fusion.column_ref), channel_id=1, source_target_pairs={{0,6},{2,0},{4,2},{6,4},{1,7},{3,1},{5,3},{7,5},{8,14},{10,8},{12,... | collective-permute-start | bytes 3342344 | tf_op jit(solution)/shard_map/ppermute | solution.py:312
  68.8 29.0 %collective-permute-start.7 = (bf16[16,8,4352]{2,1,0:T(8,128)(2,1)}, bf16[16,8,4352]{2,1,0:T(8,128)(2,1)S(1)}, u32[]{:S(2)}, u32[]{:S(2)}) collective-permute-start(bf16[16,8,4352]{2,1,0:T(8,128)(2,1)} %constant_dynamic-update-slice_fusion.column_ref), channel_id=1, source_target_pairs={{0,2},{2,4},{4,6},{6,0},{1,3},{3,5},{5,7},{7,1},{8,10},{10,12},{12... | collective-permute-start | bytes 3342344 | tf_op jit(solution)/shard_map/ppermute | solution.py:312
  72.8 47.6 %all-to-all-start.1 = ((bf16[128,8,256]{2,1,0:T(8,128)(2,1)}), bf16[128,8,256]{2,1,0:T(8,128)(2,1)S(1)}, u32[]{:S(2)}, u32[]{:S(2)}) async-start(bf16[128,8,256]{2,1,0:T(8,128)(2,1)} %table.1), calls=%async_computation.1 | async-start | bytes 1048576 | tf_op jit(solution)/shard_map/all_to_all | solution.py:352
  87.8 16.4 %collective-permute-start.13 = (bf16[16,8,4352]{2,1,0:T(8,128)(2,1)}, bf16[16,8,4352]{2,1,0:T(8,128)(2,1)S(1)}, u32[]{:S(2)}, u32[]{:S(2)}) collective-permute-start(bf16[16,8,4352]{2,1,0:T(8,128)(2,1)} %constant_dynamic-update-slice_fusion.column_ref), channel_id=1, source_target_pairs={{0,1},{1,0},{2,3},{3,2},{4,5},{5,4},{6,7},{7,6},{8,9},{9,8},{10,11... | collective-permute-start | bytes 3342344 | tf_op jit(solution)/shard_map/ppermute | solution.py:312
  92.0 18.7 %collective-permute-start.12 = (bf16[8,8,4352]{2,1,0:T(8,128)(2,1)S(1)}, bf16[8,8,4352]{2,1,0:T(8,128)(2,1)S(1)}, u32[]{:S(2)}, u32[]{:S(2)}) collective-permute-start(bf16[8,8,4352]{2,1,0:T(8,128)(2,1)S(1)} %slice.13), channel_id=1, source_target_pairs={{0,6},{2,0},{4,2},{6,4},{1,7},{3,1},{5,3},{7,5},{8,14},{10,8},{12,... | collective-permute-start | bytes 1671176 | tf_op jit(solution)/shard_map/ppermute | solution.py:312
  97.8 22.7 %copy-start.1 = (bf16[4,1024]{1,0:T(4,128)(2,1)S(1)}, bf16[4,1024]{1,0:T(4,128)(2,1)}, u32[]{:S(2)}) copy-start(bf16[4,1024]{1,0:T(4,128)(2,1)} %state_ref.1) | copy-start | bytes 24580
  97.8 22.7 %copy-start.2 = (f32[1,1024]{1,0:T(1,128)S(1)}, f32[1,1024]{1,0:T(1,128)}, u32[]{:S(2)}) copy-start(f32[1,1024]{1,0:T(1,128)} %gain_ref.1) | copy-start | bytes 12292
  97.8 22.6 %copy-start.4 = (s32[1,4]{1,0:T(1,128)S(1)}, s32[1,4]{1,0:T(1,128)}, u32[]{:S(2)}) copy-start(s32[1,4]{1,0:T(1,128)} %count_ref.1) | copy-start | bytes 52
  97.9 18.1 %collective-permute-start.11 = (bf16[8,8,4352]{2,1,0:T(8,128)(2,1)S(1)}, bf16[8,8,4352]{2,1,0:T(8,128)(2,1)}, u32[]{:S(2)}, u32[]{:S(2)}) collective-permute-start(bf16[8,8,4352]{2,1,0:T(8,128)(2,1)S(1)} %slice.12), channel_id=1, source_target_pairs={{0,2},{2,4},{4,6},{6,0},{1,3},{3,5},{5,7},{7,1},{8,10},{10,12},{12... | collective-permute-start | bytes 1671176 | tf_op jit(solution)/shard_map/ppermute | solution.py:312
  99.9 21.6 %collective-permute-start.10 = (bf16[16,8,4352]{2,1,0:T(8,128)(2,1)S(1)}, bf16[16,8,4352]{2,1,0:T(8,128)(2,1)}, u32[]{:S(2)}, u32[]{:S(2)}) collective-permute-start(bf16[16,8,4352]{2,1,0:T(8,128)(2,1)S(1)} %collective-permute-done.9.refs_1_), channel_id=1, source_target_pairs={{0,1},{1,0},{2,3},{3,2},{4,5},{5,4},{6,7},{7,6},{8,9},{9,8},{10,11... | collective-permute-start | bytes 3342344 | tf_op jit(solution)/shard_map/ppermute | solution.py:312
  101.9 19.7 %collective-permute-start.8 = (bf16[16,8,4352]{2,1,0:T(8,128)(2,1)S(1)}, bf16[16,8,4352]{2,1,0:T(8,128)(2,1)}, u32[]{:S(2)}, u32[]{:S(2)}) collective-permute-start(bf16[16,8,4352]{2,1,0:T(8,128)(2,1)S(1)} %collective-permute-done.7.refs_0_), channel_id=1, source_target_pairs={{0,1},{1,0},{2,3},{3,2},{4,5},{5,4},{6,7},{7,6},{8,9},{9,8},{10,11... | collective-permute-start | bytes 3342344 | tf_op jit(solution)/shard_map/ppermute | solution.py:312
  116.0 5.6 %collective-permute-start.14 = (bf16[8,8,4352]{2,1,0:T(8,128)(2,1)}, bf16[8,8,4352]{2,1,0:T(8,128)(2,1)}, u32[]{:S(2)}, u32[]{:S(2)}) collective-permute-start(bf16[8,8,4352]{2,1,0:T(8,128)(2,1)} %collective-permute-done.11.low_ref), channel_id=1, source_target_pairs={{0,1},{1,0},{2,3},{3,2},{4,5},{5,4},{6,7},{7,6},{8,9},{9,8},{10,11... | collective-permute-start | bytes 1671176 | tf_op jit(solution)/shard_map/ppermute | solution.py:312
  117.9 4.1 %collective-permute-start.15 = (bf16[8,8,4352]{2,1,0:T(8,128)(2,1)S(1)}, bf16[8,8,4352]{2,1,0:T(8,128)(2,1)}, u32[]{:S(2)}, u32[]{:S(2)}) collective-permute-start(bf16[8,8,4352]{2,1,0:T(8,128)(2,1)S(1)} %collective-permute-done.12.high_ref), channel_id=1, source_target_pairs={{0,1},{1,0},{2,3},{3,2},{4,5},{5,4},{6,7},{7,6},{8,9},{9,8},{10,11... | collective-permute-start | bytes 1671176 | tf_op jit(solution)/shard_map/ppermute | solution.py:312
